TPU v7x, 512 devices: a whole 4x4x16 slice. The times are simulated.
512 devices in a mesh: rows: 128 (over z, x, core), cls: 4 (over y).
Axes of the slice: x: 4, y: 4, z: 16, core: 2. Of those that a mesh axis runs over, the one named last changes fastest.
Arguments:
- centers: bfloat16 [32768, 1280], P('rows', 'cls'), may hold values from 0 to 4
- coefficients: float32 [1000, 32768], P('cls', 'rows'), may hold values from -0.6 to 0.6
- batch_features: bfloat16 [1024, 1280], P('rows', 'cls'), may hold values from 0 to 4
- batch_labels: int32 [1024], replicated, may hold values from 0 to 999
- batch_index: int32 [1024], replicated, may hold values from 0 to 32767
- subset_index: int32 [8192], P('rows'), may hold values from 0 to 32767, as said below
- eigen_vectors: float32 [8192, 512], P('rows'), may hold values from -0.0625 to 0.0625
- eigen_scale: float32 [512], replicated, may hold values from 0.2 to 2
Outputs:
- predicted: float32 [1000, 1024], P('cls')
- new_coefficients: float32 [1000, 32768], P('cls', 'rows')
Inputs may be any that keep to these rules, and one draw needn't show every extreme that they name: `subset_index`: entry s lies among the centers (s // 64) * 256 to (s // 64 + 1) * 256 - 1; entry 0 is 0 and the last is 32767.
All inputs are finite; a program needn't handle non-finite values.
Results may differ from a plain program's by a relative error of at most 0.0003.
Values may be sent and summed in bfloat16 or wider, within the bound.
No kernel may reach another device: no remote copies, remote signals or barrier semaphores. Data moves between devices by JAX's collectives and lax.ppermute only.
A program may use at most 64 MiB of HBM per device.

v0:
```python
import jax
import jax.numpy as jnp
from jax import lax
from jax.sharding import Mesh
from jax.sharding import PartitionSpec as P

ROWS = ("rows_0", "rows_1", "rows_2")


spread = 4.0
step_rate = 0.5


def sent_to_all(value, axis):
    copies = jnp.broadcast_to(value, (lax.axis_size(axis), *value.shape))
    return lax.all_to_all(copies, axis, split_axis=0, concat_axis=0, tiled=True)


def joined_along(tiles, dim):
    shape = list(tiles.shape[1:])
    shape[dim] *= tiles.shape[0]
    return jnp.moveaxis(tiles, 0, dim).reshape(shape)


def whole_of(value, axes, dim):
    far, near = axes
    first = sent_to_all(value, far)
    tiles = jnp.swapaxes(sent_to_all(first, near), 0, 1)
    return joined_along(tiles.reshape(-1, *value.shape), dim)


def gather_directly(value, axis, dim):
    return joined_along(sent_to_all(value, axis), dim)


def rows_first(arrays, axis, dims):
    turned = [jnp.moveaxis(a, dim, 0) for a, dim in zip(arrays, dims)]
    both = jnp.concatenate([t.reshape(len(t), -1) for t in turned], axis=1)
    filled, at, done = (lax.all_gather(both, axis, axis=0, tiled=True), 0, [])
    for t, dim in zip(turned, dims):
        piece = filled[:, at : at + t[0].size].reshape(-1, *t.shape[1:])
        done.append(jnp.moveaxis(piece, 0, dim))
        at += t[0].size
    return tuple(done)


def cut_along(value, dim, count):
    shape = value.shape
    tiles = value.reshape(*shape[:dim], count, shape[dim] // count, *shape[dim + 1 :])
    return jnp.moveaxis(tiles, dim, 0)


def sent_and_summed(value, axis, dim):
    count = lax.axis_size(axis)
    tiles = lax.all_to_all(cut_along(value, dim, count), axis, 0, 0, tiled=True)
    return jnp.sum(tiles, axis=0)


def sum_in_two_steps(value, axes, dim):
    far, near = axes
    tiles = cut_along(value, dim, lax.axis_size(far))
    nearer = sent_and_summed(tiles, near, dim + 1)
    arrived = lax.all_to_all(nearer, far, split_axis=0, concat_axis=0, tiled=True)
    return arrived.sum(axis=0)


def padded_to(lines, count):
    spare = -len(lines) % count
    return jnp.pad(lines, [(0, spare)] + [(0, 0)] * (lines.ndim - 1))


def nested_sum(value, axes):
    own = sum_in_two_steps(
        padded_to(value, lax.axis_size(axes[0]) * lax.axis_size(axes[1])), axes, 0
    )
    whole = whole_of(own, axes, 0)
    return whole[: len(value)].reshape(value.shape)


def together(arrays, axis):
    ends = [0]
    for a in arrays:
        ends.append(ends[-1] + a.size)
    total = nested_sum(jnp.concatenate([a.ravel() for a in arrays]), axis)
    return tuple((total[b:e].reshape(a.shape) for a, b, e in zip(arrays, ends, ends[1:])))


def kernel_block(inner, row_norm, col_norm):
    squared = row_norm[:, None] + col_norm[None, :] - 2.0 * inner
    return jnp.exp(-jnp.sqrt(jnp.maximum(squared, 0.0)) / spread)


def square_norm(features):
    return jnp.sum(jnp.square(features.astype(jnp.float32)), axis=1)


def shards(
    centers,
    coefficients,
    batch_features,
    batch_labels,
    batch_index,
    subset_index,
    eigen_vectors,
    eigen_scale,
):
    row_count = centers.shape[0]
    first_row = lax.axis_index(ROWS) * row_count
    subset_local = subset_index - first_row
    subset_rows = centers[subset_local]
    batch_rows = whole_of(batch_features, (("rows_0", "rows_1"), "rows_2"), 0)
    batch_whole = gather_directly(batch_rows, "cls", 1)
    batch_norm = square_norm(batch_whole)
    pieces = rows_first((centers, subset_rows), "cls", (1, 1))
    center_inner = jnp.einsum(
        "cd,bd->cb", pieces[0], batch_whole, preferred_element_type=jnp.float32
    )
    center_norm = square_norm(pieces[0])
    subset_inner = jnp.einsum(
        "cd,bd->cb", pieces[1], batch_whole, preferred_element_type=jnp.float32
    )
    subset_norm = square_norm(pieces[1])
    center_inner, center_norm, subset_inner, subset_norm = (
        center_inner,
        center_norm,
        subset_inner,
        subset_norm,
    )
    kernel_centers = kernel_block(center_inner, center_norm, batch_norm)
    subset_kernel = kernel_block(subset_inner, subset_norm, batch_norm)
    partial_pred = jnp.dot(coefficients, kernel_centers, precision=lax.Precision.HIGHEST)
    class_count = coefficients.shape[0]
    class_start = lax.axis_index("cls") * class_count
    class_ids = jnp.arange(class_count, dtype=jnp.int32) + class_start
    targets = (batch_labels[None, :] == class_ids[:, None]).astype(jnp.float32)
    basis_part = jnp.dot(eigen_vectors.T, subset_kernel, precision=lax.Precision.HIGHEST)
    predicted, basis_sum = together((partial_pred, basis_part), (("rows_0", "rows_1"), "rows_2"))
    gradient = predicted - targets
    projected = jnp.dot(gradient, basis_sum.T, precision=lax.Precision.HIGHEST)
    correction = jnp.dot(
        projected * eigen_scale[None, :], eigen_vectors.T, precision=lax.Precision.HIGHEST
    )
    batch_local = batch_index - first_row
    is_owned = (batch_local >= 0) & (batch_local < row_count)
    batch_slot = jnp.where(is_owned, batch_local, row_count)
    updated = coefficients.at[:, batch_slot].add(-step_rate * gradient, mode="drop")
    updated = updated.at[:, subset_local].add(step_rate * correction)
    return (predicted, updated)


def solution(mesh):
    finer = Mesh(
        mesh.devices.reshape(16, 4, 2, mesh.shape["cls"]), ("rows_0", "rows_1", "rows_2", "cls")
    )
    placed = (P(ROWS, "cls"), P("cls", ROWS), P(ROWS, "cls"), P(), P(), P(ROWS), P(ROWS, None), P())
    return jax.shard_map(
        shards,
        mesh=finer,
        in_specs=placed,
        out_specs=(P("cls", None), P("cls", ROWS)),
        check_vma=False,
    )
```

profile of v0, /device:TPU:1, one launch (start us, length us, event | category | flops | bytes accessed | tf_op | source)
XLA Modules:
  0.0 340.8 jit_solution(2547921462487290081)
XLA Ops:
  0.6 0.8 broadcast_in_dim.32
  1.4 43.8 %all_to_all.43 = bf16[64,8,320]{2,1,0:T(8,128)(2,1)S(1)} all-to-all(bf16[64,8,320]{2,1,0:T(8,128)(2,1)S(1)} %broadcast_in_dim.32), channel_id=1, replica_groups=mesh['rows_0'=16,'rows_1'=4,'rows_2'=2,'cls'=4] {'rows_0','rows_1'}, dimensions={0} | all-to-all | bytes 655360 | tf_op jit(solution)/shard_map/all_to_all | solution.py:16
  45.3 7.3 %all_to_all.44 = bf16[2,64,8,320]{3,2,1,0:T(8,128)(2,1)S(1)} all-to-all(bf16[2,64,8,320]{3,2,1,0:T(8,128)(2,1)S(1)} %broadcast_in_dim.33), channel_id=1, replica_groups=mesh['rows_0'=16,'rows_1'=4,'rows_2'=2,'cls'=4] {'rows_2'}, dimensions={0} | all-to-all | bytes 1310720 | tf_op jit(solution)/shard_map/all_to_all | solution.py:16
  52.6 0.1 copy.34
  52.6 0.3 copy.35
  52.9 1.8 broadcast_in_dim.34
  54.8 4.3 %all-to-all-start.2 = ((bf16[4,1024,320]{1,2,0:T(8,128)(2,1)}), bf16[4,1024,320]{1,2,0:T(8,128)(2,1)S(1)}, u32[]{:S(2)}, u32[]{:S(2)}) async-start(bf16[4,1024,320]{1,2,0:T(8,128)(2,1)} %broadcast_in_dim.34), calls=%async_computation.2 | async-start | bytes 5242880 | tf_op jit(solution)/shard_map/all_to_all | solution.py:16
  59.1 0.2 copy.32
  59.3 0.7 gather_fusion
  60.0 0.1 copy.33
  60.2 37.9 %all_gather.3 = bf16[1280,320]{1,0:T(8,128)(2,1)S(1)} all-gather(bf16[320,320]{1,0:T(8,128)(2,1)S(1)} %pad_maximum_fusion.1), channel_id=1, replica_groups=mesh['rows_0'=16,'rows_1'=4,'rows_2'=2,'cls'=4] {'cls'}, dimensions={0}, use_global_device_ids=true | all-gather | bytes 1024000 | tf_op jit(solution)/shard_map/all_gather | solution.py:39
  98.1 0.2 multiply_reduce_fusion.2
  98.2 0.8 copy-done.1
  99.0 0.2 multiply_reduce_fusion.1
  99.2 0.6 multiply_reduce_fusion
  99.8 0.6 copy-done.2
  100.4 1.2 fusion.7
  101.7 2.8 convolution_bitcast_fusion.1
  104.5 2.5 copy.36
  107.0 2.3 reshape.35
  109.3 1.6 fusion.16
  111.0 1.8 convolution_bitcast_fusion
  112.8 1.9 copy.37
  114.7 2.1 copy.44
  116.9 1.9 pad_maximum_fusion
  118.8 4.3 %reshape_reshape.8 = f32[64,2,6096]{2,1,0:T(2,128)S(1)} reshape(f32[780288]{0:T(1024)} %pad_maximum_fusion) | data formatting | bytes 6242304 | tf_op jit(solution)/shard_map/reshape;reshape | solution.py:49
  123.1 1.8 copy.38
  124.9 10.5 %all_to_all.45 = f32[2,64,6096]{2,1,0:T(8,128)S(1)} all-to-all(f32[2,64,6096]{2,1,0:T(8,128)S(1)} %copy.38), channel_id=1, replica_groups=mesh['rows_0'=16,'rows_1'=4,'rows_2'=2,'cls'=4] {'rows_2'}, dimensions={0} | all-to-all | bytes 6242304 | tf_op jit(solution)/shard_map/all_to_all | solution.py:55
  135.4 1.5 reduce_sum.48
  136.9 2.5 all_to_all.31
  139.4 80.4 %all_to_all.46 = f32[64,1,6096]{2,1,0:T(1,128)S(1)} all-to-all(f32[64,1,6096]{2,1,0:T(1,128)S(1)} %all_to_all.31), channel_id=1, replica_groups=mesh['rows_0'=16,'rows_1'=4,'rows_2'=2,'cls'=4] {'rows_0','rows_1'}, dimensions={0} | all-to-all | bytes 3121152 | tf_op jit(solution)/shard_map/all_to_all | solution.py:63
  219.8 1.0 reduce_sum.49
  220.9 2.0 broadcast_in_dim.35
  222.8 8.2 %all-to-all-start.5 = ((f32[64,1,6096]{2,1,0:T(1,128)}), f32[64,1,6096]{2,1,0:T(1,128)S(1)}, u32[]{:S(2)}, u32[]{:S(2)}) async-start(f32[64,1,6096]{2,1,0:T(1,128)} %broadcast_in_dim.35), calls=%async_computation.5 | async-start | bytes 3145728 | tf_op jit(solution)/shard_map/all_to_all | solution.py:16
  231.0 0.1 copy.40
  231.2 72.8 %all-to-all-done.5 = f32[64,1,6096]{2,1,0:T(1,128)S(1)} async-done(((f32[64,1,6096]{2,1,0:T(1,128)}), f32[64,1,6096]{2,1,0:T(1,128)S(1)}, u32[]{:S(2)}, u32[]{:S(2)}) %all-to-all-start.5) | async-done | bytes 1560608 | tf_op jit(solution)/shard_map/all_to_all | solution.py:16
  304.0 0.5 copy.46
  304.5 0.4 broadcast_in_dim.36
  304.8 11.7 %all_to_all.47 = f32[2,64,6096]{2,1,0:T(8,128)S(1)} all-to-all(f32[2,64,6096]{2,1,0:T(8,128)S(1)} %broadcast_in_dim.36), channel_id=1, replica_groups=mesh['rows_0'=16,'rows_1'=4,'rows_2'=2,'cls'=4] {'rows_2'}, dimensions={0} | all-to-all | bytes 6242304 | tf_op jit(solution)/shard_map/all_to_all | solution.py:16
  316.6 4.1 %copy.39 = f32[64,2,6096]{2,1,0:T(2,128)} copy(f32[64,2,6096]{2,0,1:T(8,128)S(1)} %bitcast.34) | data formatting | bytes 6242304 | tf_op jit(solution)/shard_map/transpose | solution.py:28
  320.7 6.1 %slice.18 = f32[762,1024]{1,0:T(8,128)S(1)} reshape(f32[64,2,6096]{2,1,0:T(2,128)} %copy.39) | data formatting | bytes 6242304 | tf_op jit(solution)/shard_map/slice | solution.py:85
  326.8 1.2 multiply_bitcast_fusion
  328.0 2.1 fusion.8
  330.2 0.6 fusion.17
  330.8 1.6 copy.41
  332.4 6.5 %scatter_fusion = f32[250,256]{0,1:T(8,128)S(1)} fusion(f32[250,256]{0,1:T(8,128)S(1)} %copy.40, s32[1024]{0:T(1024)S(1)} %compare_select_fusion, f32[1024,250]{1,0:T(8,128)S(1)} %copy.41), kind=kCustom, calls=%fused_computation.1 | custom fusion | flops 256000 | bytes 3076096 | tf_op jit(solution)/shard_map/scatter-add | solution.py:146
  338.8 1.1 scatter_fusion.1
  339.9 0.8 copy.42
  (27 shorter events, 0.2 us)
Async XLA Ops:
  0.6 110.4 %copy-start = (f32[64,512]{1,0:T(8,128)S(1)}, f32[64,512]{1,0:T(8,128)}, u32[]{:S(2)}) copy-start(f32[64,512]{1,0:T(8,128)} %param.14) | copy-start | bytes 393220
  54.8 4.3 %copy-start.6 = (bf16[256,320]{0,1:T(8,128)(2,1)S(1)}, bf16[256,320]{0,1:T(8,128)(2,1)}, u32[]{:S(2)}) copy-start(bf16[256,320]{0,1:T(8,128)(2,1)} %param.8) | copy-start | bytes 491524
  54.8 4.5 %copy-start.10 = (s32[64]{0:T(128)S(1)}, s32[64]{0:T(128)}, u32[]{:S(2)}) copy-start(s32[64]{0:T(128)} %param.13) | copy-start | bytes 772
  54.8 44.5 %all-to-all-start.2 = ((bf16[4,1024,320]{1,2,0:T(8,128)(2,1)}), bf16[4,1024,320]{1,2,0:T(8,128)(2,1)S(1)}, u32[]{:S(2)}, u32[]{:S(2)}) async-start(bf16[4,1024,320]{1,2,0:T(8,128)(2,1)} %broadcast_in_dim.34), calls=%async_computation.2 | async-start | bytes 5242880 | tf_op jit(solution)/shard_map/all_to_all | solution.py:16
  98.1 1.0 copy-start.1
  99.2 1.2 copy-start.2
  100.4 1.2 copy-start.5
  114.7 2.2 copy-start.4
  220.8 10.3 %copy-start.8 = (s32[1024]{0:T(1024)S(1)}, s32[1024]{0:T(1024)}, u32[]{:S(2)}) copy-start(s32[1024]{0:T(1024)} %param.12) | copy-start | bytes 12292
  222.8 81.2 %all-to-all-start.5 = ((f32[64,1,6096]{2,1,0:T(1,128)}), f32[64,1,6096]{2,1,0:T(1,128)S(1)}, u32[]{:S(2)}, u32[]{:S(2)}) async-start(f32[64,1,6096]{2,1,0:T(1,128)} %broadcast_in_dim.35), calls=%async_computation.5 | async-start | bytes 3145728 | tf_op jit(solution)/shard_map/all_to_all | solution.py:16
  320.7 6.1 %copy-start.7 = (s32[1024]{0:T(1024)S(1)}, s32[1024]{0:T(1024)}, u32[]{:S(2)}) copy-start(s32[1024]{0:T(1024)} %param.11) | copy-start | bytes 12292
  326.8 1.2 copy-start.9
  328.0 2.2 copy-start.3
where the time goes:
time: 342 us; the launch traced here: 341 us
  blocking collectives  192 us (56%)
  waiting for transfers between devices  72.8 us (21%)
  local copies, waits for them, and re-layouts  38.5 us (11%)
  other arithmetic  14.2 us (4%)
  starting transfers between devices  12.5 us (4%)
  matrix products  10.2 us (3%)
    all_to_all x1, blocking collectives, sum_in_two_steps(): lax.all_to_all(nearer, far, split_axis=0, concat_axis=0, tiled=True)  80.4 us
    all_to_all x2, waiting for transfers between devices, sent_to_all(): return lax.all_to_all(copies, axis, split_axis=0, concat_axis=0, tiled=True)  72.8 us
    all_to_all x3, blocking collectives, sent_to_all(): return lax.all_to_all(copies, axis, split_axis=0, concat_axis=0, tiled=True)  62.8 us
    all_gather x1, blocking collectives, rows_first(): filled, at, done = (lax.all_gather(both, axis, axis=0, tiled=True), 0, [])  37.9 us
    all_to_all x2, starting transfers between devices, sent_to_all(): return lax.all_to_all(copies, axis, split_axis=0, concat_axis=0, tiled=True)  12.5 us
    all_to_all x1, blocking collectives, sent_and_summed(): tiles = lax.all_to_all(cut_along(value, dim, count), axis, 0, 0, tiled=True)  10.5 us
  transfers between devices with their start and end apart: 2, of which 1 were waited for; matrix products, arithmetic and copies ran while one was open for 0% of the time, Pallas kernels for 0%

commit v1 on v0

v1 whole, which is shorter than its diff:
```python
import functools

import jax
import jax.numpy as jnp
from jax import lax
from jax.experimental import pallas as pl
from jax.experimental.pallas import tpu as pltpu
from jax.sharding import Mesh
from jax.sharding import PartitionSpec as P

Z, X, K, Y = "rows_z", "rows_x", "rows_k", "cls"
ROWS = (Z, X, K)
LANES = 128
INTERPRET = False

spread = 4.0
step_rate = 0.5

HIGHEST = lax.Precision.HIGHEST
LAST = (((1,), (1,)), ((), ()))
FIRST = (((0,), (0,)), ((), ()))


def gathered(value, axis):
    copies = jnp.broadcast_to(value, (lax.axis_size(axis), *value.shape))
    return lax.all_to_all(copies, axis, 0, 0, tiled=True)


def scattered(tiles, axis):
    return jnp.sum(lax.all_to_all(tiles, axis, 0, 0, tiled=True), axis=0)


def kernel_products(
    place, batch, centers, coefficients, basis, sums, norms, *, classes, padded, split
):
    block = pl.program_id(0)
    cores, chips, _, depth, rows, width = batch.shape
    groups = centers.shape[0]
    count = centers.shape[1]

    @pl.when(block == 0)
    def _():
        total = jnp.zeros((count, 1), jnp.float32)
        for y in range(groups):
            own = centers[y].astype(jnp.float32)
            total += jnp.sum(own * own, axis=1, keepdims=True)
        norms[...] = jnp.broadcast_to(total, norms.shape)
        for b in range(sums.shape[0]):
            sums[b, classes:padded, :] = jnp.zeros((padded - classes, LANES), jnp.float32)

    inner = jnp.zeros((count, LANES), jnp.float32)
    squares = jnp.zeros((8, LANES), jnp.float32)
    ones = jnp.ones((8, width), jnp.float32)
    for y in range(groups):
        pieces = [
            batch[k, x, y, z]
            for z in range(depth)
            for x in range(chips)
            for k in range(cores)
        ]
        lines = jnp.concatenate(pieces, axis=0)
        inner += lax.dot_general(centers[y], lines, LAST, preferred_element_type=jnp.float32)
        wide = lines.astype(jnp.float32)
        squares += lax.dot_general(
            ones, wide * wide, LAST, precision=HIGHEST, preferred_element_type=jnp.float32
        )
    squared = norms[...] + squares[:1] - 2.0 * inner
    values = jnp.exp(-jnp.sqrt(jnp.maximum(squared, 0.0)) / spread)
    outputs = jnp.dot(
        coefficients[...], values, precision=HIGHEST, preferred_element_type=jnp.float32
    )
    sums[pl.ds(block, 1), :classes, :] = outputs[None]
    own = basis[...].reshape(-1, count)
    part = jnp.dot(own, values, precision=HIGHEST, preferred_element_type=jnp.float32)
    start = pl.multiple_of(padded + block * split, 8)
    sums[:, pl.ds(start, split), :] = part.reshape(-1, split, LANES)


def project(place, predicted, basis, labels, projected, *, classes):
    block = pl.program_id(0)
    rows = predicted.shape[1]
    ids = lax.broadcasted_iota(jnp.int32, (rows, LANES), 0) + place[0] * classes
    gradient = predicted[0] - (labels[0] == ids).astype(jnp.float32)
    own = basis[...].reshape(-1, LANES)
    part = lax.dot_general(
        own, gradient, LAST, precision=HIGHEST, preferred_element_type=jnp.float32
    )

    @pl.when(block == 0)
    def _():
        projected[...] = part

    @pl.when(block > 0)
    def _():
        projected[...] += part


def step_batch(place, predicted, labels, index, coefficients, output, updated, *, classes):
    block = pl.program_id(0)
    rows = predicted.shape[1]
    count = coefficients.shape[1]
    ids = lax.broadcasted_iota(jnp.int32, (rows, LANES), 0) + place[0] * classes
    gradient = predicted[0] - (labels[0] == ids).astype(jnp.float32)
    output[...] = predicted[0, :classes]
    slots = lax.broadcasted_iota(jnp.int32, (count, LANES), 0) + place[1] * count
    hits = (index[0] == slots).astype(jnp.float32)
    part = lax.dot_general(
        gradient, hits, LAST, precision=HIGHEST, preferred_element_type=jnp.float32
    )

    @pl.when(block == 0)
    def _():
        updated[...] = coefficients[...] - step_rate * part[:classes]

    @pl.when(block > 0)
    def _():
        updated[...] += -step_rate * part[:classes]


def correct(updated, projected, weights, result):
    classes = updated.shape[0]
    change = lax.dot_general(
        projected[...], weights[...], FIRST, precision=HIGHEST, preferred_element_type=jnp.float32
    )
    result[...] = updated[...] + change[:classes]


def shards(
    centers,
    coefficients,
    batch_features,
    batch_labels,
    batch_index,
    subset_index,
    eigen_vectors,
    eigen_scale,
):
    depth, chips, cores, groups = (lax.axis_size(a) for a in (Z, X, K, Y))
    blocks = chips * cores
    count = centers.shape[0]
    classes = coefficients.shape[0]
    rank = lax.axis_index(ROWS)
    place = jnp.stack([lax.axis_index(Y), rank]).astype(jnp.int32)
    vectors = eigen_vectors.shape[1]
    split = vectors // groups // blocks
    padded = -(-classes // 8) * 8
    while (padded + vectors // groups) % (8 * depth):
        padded += 8
    lines = padded + vectors // groups
    batch = blocks * LANES
    near = depth // blocks

    centers_all = gathered(centers, Y)
    batch_all = batch_features
    for axis in (Z, Y, X, K):
        batch_all = gathered(batch_all, axis)

    spots = jnp.arange(count, dtype=jnp.int32) + rank * count
    chosen = (subset_index[:, None] == spots[None, :]).astype(jnp.float32)
    lifted = lax.dot_general(eigen_vectors, chosen, FIRST, precision=HIGHEST)
    weights = lifted * (step_rate * eigen_scale)[:, None]
    labels = batch_labels.reshape(blocks, 1, LANES)
    index = batch_index.reshape(blocks, 1, LANES)

    whole = lambda shape: pl.BlockSpec(shape, lambda j, p: (0,) * len(shape))
    sums = pl.pallas_call(
        functools.partial(kernel_products, classes=classes, padded=padded, split=split),
        out_shape=jax.ShapeDtypeStruct((blocks, lines, LANES), jnp.float32),
        grid_spec=pltpu.PrefetchScalarGridSpec(
            num_scalar_prefetch=1,
            grid=(blocks,),
            in_specs=[
                pl.BlockSpec(
                    (cores, chips, groups, near, *batch_features.shape),
                    lambda j, p: (0, 0, 0, j, 0, 0),
                ),
                whole(centers_all.shape),
                whole(coefficients.shape),
                pl.BlockSpec(
                    (blocks, None, split, count), lambda j, p: (0, p[0], 0, 0)
                ),
            ],
            out_specs=whole((blocks, lines, LANES)),
            scratch_shapes=[pltpu.VMEM((count, LANES), jnp.float32)],
        ),
        interpret=INTERPRET,
        name="kernel_products",
    )(
        place,
        batch_all,
        centers_all,
        coefficients,
        lifted.reshape(blocks, groups, split, count),
    )

    own = scattered(sums.reshape(cores, chips, lines, LANES), K)
    own = scattered(own, X)
    own = scattered(own.reshape(depth, lines // depth, LANES), Z)
    own = gathered(own, Z).reshape(lines, LANES)
    basis = gathered(own[padded:].reshape(blocks, split, LANES), Y)
    predicted = gathered(gathered(own[:padded], X), K).reshape(blocks, padded, LANES)

    part = pl.pallas_call(
        functools.partial(project, classes=classes),
        out_shape=jax.ShapeDtypeStruct((groups * split, padded), jnp.float32),
        grid_spec=pltpu.PrefetchScalarGridSpec(
            num_scalar_prefetch=1,
            grid=(blocks,),
            in_specs=[
                pl.BlockSpec((1, padded, LANES), lambda j, p: (j, 0, 0)),
                pl.BlockSpec((groups, None, split, LANES), lambda j, p: (0, j, 0, 0)),
                pl.BlockSpec((1, 1, LANES), lambda j, p: (j, 0, 0)),
            ],
            out_specs=whole((groups * split, padded)),
        ),
        interpret=INTERPRET,
        name="project",
    )(place, predicted, basis, labels)
    projected = gathered(gathered(part, X), K).reshape(vectors, padded)

    output, updated = pl.pallas_call(
        functools.partial(step_batch, classes=classes),
        out_shape=(
            jax.ShapeDtypeStruct((classes, batch), jnp.float32),
            jax.ShapeDtypeStruct((classes, count), jnp.float32),
        ),
        grid_spec=pltpu.PrefetchScalarGridSpec(
            num_scalar_prefetch=1,
            grid=(blocks,),
            in_specs=[
                pl.BlockSpec((1, padded, LANES), lambda j, p: (j, 0, 0)),
                pl.BlockSpec((1, 1, LANES), lambda j, p: (j, 0, 0)),
                pl.BlockSpec((1, 1, LANES), lambda j, p: (j, 0, 0)),
                whole(coefficients.shape),
            ],
            out_specs=(
                pl.BlockSpec((classes, LANES), lambda j, p: (0, j)),
                whole((classes, count)),
            ),
        ),
        interpret=INTERPRET,
        name="step_batch",
    )(place, predicted, labels, index, coefficients)

    result = pl.pallas_call(
        correct,
        out_shape=jax.ShapeDtypeStruct((classes, count), jnp.float32),
        interpret=INTERPRET,
        name="correct",
    )(updated, projected, weights)
    return (output, result)


def solution(mesh, shape=(16, 4, 2)):
    finer = Mesh(mesh.devices.reshape(*shape, mesh.shape["cls"]), (*ROWS, Y))
    placed = (P(ROWS, Y), P(Y, ROWS), P(ROWS, Y), P(), P(), P(ROWS), P(ROWS, None), P())
    return jax.shard_map(
        shards,
        mesh=finer,
        in_specs=placed,
        out_specs=(P(Y, None), P(Y, ROWS)),
        check_vma=False,
    )
```

time: 342 us -> 226 us (0.66)
  waiting for transfers between devices: 72.8 us -> 17 us
  blocking collectives: 192 us -> 148 us
  Pallas kernels: 0 us -> 38.5 us
  local copies, waits for them, and re-layouts: 38.5 us -> 7.22 us
  other arithmetic: 14.2 us -> 0.88 us
  matrix products: 10.2 us -> 1.5 us
    all_to_all x2 -> x3, waiting for transfers between devices: 72.8 us -> 17 us  [gathered(): return lax.all_to_all(copies, axis, 0, 0, tiled=True)]
    pallas_call x0 -> x4, Pallas kernels: none -> 38.5 us  [the longest x1 21.7 us: shards(): pl.pallas_call(functools.partial(kernel_products, classes=classes, padded...]
    all_gather x1 -> x0, blocking collectives: 37.9 us -> none  [rows_first(): filled, at, done = (lax.all_gather(both, axis, axis=0, tiled=True), 0, [])]
    dot_general x6 -> x1, matrix products: 10.2 us -> 1.5 us  [shards(): lifted = lax.dot_general(eigen_vectors, chosen, FIRST, precision=HIGHEST)]
    scatter-add x2 -> x0, other arithmetic: 7.54 us -> none  [the longest x1 6.48 us: shards(): coefficients.at[:, batch_slot].add(-step_rate * gradient, mode='drop')]
    transpose x4 -> x0, local copies, waits for them, and re-layouts: 6.12 us -> none  [the longest x2 4.17 us: whole_of(): tiles = jnp.swapaxes(sent_to_all(first, near), 0, 1)]
    slice x1 -> x2, local copies, waits for them, and re-layouts: 6.11 us -> 0.02 us  [the longest x1 0.01 us: shards(): own[:padded]]
    all_to_all x5 -> x11, blocking collectives: 154 us -> 148 us  [the longest x8 109 us: gathered(): return lax.all_to_all(copies, axis, 0, 0, tiled=True)]
  transfers between devices with their start and end apart: 2 -> 3, of which waited for: 1 -> 2; matrix products, arithmetic and copies ran while one was open for 0% -> 1% of each run, Pallas kernels for 0% -> 3%
where the time goes in v1:
time: 226 us; the launch traced here: 225 us
  blocking collectives  148 us (65%)
  Pallas kernels  38.5 us (17%)
  waiting for transfers between devices  17 us (8%)
  starting transfers between devices  11 us (5%)
  local copies, waits for them, and re-layouts  7.22 us (3%)
    all_to_all x8, blocking collectives, gathered(): return lax.all_to_all(copies, axis, 0, 0, tiled=True)  109 us
    all_to_all x3, blocking collectives, scattered(): return jnp.sum(lax.all_to_all(tiles, axis, 0, 0, tiled=True), axis=0)  39.2 us
    pallas_call x1, Pallas kernels, shards(): pl.pallas_call(functools.partial(kernel_products, classes=classes, padded...  21.7 us
    all_to_all x3, waiting for transfers between devices, gathered(): return lax.all_to_all(copies, axis, 0, 0, tiled=True)  17 us
    all_to_all x3, starting transfers between devices, gathered(): return lax.all_to_all(copies, axis, 0, 0, tiled=True)  11 us
    pallas_call x1, Pallas kernels, shards(): pl.pallas_call(functools.partial(step_batch, classes=classes), out_shape=...  7.7 us
    pallas_call x1, Pallas kernels, shards(): pl.pallas_call(functools.partial(project, classes=classes), out_shape=jax...  6.37 us
    broadcast_in_dim x11, local copies, waits for them, and re-layouts, gathered(): copies = jnp.broadcast_to(value, (lax.axis_size(axis), *value.shape))  6.03 us
  transfers between devices with their start and end apart: 3, of which 2 were waited for; matrix products, arithmetic and copies ran while one was open for 1% of the time, Pallas kernels for 3%

profile of v1, /device:TPU:1, one launch (start us, length us, event | category | flops | bytes accessed | tf_op | source)
XLA Modules:
  0.0 224.6 jit_solution(1788897533349796728)
XLA Ops:
  0.6 0.0 copy-start
  0.6 0.7 broadcast_in_dim.36
  1.4 27.4 %all_to_all.70 = bf16[16,8,320]{2,1,0:T(8,128)(2,1)S(1)} all-to-all(bf16[16,8,320]{2,1,0:T(8,128)(2,1)S(1)} %broadcast_in_dim.36), channel_id=1, replica_groups=mesh['rows_z'=16,'rows_x'=4,'rows_k'=2,'cls'=4] {'rows_z'}, dimensions={0} | all-to-all | bytes 163840 | tf_op jit(solution)/shard_map/all_to_all | solution.py:26
  28.8 1.0 broadcast_in_dim.40
  29.7 11.6 %all_to_all.71 = bf16[4,256,320]{1,2,0:T(8,128)(2,1)S(1)} all-to-all(bf16[4,256,320]{1,2,0:T(8,128)(2,1)S(1)} %broadcast_in_dim.40), channel_id=1, replica_groups=mesh['rows_z'=16,'rows_x'=4,'rows_k'=2,'cls'=4] {'cls'}, dimensions={0} | all-to-all | bytes 1310720 | tf_op jit(solution)/shard_map/all_to_all | solution.py:26
  41.4 8.6 %all_to_all.72 = bf16[4,16,8,320]{3,2,1,0:T(8,128)(2,1)S(1)} all-to-all(bf16[4,16,8,320]{3,2,1,0:T(8,128)(2,1)S(1)} %broadcast_in_dim.37), channel_id=1, replica_groups=mesh['rows_z'=16,'rows_x'=4,'rows_k'=2,'cls'=4] {'cls'}, dimensions={0} | all-to-all | bytes 655360 | tf_op jit(solution)/shard_map/all_to_all | solution.py:26
  50.0 1.4 broadcast_in_dim.38
  51.4 0.0 copy-start.2
  51.4 0.0 copy-start.3
  51.4 4.1 %all-to-all-start.2 = ((bf16[4,4,16,8,320]{4,3,2,1,0:T(8,128)(2,1)}), bf16[4,4,16,8,320]{4,3,2,1,0:T(8,128)(2,1)S(1)}, u32[]{:S(2)}, u32[]{:S(2)}) async-start(bf16[4,4,16,8,320]{4,3,2,1,0:T(8,128)(2,1)} %broadcast_in_dim.38), calls=%async_computation.2 | async-start | bytes 3145728 | tf_op jit(solution)/shard_map/all_to_all | solution.py:26
  55.6 0.7 pad_add_fusion.place
  56.2 0.0 copy-done.2
  56.2 0.0 copy-done
  56.2 0.0 copy-done.3
  56.2 1.5 bitcast_multiply_fusion
  57.7 1.2 copy.15.centers
  58.9 11.6 %all-to-all-done.2 = bf16[4,4,16,8,320]{4,3,2,1,0:T(8,128)(2,1)S(1)} async-done(((bf16[4,4,16,8,320]{4,3,2,1,0:T(8,128)(2,1)}), bf16[4,4,16,8,320]{4,3,2,1,0:T(8,128)(2,1)S(1)}, u32[]{:S(2)}, u32[]{:S(2)}) %all-to-all-start.2) | async-done | bytes 1310752 | tf_op jit(solution)/shard_map/all_to_all | solution.py:26
  70.5 0.5 broadcast_in_dim.39
  70.9 13.6 %all_to_all.73.batch = bf16[2,4,4,16,8,320]{5,4,3,2,1,0:T(8,128)(2,1)} all-to-all(bf16[2,4,4,16,8,320]{5,4,3,2,1,0:T(8,128)(2,1)S(1)} %broadcast_in_dim.39), channel_id=1, replica_groups=mesh['rows_z'=16,'rows_x'=4,'rows_k'=2,'cls'=4] {'rows_k'}, dimensions={0} | all-to-all | bytes 5242880 | tf_op jit(solution)/shard_map/all_to_all | solution.py:26
  84.6 21.7 %kernel_products.1 = f32[8,384,128]{2,1,0:T(8,128)} custom-call(s32[2]{0:T(128)} %pad_add_fusion.place, bf16[2,4,4,16,8,320]{5,4,3,2,1,0:T(8,128)(2,1)} %all_to_all.73.batch, bf16[4,256,320]{2,1,0:T(8,128)(2,1)} %copy.15.centers, f32[250,256]{1,0:T(8,128)} %coefficients.3, f32[8,4,16,256]{3,2,1,0:T(8,128)} %bitcast.18), custom_call_target="tpu_custom_call" | custom-call | tf_op jit(solution)/shard_map/kernel_products/pallas_call | solution.py:166
  106.3 6.2 %all_to_all.74 = f32[2,4,384,128]{3,2,1,0:T(8,128)S(1)} all-to-all(f32[2,4,384,128]{3,2,1,0:T(8,128)} %bitcast.17), channel_id=1, replica_groups=mesh['rows_z'=16,'rows_x'=4,'rows_k'=2,'cls'=4] {'rows_k'}, dimensions={0} | all-to-all | bytes 3145728 | tf_op jit(solution)/shard_map/all_to_all | solution.py:30
  112.4 0.2 reduce_sum.27
  112.6 14.4 %all_to_all.75 = f32[4,384,128]{2,1,0:T(8,128)S(1)} all-to-all(f32[4,384,128]{2,1,0:T(8,128)S(1)} %reduce_sum.27), channel_id=1, replica_groups=mesh['rows_z'=16,'rows_x'=4,'rows_k'=2,'cls'=4] {'rows_x'}, dimensions={0} | all-to-all | bytes 1572864 | tf_op jit(solution)/shard_map/all_to_all | solution.py:30
  127.1 18.6 %all_to_all.76 = f32[16,24,128]{2,1,0:T(8,128)S(1)} all-to-all(f32[16,24,128]{2,1,0:T(8,128)S(1)} %bitcast.20), channel_id=1, replica_groups=mesh['rows_z'=16,'rows_x'=4,'rows_k'=2,'cls'=4] {'rows_z'}, dimensions={0} | all-to-all | bytes 393216 | tf_op jit(solution)/shard_map/all_to_all | solution.py:30
  145.7 20.7 %all_to_all.77 = f32[16,24,128]{2,1,0:T(8,128)S(1)} all-to-all(f32[16,24,128]{2,1,0:T(8,128)S(1)} %broadcast_in_dim.41), channel_id=1, replica_groups=mesh['rows_z'=16,'rows_x'=4,'rows_k'=2,'cls'=4] {'rows_z'}, dimensions={0} | all-to-all | bytes 393216 | tf_op jit(solution)/shard_map/all_to_all | solution.py:26
  166.5 0.7 broadcast_in_dim.44
  167.2 3.4 %all-to-all-start.11 = ((f32[4,8,16,128]{3,2,1,0:T(8,128)}), f32[4,8,16,128]{3,2,1,0:T(8,128)S(1)}, u32[]{:S(2)}, u32[]{:S(2)}) async-start(f32[4,8,16,128]{3,2,1,0:T(8,128)} %broadcast_in_dim.44), calls=%async_computation.11 | async-start | bytes 524288 | tf_op jit(solution)/shard_map/all_to_all | solution.py:26
  170.6 5.5 %all-to-all-done.11.basis = f32[4,8,16,128]{3,2,1,0:T(8,128)S(1)} async-done(((f32[4,8,16,128]{3,2,1,0:T(8,128)}), f32[4,8,16,128]{3,2,1,0:T(8,128)S(1)}, u32[]{:S(2)}, u32[]{:S(2)}) %all-to-all-start.11) | async-done | bytes 262176 | tf_op jit(solution)/shard_map/all_to_all | solution.py:26
  176.1 0.0 copy-start.1
  176.1 9.3 %all_to_all.78 = f32[4,256,128]{2,1,0:T(8,128)S(1)} all-to-all(f32[4,256,128]{2,1,0:T(8,128)S(1)} %broadcast_in_dim.42), channel_id=1, replica_groups=mesh['rows_z'=16,'rows_x'=4,'rows_k'=2,'cls'=4] {'rows_x'}, dimensions={0} | all-to-all | bytes 1048576 | tf_op jit(solution)/shard_map/all_to_all | solution.py:26
  185.5 0.1 broadcast_in_dim.43
  185.6 0.0 copy-done.1
  185.6 12.4 %all_to_all.79 = f32[2,4,256,128]{3,2,1,0:T(8,128)} all-to-all(f32[2,4,256,128]{3,2,1,0:T(8,128)S(1)} %broadcast_in_dim.43), channel_id=1, replica_groups=mesh['rows_z'=16,'rows_x'=4,'rows_k'=2,'cls'=4] {'rows_k'}, dimensions={0} | all-to-all | bytes 2097152 | tf_op jit(solution)/shard_map/all_to_all | solution.py:26
  197.9 6.4 %project.1 = f32[64,256]{1,0:T(8,128)} custom-call(s32[2]{0:T(128)} %pad_add_fusion.place, f32[8,256,128]{2,1,0:T(8,128)} %bitcast.15, f32[4,8,16,128]{3,2,1,0:T(8,128)} %copy-done.1, s32[8,1,128]{2,1,0:T(1,128)} %bitcast.24), custom_call_target="tpu_custom_call" | custom-call | tf_op jit(solution)/shard_map/project/pallas_call | solution.py:203
  204.3 1.6 broadcast_in_dim.45
  205.9 3.4 %all-to-all-start.12 = ((f32[4,64,256]{2,1,0:T(8,128)}), f32[4,64,256]{2,1,0:T(8,128)S(1)}, u32[]{:S(2)}, u32[]{:S(2)}) async-start(f32[4,64,256]{2,1,0:T(8,128)} %broadcast_in_dim.45), calls=%async_computation.12 | async-start | bytes 524288 | tf_op jit(solution)/shard_map/all_to_all | solution.py:26
  209.3 7.7 %step_batch.1 = (f32[250,1024]{1,0:T(8,128)}, f32[250,256]{1,0:T(8,128)}) custom-call(s32[2]{0:T(128)} %pad_add_fusion.place, f32[8,256,128]{2,1,0:T(8,128)} %bitcast.16, s32[8,1,128]{2,1,0:T(1,128)} %bitcast.25, s32[8,1,128]{2,1,0:T(1,128)} %bitcast.26, f32[250,256]{1,0:T(8,128)} %coefficients.3), custom_call_target="tpu_custom_call" | custom-call | tf_op jit(solution)/shard_map/step_batch/pallas_call | solution.py:221
  217.0 0.0 all-to-all-done.12
  217.0 4.9 %all_to_all.80 = f32[2,4,64,256]{3,2,1,0:T(8,128)} all-to-all(f32[2,4,64,256]{3,2,1,0:T(8,128)S(1)} %broadcast_in_dim.46), channel_id=1, replica_groups=mesh['rows_z'=16,'rows_x'=4,'rows_k'=2,'cls'=4] {'rows_k'}, dimensions={0} | all-to-all | bytes 1048576 | tf_op jit(solution)/shard_map/all_to_all | solution.py:26
  221.9 2.7 %correct.1 = f32[250,256]{1,0:T(8,128)} custom-call(f32[250,256]{1,0:T(8,128)} %get-tuple-element.5.updated, f32[512,256]{1,0:T(8,128)} %bitcast.19, f32[512,256]{1,0:T(8,128)} %get-tuple-element.6.weights), custom_call_target="tpu_custom_call" | custom-call | tf_op jit(solution)/shard_map/correct/pallas_call | solution.py:245
  (10 shorter events, 0.2 us)
Async XLA Ops:
  0.6 55.6 %copy-start = (f32[64,512]{1,0:T(8,128)S(1)}, f32[64,512]{1,0:T(8,128)}, u32[]{:S(2)}) copy-start(f32[64,512]{1,0:T(8,128)} %param.14) | copy-start | bytes 393220
  51.4 4.8 %copy-start.2 = (f32[512]{0:T(512)S(1)}, f32[512]{0:T(512)}, u32[]{:S(2)}) copy-start(f32[512]{0:T(512)} %param.15) | copy-start | bytes 6148
  51.4 4.8 %copy-start.3 = (s32[64]{0:T(128)S(1)}, s32[64]{0:T(128)}, u32[]{:S(2)}) copy-start(s32[64]{0:T(128)} %param.13) | copy-start | bytes 772
  51.4 19.0 %all-to-all-start.2 = ((bf16[4,4,16,8,320]{4,3,2,1,0:T(8,128)(2,1)}), bf16[4,4,16,8,320]{4,3,2,1,0:T(8,128)(2,1)S(1)}, u32[]{:S(2)}, u32[]{:S(2)}) async-start(bf16[4,4,16,8,320]{4,3,2,1,0:T(8,128)(2,1)} %broadcast_in_dim.38), calls=%async_computation.2 | async-start | bytes 3145728 | tf_op jit(solution)/shard_map/all_to_all | solution.py:26
  167.2 8.9 %all-to-all-start.11 = ((f32[4,8,16,128]{3,2,1,0:T(8,128)}), f32[4,8,16,128]{3,2,1,0:T(8,128)S(1)}, u32[]{:S(2)}, u32[]{:S(2)}) async-start(f32[4,8,16,128]{3,2,1,0:T(8,128)} %broadcast_in_dim.44), calls=%async_computation.11 | async-start | bytes 524288 | tf_op jit(solution)/shard_map/all_to_all | solution.py:26
  176.1 9.4 %copy-start.1 = (f32[4,8,16,128]{3,2,1,0:T(8,128)}, f32[4,8,16,128]{3,2,1,0:T(8,128)S(1)}, u32[]{:S(2)}) copy-start(f32[4,8,16,128]{3,2,1,0:T(8,128)S(1)} %all-to-all-done.11.basis) | copy-start | bytes 786436
  205.9 11.1 %all-to-all-start.12 = ((f32[4,64,256]{2,1,0:T(8,128)}), f32[4,64,256]{2,1,0:T(8,128)S(1)}, u32[]{:S(2)}, u32[]{:S(2)}) async-start(f32[4,64,256]{2,1,0:T(8,128)} %broadcast_in_dim.45), calls=%async_computation.12 | async-start | bytes 524288 | tf_op jit(solution)/shard_map/all_to_all | solution.py:26

commit v2 on v0

v2 whole, which is shorter than its diff:
```python
import functools

import jax
import jax.numpy as jnp
from jax import lax
from jax.experimental import pallas as pl
from jax.experimental.pallas import tpu as pltpu
from jax.sharding import Mesh
from jax.sharding import PartitionSpec as P

Z, X, K, Y = "rows_z", "rows_x", "rows_k", "cls"
ROWS = (Z, X, K)
LANES = 128
INTERPRET = False

spread = 4.0
step_rate = 0.5

HIGHEST = lax.Precision.HIGHEST
LAST = (((1,), (1,)), ((), ()))
FIRST = (((0,), (0,)), ((), ()))


def gathered(value, axis):
    copies = jnp.broadcast_to(value, (lax.axis_size(axis), *value.shape))
    return lax.all_to_all(copies, axis, 0, 0, tiled=True)


def scattered(tiles, axis):
    return jnp.sum(lax.all_to_all(tiles, axis, 0, 0, tiled=True), axis=0)


def in_two(value):
    high = value.astype(jnp.bfloat16)
    low = (value - high.astype(jnp.float32)).astype(jnp.bfloat16)
    return high, low


def product(left, right, dims):
    (a, b), (c, d) = left, right
    one = lambda u, v: lax.dot_general(u, v, dims, preferred_element_type=jnp.float32)
    return one(a, d) + one(b, c) + one(a, c)


def kernel_products(
    place, own, other, first, second, third, fourth, coefficients, basis, sums, stacked
):
    chips, groups, depth, rows, width = own.shape
    blocks, lines, lanes = sums.shape
    classes, count = coefficients.shape
    split = basis.shape[2]
    padded = lines - blocks * split
    near = depth // blocks
    centers = (first, second, third, fourth)[:groups]
    is_low = place[2] == 0

    center_norm = jnp.zeros((1, count), jnp.float32)
    for piece in centers:
        wide = piece[...].astype(jnp.float32)
        center_norm += jnp.sum(wide * wide, axis=0, keepdims=True)
    stacked[padded - 8 : padded, :] = jnp.zeros((8, count), jnp.float32)
    stacked[:classes, :] = coefficients[...]
    stacked[padded:, :] = basis[:, pl.ds(place[0], 1)].reshape(-1, count)
    weights = in_two(stacked[...])

    for t in range(0, blocks, 2):
        inner = jnp.zeros((2 * lanes, count), jnp.float32)
        batch_norm = jnp.zeros((2 * lanes, 1), jnp.float32)
        for s in range(groups):
            y = lax.rem(place[0] + s, groups)
            pieces = []
            for z in range(t * near, (t + 2) * near):
                for x in range(chips):
                    a, b = own[x, y, z], other[x, y, z]
                    pieces += [jnp.where(is_low, a, b), jnp.where(is_low, b, a)]
            block = jnp.concatenate(pieces, axis=0)
            inner += jnp.dot(block, centers[s][...], preferred_element_type=jnp.float32)
            wide = block.astype(jnp.float32)
            batch_norm += jnp.sum(wide * wide, axis=1, keepdims=True)
        squared = center_norm + batch_norm - 2.0 * inner
        values = jnp.exp(-jnp.sqrt(jnp.maximum(squared, 0.0)) / spread)
        out = product(weights, in_two(values), LAST)
        for j in range(2):
            part = out[:, j * lanes : (j + 1) * lanes]
            sums[t + j, :padded, :] = part[:padded]
            at = padded + (t + j) * split
            sums[:, at : at + split, :] = part[padded:].reshape(blocks, split, lanes)


def gradient_of(place, predicted, labels, j, classes):
    cores, chips, rows, lanes = predicted.shape
    ids = lax.broadcasted_iota(jnp.int32, (rows, lanes), 0) + place[0] * classes
    return predicted[j // chips, j % chips] - (labels[j] == ids).astype(jnp.float32)


def project(place, predicted, first, second, third, fourth, labels, projected, *, classes):
    blocks, split, lanes = first.shape
    groups = projected.shape[1] // split
    pieces = (first, second, third, fourth)[:groups]
    total = jnp.zeros(projected.shape[1:], jnp.float32)
    for t in range(0, blocks, 2):
        pair = (t, t + 1)
        lines = [jnp.concatenate([p[j] for j in pair], axis=1) for p in pieces]
        gradient = [gradient_of(place, predicted, labels, j, classes) for j in pair]
        total += product(
            in_two(jnp.concatenate(lines, axis=0)),
            in_two(jnp.concatenate(gradient, axis=1)),
            LAST,
        )
    for s in range(groups):
        at = pl.multiple_of(lax.rem(place[0] + s, groups) * split, split)
        part = total[s * split : (s + 1) * split]
        projected[:, pl.ds(at, split), :] = jnp.broadcast_to(
            part[None], (projected.shape[0], *part.shape)
        )


def step_batch(place, predicted, labels, index, coefficients, output, updated):
    cores, chips, rows, lanes = predicted.shape
    classes, count = coefficients.shape
    total = jnp.zeros((rows, count), jnp.float32)
    slots = lax.broadcasted_iota(jnp.int32, (count, lanes), 0) + place[1] * count
    for t in range(0, cores * chips, 2):
        pair = (t, t + 1)
        gradient = [gradient_of(place, predicted, labels, j, classes) for j in pair]
        hits = [(index[j] == slots).astype(jnp.float32) for j in pair]
        spots = jnp.concatenate(hits, axis=1).astype(jnp.bfloat16)
        for part in in_two(jnp.concatenate(gradient, axis=1)):
            total += lax.dot_general(part, spots, LAST, preferred_element_type=jnp.float32)
        for j in pair:
            output[:, j * lanes : (j + 1) * lanes] = predicted[j // chips, j % chips, :classes]
    updated[...] = coefficients[...] - step_rate * total[:classes]


def correct(updated, projected, weights, result):
    classes = updated.shape[0]
    change = product(in_two(projected[...]), in_two(weights[...]), FIRST)
    result[...] = updated[...] + change[:classes]


def kernel(body, outs, name, scratch=(), **settings):
    near = pl.BlockSpec(memory_space=pltpu.VMEM)

    def call(*operands):
        return pl.pallas_call(
            functools.partial(body, **settings),
            out_shape=outs,
            in_specs=[
                pl.BlockSpec(memory_space=pltpu.SMEM) if o.size < 8 else near for o in operands
            ],
            out_specs=jax.tree.map(lambda _: near, outs),
            scratch_shapes=scratch,
            compiler_params=pltpu.CompilerParams(vmem_limit_bytes=24 * 2**20),
            interpret=INTERPRET,
            name=name,
        )(*operands)

    return call


def from_others(value, axis):
    size = lax.axis_size(axis)
    pieces = [value]
    for s in range(1, size):
        pieces.append(lax.ppermute(value, axis, [((d + s) % size, d) for d in range(size)]))
    return pieces + [value] * (4 - size)


def shards(
    centers,
    coefficients,
    batch_features,
    batch_labels,
    batch_index,
    subset_index,
    eigen_vectors,
    eigen_scale,
):
    depth, chips, cores, groups = (lax.axis_size(a) for a in (Z, X, K, Y))
    blocks = chips * cores
    count = centers.shape[0]
    classes = coefficients.shape[0]
    rank = lax.axis_index(ROWS)
    place = jnp.stack([lax.axis_index(Y), rank, lax.axis_index(K)]).astype(jnp.int32)
    vectors = eigen_vectors.shape[1]
    split = vectors // groups // blocks
    padded = -(-classes // 8) * 8
    while (padded + vectors // groups) % (8 * depth):
        padded += 8
    lines = padded + vectors // groups
    batch = blocks * LANES
    array = lambda *shape: jax.ShapeDtypeStruct(shape, jnp.float32)

    with jax.named_scope("centers_gather"):
        center_pieces = from_others(centers.T, Y)
    batch_own = batch_features
    for axis in (Z, Y, X):
        with jax.named_scope("batch_" + axis):
            batch_own = gathered(batch_own, axis)
        if axis == Z:
            batch_own, center_pieces = lax.optimization_barrier((batch_own, center_pieces))
    batch_other = from_others(batch_own, K)[1]

    spots = jnp.arange(count, dtype=jnp.int32) + rank * count
    chosen = (subset_index[:, None] == spots[None, :]).astype(jnp.float32)
    lifted = lax.dot_general(eigen_vectors, chosen, FIRST, precision=HIGHEST)
    weights = lifted * (step_rate * eigen_scale)[:, None]
    labels = batch_labels.reshape(blocks, 1, LANES)
    index = batch_index.reshape(blocks, 1, LANES)

    sums = kernel(
        kernel_products,
        array(blocks, lines, LANES),
        "kernel_products",
        (pltpu.VMEM((lines, count), jnp.float32),),
    )(
        place,
        batch_own,
        batch_other,
        *center_pieces,
        coefficients,
        lifted.reshape(blocks, groups, split, count),
    )

    own = scattered(sums.reshape(cores, chips, lines, LANES), K)
    own = scattered(own, X)
    own = scattered(own.reshape(depth, lines // depth, LANES), Z)
    own = gathered(own, Z).reshape(lines, LANES)
    with jax.named_scope("basis_gather"):
        basis = from_others(own[padded:].reshape(blocks, split, LANES), Y)
    predicted = gathered(gathered(own[:padded], X), K)

    copies = kernel(
        project, array(blocks, groups * split, padded), "project", classes=classes
    )(place, predicted, *basis, labels)
    with jax.named_scope("projected_gather"):
        projected = lax.all_to_all(
            copies, (X, K), 0, 0, tiled=True
        )
    projected = projected.reshape(chips, cores, -1, padded).swapaxes(0, 1)
    projected = projected.reshape(vectors, padded)

    output, updated = kernel(
        step_batch, (array(classes, batch), array(classes, count)), "step_batch"
    )(place, predicted, labels, index, coefficients)
    result = kernel(correct, array(classes, count), "correct")(updated, projected, weights)
    return (output, result)


def solution(mesh, shape=(16, 4, 2)):
    finer = Mesh(mesh.devices.reshape(*shape, mesh.shape["cls"]), (*ROWS, Y))
    placed = (P(ROWS, Y), P(Y, ROWS), P(ROWS, Y), P(), P(), P(ROWS), P(ROWS, None), P())
    return jax.shard_map(
        shards,
        mesh=finer,
        in_specs=placed,
        out_specs=(P(Y, None), P(Y, ROWS)),
        check_vma=False,
    )
```

time: 342 us -> 186 us (0.54)
  blocking collectives: 192 us -> 95 us
  waiting for transfers between devices: 72.8 us -> 15.1 us
  starting transfers between devices: 12.5 us -> 59 us
  local copies, waits for them, and re-layouts: 38.5 us -> 3.59 us
  other arithmetic: 14.2 us -> 0.32 us
  Pallas kernels: 0 us -> 10.9 us
  matrix products: 10.2 us -> 0.44 us
    all_to_all x2 -> x4, waiting for transfers between devices: 72.8 us -> 9.02 us  [the longest x1 7.29 us: shards(): projected = lax.all_to_all(copies, (X, K), 0, 0, tiled=True)]
    all_to_all x5 -> x6, blocking collectives: 154 us -> 95 us  [the longest x3 52.4 us: gathered(): return lax.all_to_all(copies, axis, 0, 0, tiled=True)]
    all_gather x1 -> x0, blocking collectives: 37.9 us -> none  [rows_first(): filled, at, done = (lax.all_gather(both, axis, axis=0, tiled=True), 0, [])]
    ppermute x0 -> x7, starting transfers between devices: none -> 25.3 us  [from_others(): lax.ppermute(value, axis, [((d + s) % size, d) for d in range(size)])]
    all_to_all x2 -> x4, starting transfers between devices: 12.5 us -> 33.7 us  [the longest x3 28.6 us: gathered(): return lax.all_to_all(copies, axis, 0, 0, tiled=True)]
    pallas_call x0 -> x4, Pallas kernels: none -> 10.9 us  [call(): pl.pallas_call(functools.partial(body, **settings), out_shape=outs, in_sp...]
    dot_general x6 -> x1, matrix products: 10.2 us -> 0.44 us  [shards(): lifted = lax.dot_general(eigen_vectors, chosen, FIRST, precision=HIGHEST)]
    scatter-add x2 -> x0, other arithmetic: 7.54 us -> none  [the longest x1 6.48 us: shards(): coefficients.at[:, batch_slot].add(-step_rate * gradient, mode='drop')]
  transfers between devices with their start and end apart: 2 -> 11, of which waited for: 1 -> 5; matrix products, arithmetic and copies ran while one was open for 0% -> 1% of each run, Pallas kernels for 0% -> 1%
where the time goes in v2:
time: 186 us; the launch traced here: 185 us
  blocking collectives  95 us (51%)
  starting transfers between devices  59 us (32%)
  waiting for transfers between devices  15.1 us (8%)
  Pallas kernels  10.9 us (6%)
  local copies, waits for them, and re-layouts  3.59 us (2%)
    all_to_all x3, blocking collectives, gathered(): return lax.all_to_all(copies, axis, 0, 0, tiled=True)  52.4 us
    all_to_all x3, blocking collectives, scattered(): return jnp.sum(lax.all_to_all(tiles, axis, 0, 0, tiled=True), axis=0)  42.6 us
    all_to_all x3, starting transfers between devices, gathered(): return lax.all_to_all(copies, axis, 0, 0, tiled=True)  28.6 us
    ppermute x7, starting transfers between devices, from_others(): lax.ppermute(value, axis, [((d + s) % size, d) for d in range(size)])  25.3 us
    pallas_call x4, Pallas kernels, call(): pl.pallas_call(functools.partial(body, **settings), out_shape=outs, in_sp...  10.9 us
    all_to_all x1, waiting for transfers between devices, shards(): projected = lax.all_to_all(copies, (X, K), 0, 0, tiled=True)  7.29 us
    ppermute x7, waiting for transfers between devices, from_others(): lax.ppermute(value, axis, [((d + s) % size, d) for d in range(size)])  6.12 us
    all_to_all x1, starting transfers between devices, shards(): projected = lax.all_to_all(copies, (X, K), 0, 0, tiled=True)  5.12 us
  transfers between devices with their start and end apart: 11, of which 5 were waited for; matrix products, arithmetic and copies ran while one was open for 1% of the time, Pallas kernels for 1%

profile of v2, /device:TPU:1, one launch (start us, length us, event | category | flops | bytes accessed | tf_op | source)
XLA Modules:
  0.0 185.4 jit_solution(9199337266035651313)
XLA Ops:
  0.6 0.0 copy-start
  0.6 1.4 broadcast_in_dim.21
  2.0 15.7 %all-to-all-start = ((bf16[16,8,320]{2,1,0:T(8,128)(2,1)}), bf16[16,8,320]{2,1,0:T(8,128)(2,1)S(1)}, u32[]{:S(2)}, u32[]{:S(2)}) async-start(bf16[16,8,320]{2,1,0:T(8,128)(2,1)} %broadcast_in_dim.21), calls=%async_computation | async-start | bytes 196608 | tf_op jit(solution)/shard_map/batch_rows_z/all_to_all | solution.py:26
  17.8 3.2 %collective-permute-start.2 = (bf16[320,256]{1,0:T(8,128)(2,1)}, bf16[320,256]{1,0:T(8,128)(2,1)S(1)}, u32[]{:S(2)}, u32[]{:S(2)}) collective-permute-start(bf16[320,256]{1,0:T(8,128)(2,1)} %bitcast.26), channel_id=1, source_target_pairs={{3,0},{0,1},{1,2},{2,3},{7,4},{4,5},{5,6},{6,7},{11,8},{8,9},{9,10... | collective-permute-start | bytes 491528 | tf_op jit(solution)/shard_map/centers_gather/ppermute | solution.py:165
  21.0 4.5 %collective-permute-start.1 = (bf16[320,256]{1,0:T(8,128)(2,1)}, bf16[320,256]{1,0:T(8,128)(2,1)S(1)}, u32[]{:S(2)}, u32[]{:S(2)}) collective-permute-start(bf16[320,256]{1,0:T(8,128)(2,1)} %bitcast.27), channel_id=1, source_target_pairs={{2,0},{3,1},{0,2},{1,3},{6,4},{7,5},{4,6},{5,7},{10,8},{11,9},{8,1... | collective-permute-start | bytes 491528 | tf_op jit(solution)/shard_map/centers_gather/ppermute | solution.py:165
  25.5 3.0 %collective-permute-start = (bf16[320,256]{1,0:T(8,128)(2,1)}, bf16[320,256]{1,0:T(8,128)(2,1)S(1)}, u32[]{:S(2)}, u32[]{:S(2)}) collective-permute-start(bf16[320,256]{1,0:T(8,128)(2,1)} %bitcast.28), channel_id=1, source_target_pairs={{1,0},{2,1},{3,2},{0,3},{5,4},{6,5},{7,6},{4,7},{9,8},{10,9},{11,1... | collective-permute-start | bytes 491528 | tf_op jit(solution)/shard_map/centers_gather/ppermute | solution.py:165
  28.5 0.0 collective-permute-done.2.fourth
  28.5 2.3 %collective-permute-done.1.third = bf16[320,256]{1,0:T(8,128)(2,1)S(1)} collective-permute-done((bf16[320,256]{1,0:T(8,128)(2,1)}, bf16[320,256]{1,0:T(8,128)(2,1)S(1)}, u32[]{:S(2)}, u32[]{:S(2)}) %collective-permute-start.1) | collective-permute-done | bytes 163872 | tf_op jit(solution)/shard_map/centers_gather/ppermute | solution.py:165
  30.8 1.2 collective-permute-done.second
  32.1 0.0 all-to-all-done
  32.1 10.3 %all_to_all.50 = bf16[4,16,8,320]{3,2,1,0:T(8,128)(2,1)S(1)} all-to-all(bf16[4,16,8,320]{3,2,1,0:T(8,128)(2,1)S(1)} %broadcast_in_dim.22), channel_id=1, replica_groups=mesh['rows_z'=16,'rows_x'=4,'rows_k'=2,'cls'=4] {'cls'}, dimensions={0} | all-to-all | bytes 655360 | tf_op jit(solution)/shard_map/batch_cls/all_to_all | solution.py:26
  42.4 0.2 broadcast_in_dim.23
  42.6 0.0 copy-start.5
  42.6 0.0 copy-start.6
  42.6 0.0 copy-start.1
  42.6 0.0 copy-start.2
  42.6 21.4 %all_to_all.51.own = bf16[4,4,16,8,320]{4,3,2,1,0:T(8,128)(2,1)S(1)} all-to-all(bf16[4,4,16,8,320]{4,3,2,1,0:T(8,128)(2,1)S(1)} %broadcast_in_dim.23), channel_id=1, replica_groups=mesh['rows_z'=16,'rows_x'=4,'rows_k'=2,'cls'=4] {'rows_x'}, dimensions={0} | all-to-all | bytes 2621440 | tf_op jit(solution)/shard_map/batch_rows_x/all_to_all | solution.py:26
  64.0 6.1 %collective-permute-start.3 = (bf16[4,4,16,8,320]{4,3,2,1,0:T(8,128)(2,1)S(1)}, bf16[4,4,16,8,320]{4,3,2,1,0:T(8,128)(2,1)}, u32[]{:S(2)}, u32[]{:S(2)}) collective-permute-start(bf16[4,4,16,8,320]{4,3,2,1,0:T(8,128)(2,1)S(1)} %all_to_all.51.own), channel_id=1, source_target_pairs={{4,0},{0,4},{5,1},{1,5},{6,2},{2,6},{7,3},{3,7},{12,8},{8,12},{13,... | collective-permute-start | bytes 3932168 | tf_op jit(solution)/shard_map/ppermute | solution.py:165
  70.2 0.1 pad_add_fusion.place
  70.3 0.0 copy-done.5
  70.3 0.4 bitcast_multiply_fusion
  70.7 2.6 %collective-permute-done.3.other = bf16[4,4,16,8,320]{4,3,2,1,0:T(8,128)(2,1)} collective-permute-done((bf16[4,4,16,8,320]{4,3,2,1,0:T(8,128)(2,1)S(1)}, bf16[4,4,16,8,320]{4,3,2,1,0:T(8,128)(2,1)}, u32[]{:S(2)}, u32[]{:S(2)}) %collective-permute-start.3) | collective-permute-done | bytes 1310752 | tf_op jit(solution)/shard_map/ppermute | solution.py:165
  73.3 5.8 %kernel_products.1 = f32[8,384,128]{2,1,0:T(8,128)S(1)} custom-call(s32[3]{0:T(128)S(1)} %pad_add_fusion.place, bf16[4,4,16,8,320]{4,3,2,1,0:T(8,128)(2,1)S(1)} %all_to_all.51.own, bf16[4,4,16,8,320]{4,3,2,1,0:T(8,128)(2,1)} %collective-permute-done.3.other, bf16[320,256]{1,0:T(8,128)(2,1)S(1)} %bitcast.29, ...), custom_call_target="tpu_custom_call" | custom-call | tf_op jit(solution)/shard_map/kernel_products/pallas_call | solution.py:145
  79.1 5.0 %all_to_all.52 = f32[2,4,384,128]{3,2,1,0:T(8,128)S(1)} all-to-all(f32[2,4,384,128]{3,2,1,0:T(8,128)S(1)} %bitcast.19), channel_id=1, replica_groups=mesh['rows_z'=16,'rows_x'=4,'rows_k'=2,'cls'=4] {'rows_k'}, dimensions={0} | all-to-all | bytes 3145728 | tf_op jit(solution)/shard_map/all_to_all | solution.py:30
  84.1 0.2 reduce_sum.27
  84.3 14.4 %all_to_all.53 = f32[4,384,128]{2,1,0:T(8,128)S(1)} all-to-all(f32[4,384,128]{2,1,0:T(8,128)S(1)} %reduce_sum.27), channel_id=1, replica_groups=mesh['rows_z'=16,'rows_x'=4,'rows_k'=2,'cls'=4] {'rows_x'}, dimensions={0} | all-to-all | bytes 1572864 | tf_op jit(solution)/shard_map/all_to_all | solution.py:30
  98.7 23.2 %all_to_all.54 = f32[16,24,128]{2,1,0:T(8,128)S(1)} all-to-all(f32[16,24,128]{2,1,0:T(8,128)S(1)} %bitcast.34), channel_id=1, replica_groups=mesh['rows_z'=16,'rows_x'=4,'rows_k'=2,'cls'=4] {'rows_z'}, dimensions={0} | all-to-all | bytes 393216 | tf_op jit(solution)/shard_map/all_to_all | solution.py:30
  122.0 20.7 %all_to_all.55 = f32[16,24,128]{2,1,0:T(8,128)S(1)} all-to-all(f32[16,24,128]{2,1,0:T(8,128)S(1)} %broadcast_in_dim.24), channel_id=1, replica_groups=mesh['rows_z'=16,'rows_x'=4,'rows_k'=2,'cls'=4] {'rows_z'}, dimensions={0} | all-to-all | bytes 393216 | tf_op jit(solution)/shard_map/all_to_all | solution.py:26
  142.8 0.8 broadcast_in_dim.25
  143.6 3.5 %all-to-all-start.7 = ((f32[4,256,128]{2,1,0:T(8,128)}), f32[4,256,128]{2,1,0:T(8,128)S(1)}, u32[]{:S(2)}, u32[]{:S(2)}) async-start(f32[4,256,128]{2,1,0:T(8,128)} %broadcast_in_dim.25), calls=%async_computation.7 | async-start | bytes 1048576 | tf_op jit(solution)/shard_map/all_to_all | solution.py:26
  147.1 0.0 copy-start.3
  147.1 2.2 %collective-permute-start.6 = (f32[8,16,128]{2,1,0:T(8,128)S(1)}, f32[8,16,128]{2,1,0:T(8,128)S(1)}, u32[]{:S(2)}, u32[]{:S(2)}) collective-permute-start(f32[8,16,128]{2,1,0:T(8,128)S(1)} %bitcast.22), channel_id=1, source_target_pairs={{3,0},{0,1},{1,2},{2,3},{7,4},{4,5},{5,6},{6,7},{11,8},{8,9},{9,10... | collective-permute-start | bytes 196616 | tf_op jit(solution)/shard_map/basis_gather/ppermute | solution.py:165
  149.3 3.8 %collective-permute-start.5 = (f32[8,16,128]{2,1,0:T(8,128)S(1)}, f32[8,16,128]{2,1,0:T(8,128)S(1)}, u32[]{:S(2)}, u32[]{:S(2)}) collective-permute-start(f32[8,16,128]{2,1,0:T(8,128)S(1)} %bitcast.23), channel_id=1, source_target_pairs={{2,0},{3,1},{0,2},{1,3},{6,4},{7,5},{4,6},{5,7},{10,8},{11,9},{8,1... | collective-permute-start | bytes 196616 | tf_op jit(solution)/shard_map/basis_gather/ppermute | solution.py:165
  153.1 2.4 %collective-permute-start.4 = (f32[8,16,128]{2,1,0:T(8,128)S(1)}, f32[8,16,128]{2,1,0:T(8,128)S(1)}, u32[]{:S(2)}, u32[]{:S(2)}) collective-permute-start(f32[8,16,128]{2,1,0:T(8,128)S(1)} %bitcast.24), channel_id=1, source_target_pairs={{1,0},{2,1},{3,2},{0,3},{5,4},{6,5},{7,6},{4,7},{9,8},{10,9},{11,1... | collective-permute-start | bytes 196616 | tf_op jit(solution)/shard_map/basis_gather/ppermute | solution.py:165
  155.5 0.0 all-to-all-done.7
  155.6 1.0 broadcast_in_dim.26
  156.6 9.4 %all-to-all-start.8 = ((f32[2,4,256,128]{3,2,1,0:T(8,128)}), f32[2,4,256,128]{3,2,1,0:T(8,128)S(1)}, u32[]{:S(2)}, u32[]{:S(2)}) async-start(f32[2,4,256,128]{3,2,1,0:T(8,128)} %broadcast_in_dim.26), calls=%async_computation.8 | async-start | bytes 2097152 | tf_op jit(solution)/shard_map/all_to_all | solution.py:26
  166.0 0.0 collective-permute-done.6.fourth
  166.0 0.0 collective-permute-done.5.third
  166.0 0.0 collective-permute-done.4.second
  166.0 1.7 all-to-all-done.8.predicted
  167.8 0.0 copy-done.3
  167.8 2.0 %project.1 = f32[8,64,256]{2,1,0:T(8,128)} custom-call(s32[3]{0:T(128)S(1)} %pad_add_fusion.place, f32[2,4,256,128]{3,2,1,0:T(8,128)S(1)} %all-to-all-done.8.predicted, f32[8,16,128]{2,1,0:T(8,128)S(1)} %bitcast.25, f32[8,16,128]{2,1,0:T(8,128)S(1)} %collective-permute-done.4.second, f32[8,16,128]{2,1,0:T(8,128)S(1)} %collective-permute-done.5.third, ...), custom_call_target="tpu_custom_call" | custom-call | tf_op jit(solution)/shard_map/project/pallas_call | solution.py:145
  169.7 5.1 %all-to-all-start.9 = ((f32[8,64,256]{2,1,0:T(8,128)}), f32[8,64,256]{2,1,0:T(8,128)S(1)}, u32[]{:S(2)}, u32[]{:S(2)}) async-start(f32[8,64,256]{2,1,0:T(8,128)} %project.1), calls=%async_computation.9 | async-start | bytes 1048576 | tf_op jit(solution)/shard_map/projected_gather/all_to_all | solution.py:237
  174.9 0.0 copy-done.4
  174.9 2.1 %step_batch.1 = (f32[250,1024]{1,0:T(8,128)}, f32[250,256]{1,0:T(8,128)S(1)}) custom-call(s32[3]{0:T(128)S(1)} %pad_add_fusion.place, f32[2,4,256,128]{3,2,1,0:T(8,128)S(1)} %all-to-all-done.8.predicted, s32[8,1,128]{2,1,0:T(1,128)S(1)} %bitcast.31, s32[8,1,128]{2,1,0:T(1,128)S(1)} %bitcast.32, f32[250,256]{1,0:T(8,128)S(1)} %copy-done.1), custom_call_target="tpu_custom_call" | custom-call | tf_op jit(solution)/shard_map/step_batch/pallas_call | solution.py:145
  176.9 7.3 %all-to-all-done.9 = f32[8,64,256]{2,1,0:T(8,128)S(1)} async-done(((f32[8,64,256]{2,1,0:T(8,128)}), f32[8,64,256]{2,1,0:T(8,128)S(1)}, u32[]{:S(2)}, u32[]{:S(2)}) %all-to-all-start.9) | async-done | bytes 524320 | tf_op jit(solution)/shard_map/projected_gather/all_to_all | solution.py:237
  184.2 1.1 correct.1
  (14 shorter events, 0.2 us)
Async XLA Ops:
  0.6 69.6 %copy-start = (f32[64,512]{1,0:T(8,128)S(1)}, f32[64,512]{1,0:T(8,128)}, u32[]{:S(2)}) copy-start(f32[64,512]{1,0:T(8,128)} %param.14) | copy-start | bytes 393220
  2.0 30.0 %all-to-all-start = ((bf16[16,8,320]{2,1,0:T(8,128)(2,1)}), bf16[16,8,320]{2,1,0:T(8,128)(2,1)S(1)}, u32[]{:S(2)}, u32[]{:S(2)}) async-start(bf16[16,8,320]{2,1,0:T(8,128)(2,1)} %broadcast_in_dim.21), calls=%async_computation | async-start | bytes 196608 | tf_op jit(solution)/shard_map/batch_rows_z/all_to_all | solution.py:26
  17.8 10.7 %collective-permute-start.2 = (bf16[320,256]{1,0:T(8,128)(2,1)}, bf16[320,256]{1,0:T(8,128)(2,1)S(1)}, u32[]{:S(2)}, u32[]{:S(2)}) collective-permute-start(bf16[320,256]{1,0:T(8,128)(2,1)} %bitcast.26), channel_id=1, source_target_pairs={{3,0},{0,1},{1,2},{2,3},{7,4},{4,5},{5,6},{6,7},{11,8},{8,9},{9,10... | collective-permute-start | bytes 491528 | tf_op jit(solution)/shard_map/centers_gather/ppermute | solution.py:165
  21.0 9.8 %collective-permute-start.1 = (bf16[320,256]{1,0:T(8,128)(2,1)}, bf16[320,256]{1,0:T(8,128)(2,1)S(1)}, u32[]{:S(2)}, u32[]{:S(2)}) collective-permute-start(bf16[320,256]{1,0:T(8,128)(2,1)} %bitcast.27), channel_id=1, source_target_pairs={{2,0},{3,1},{0,2},{1,3},{6,4},{7,5},{4,6},{5,7},{10,8},{11,9},{8,1... | collective-permute-start | bytes 491528 | tf_op jit(solution)/shard_map/centers_gather/ppermute | solution.py:165
  25.5 6.5 %collective-permute-start = (bf16[320,256]{1,0:T(8,128)(2,1)}, bf16[320,256]{1,0:T(8,128)(2,1)S(1)}, u32[]{:S(2)}, u32[]{:S(2)}) collective-permute-start(bf16[320,256]{1,0:T(8,128)(2,1)} %bitcast.28), channel_id=1, source_target_pairs={{1,0},{2,1},{3,2},{0,3},{5,4},{6,5},{7,6},{4,7},{9,8},{10,9},{11,1... | collective-permute-start | bytes 491528 | tf_op jit(solution)/shard_map/centers_gather/ppermute | solution.py:165
  42.6 27.7 %copy-start.5 = (f32[512]{0:T(512)S(1)}, f32[512]{0:T(512)}, u32[]{:S(2)}) copy-start(f32[512]{0:T(512)} %param.15) | copy-start | bytes 6148
  42.6 27.7 %copy-start.6 = (s32[64]{0:T(128)S(1)}, s32[64]{0:T(128)}, u32[]{:S(2)}) copy-start(s32[64]{0:T(128)} %param.13) | copy-start | bytes 772
  42.6 30.7 %copy-start.1 = (f32[250,256]{1,0:T(8,128)S(1)}, f32[250,256]{1,0:T(8,128)}, u32[]{:S(2)}) copy-start(f32[250,256]{1,0:T(8,128)} %coefficients.3) | copy-start | bytes 768004
  42.6 30.7 %copy-start.2 = (bf16[256,320]{0,1:T(8,128)(2,1)S(1)}, bf16[256,320]{0,1:T(8,128)(2,1)}, u32[]{:S(2)}) copy-start(bf16[256,320]{0,1:T(8,128)(2,1)} %param.8) | copy-start | bytes 491524
  64.0 9.3 %collective-permute-start.3 = (bf16[4,4,16,8,320]{4,3,2,1,0:T(8,128)(2,1)S(1)}, bf16[4,4,16,8,320]{4,3,2,1,0:T(8,128)(2,1)}, u32[]{:S(2)}, u32[]{:S(2)}) collective-permute-start(bf16[4,4,16,8,320]{4,3,2,1,0:T(8,128)(2,1)S(1)} %all_to_all.51.own), channel_id=1, source_target_pairs={{4,0},{0,4},{5,1},{1,5},{6,2},{2,6},{7,3},{3,7},{12,8},{8,12},{13,... | collective-permute-start | bytes 3932168 | tf_op jit(solution)/shard_map/ppermute | solution.py:165
  143.6 11.9 %all-to-all-start.7 = ((f32[4,256,128]{2,1,0:T(8,128)}), f32[4,256,128]{2,1,0:T(8,128)S(1)}, u32[]{:S(2)}, u32[]{:S(2)}) async-start(f32[4,256,128]{2,1,0:T(8,128)} %broadcast_in_dim.25), calls=%async_computation.7 | async-start | bytes 1048576 | tf_op jit(solution)/shard_map/all_to_all | solution.py:26
  147.1 20.7 %copy-start.3 = (s32[1024]{0:T(1024)S(1)}, s32[1024]{0:T(1024)}, u32[]{:S(2)}) copy-start(s32[1024]{0:T(1024)} %param.11) | copy-start | bytes 12292
  147.1 18.9 %collective-permute-start.6 = (f32[8,16,128]{2,1,0:T(8,128)S(1)}, f32[8,16,128]{2,1,0:T(8,128)S(1)}, u32[]{:S(2)}, u32[]{:S(2)}) collective-permute-start(f32[8,16,128]{2,1,0:T(8,128)S(1)} %bitcast.22), channel_id=1, source_target_pairs={{3,0},{0,1},{1,2},{2,3},{7,4},{4,5},{5,6},{6,7},{11,8},{8,9},{9,10... | collective-permute-start | bytes 196616 | tf_op jit(solution)/shard_map/basis_gather/ppermute | solution.py:165
  149.3 16.7 %collective-permute-start.5 = (f32[8,16,128]{2,1,0:T(8,128)S(1)}, f32[8,16,128]{2,1,0:T(8,128)S(1)}, u32[]{:S(2)}, u32[]{:S(2)}) collective-permute-start(f32[8,16,128]{2,1,0:T(8,128)S(1)} %bitcast.23), channel_id=1, source_target_pairs={{2,0},{3,1},{0,2},{1,3},{6,4},{7,5},{4,6},{5,7},{10,8},{11,9},{8,1... | collective-permute-start | bytes 196616 | tf_op jit(solution)/shard_map/basis_gather/ppermute | solution.py:165
  153.1 12.9 %collective-permute-start.4 = (f32[8,16,128]{2,1,0:T(8,128)S(1)}, f32[8,16,128]{2,1,0:T(8,128)S(1)}, u32[]{:S(2)}, u32[]{:S(2)}) collective-permute-start(f32[8,16,128]{2,1,0:T(8,128)S(1)} %bitcast.24), channel_id=1, source_target_pairs={{1,0},{2,1},{3,2},{0,3},{5,4},{6,5},{7,6},{4,7},{9,8},{10,9},{11,1... | collective-permute-start | bytes 196616 | tf_op jit(solution)/shard_map/basis_gather/ppermute | solution.py:165
  156.6 11.2 %all-to-all-start.8 = ((f32[2,4,256,128]{3,2,1,0:T(8,128)}), f32[2,4,256,128]{3,2,1,0:T(8,128)S(1)}, u32[]{:S(2)}, u32[]{:S(2)}) async-start(f32[2,4,256,128]{3,2,1,0:T(8,128)} %broadcast_in_dim.26), calls=%async_computation.8 | async-start | bytes 2097152 | tf_op jit(solution)/shard_map/all_to_all | solution.py:26
  166.0 8.8 %copy-start.4 = (s32[1024]{0:T(1024)S(1)}, s32[1024]{0:T(1024)}, u32[]{:S(2)}) copy-start(s32[1024]{0:T(1024)} %param.12) | copy-start | bytes 12292
  169.7 14.5 %all-to-all-start.9 = ((f32[8,64,256]{2,1,0:T(8,128)}), f32[8,64,256]{2,1,0:T(8,128)S(1)}, u32[]{:S(2)}, u32[]{:S(2)}) async-start(f32[8,64,256]{2,1,0:T(8,128)} %project.1), calls=%async_computation.9 | async-start | bytes 1048576 | tf_op jit(solution)/shard_map/projected_gather/all_to_all | solution.py:237

commit v3 on v2

v3 whole, which is shorter than its diff:
```python
import functools

import jax
import jax.numpy as jnp
from jax import lax
from jax.experimental import pallas as pl
from jax.experimental.pallas import tpu as pltpu
from jax.sharding import Mesh
from jax.sharding import PartitionSpec as P

Z, X, K, Y = "rows_z", "rows_x", "rows_k", "cls"
ROWS = (Z, X, K)
LANES = 128
INTERPRET = False

spread = 4.0
step_rate = 0.5

HIGHEST = lax.Precision.HIGHEST
LAST = (((1,), (1,)), ((), ()))
FIRST = (((0,), (0,)), ((), ()))


def gathered(value, axis):
    copies = jnp.broadcast_to(value, (lax.axis_size(axis), *value.shape))
    return lax.all_to_all(copies, axis, 0, 0, tiled=True)


def scattered(tiles, axis):
    return jnp.sum(lax.all_to_all(tiles, axis, 0, 0, tiled=True), axis=0)


def in_two(value):
    high = value.astype(jnp.bfloat16)
    low = (value - high.astype(jnp.float32)).astype(jnp.bfloat16)
    return high, low


def product(left, right, dims):
    (a, b), (c, d) = left, right
    one = lambda u, v: lax.dot_general(u, v, dims, preferred_element_type=jnp.float32)
    return one(a, d) + one(b, c) + one(a, c)


def pack(batch, copies, granules):
    depth, rows, width = batch.shape
    full, rest = width // LANES, width % LANES
    half = depth // 2
    for z in range(depth):
        for h in range(full):
            granules[z * full + h] = batch[z, :, h * LANES : (h + 1) * LANES]
    for z in range(half):
        at = depth * full + z
        granules[at, :, :rest] = batch[z, :, full * LANES :]
        granules[at, :, rest:] = batch[z + half, :, full * LANES :]
    copies[...] = jnp.broadcast_to(granules[...][None], copies.shape)


def kernel_products(
    own, other, first, second, third, fourth, coefficients, basis, sums, stacked
):
    chips, groups, granules, rows, lanes = own.shape
    blocks, lines, _ = sums.shape
    classes, count = coefficients.shape
    full, rest = first.shape[0] // lanes, first.shape[0] % lanes
    depth = 2 * granules // (2 * full + 1)
    half = depth // 2
    split = basis.shape[2]
    padded = lines - blocks * split
    near = depth // blocks
    centers = (first, second, third, fourth)[:groups]
    is_low = lax.axis_index(K) == 0

    center_norm = jnp.zeros((1, count), jnp.float32)
    tails = []
    for piece in centers:
        wide = piece[...].astype(jnp.float32)
        center_norm += jnp.sum(wide * wide, axis=0, keepdims=True)
        tails.append(piece[full * lanes :])
    none = jnp.zeros((rest, count), tails[0].dtype)
    low_tail = jnp.concatenate([v for t in tails for v in (t, none)], axis=0)
    high_tail = jnp.concatenate([v for t in tails for v in (none, t)], axis=0)
    stacked[padded - 8 : padded, :] = jnp.zeros((8, count), jnp.float32)
    stacked[:classes, :] = coefficients[...]
    stacked[padded:, :] = basis[:, pl.ds(lax.axis_index(Y), 1)].reshape(-1, count)
    weights = in_two(stacked[...])
    lane = lax.broadcasted_iota(jnp.int32, (2 * lanes, lanes), 1)

    for t in range(0, blocks, 2):
        inner = jnp.zeros((2 * lanes, count), jnp.float32)
        batch_norm = jnp.zeros((2 * lanes, 1), jnp.float32)
        is_high = t * near >= half
        is_own = (lane >= rest) if is_high else (lane < rest)
        ends = []
        for s in range(groups):
            y = lax.rem(lax.axis_index(Y) + s, groups)
            columns = []
            for h in range(full + 1):
                pieces = []
                for z in range(t * near, (t + 2) * near):
                    at = z * full + h if h < full else depth * full + z % half
                    for x in range(chips):
                        a, b = own[x, y, at], other[x, y, at]
                        pieces += [jnp.where(is_low, a, b), jnp.where(is_low, b, a)]
                columns.append(jnp.concatenate(pieces, axis=0))
                wide = columns[h].astype(jnp.float32)
                wide = wide if h < full else jnp.where(is_own, wide, 0.0)
                batch_norm += jnp.sum(wide * wide, axis=1, keepdims=True)
            ends.append(columns.pop())
            inner += jnp.dot(
                jnp.concatenate(columns, axis=1),
                centers[s][: full * lanes],
                preferred_element_type=jnp.float32,
            )
        inner += jnp.dot(
            jnp.concatenate(ends, axis=1),
            high_tail if is_high else low_tail,
            preferred_element_type=jnp.float32,
        )
        squared = center_norm + batch_norm - 2.0 * inner
        values = jnp.exp(-jnp.sqrt(jnp.maximum(squared, 0.0)) / spread)
        out = product(weights, in_two(values), LAST)
        for j in range(2):
            part = out[:, j * lanes : (j + 1) * lanes]
            sums[t + j, :padded, :] = part[:padded]
            at = padded + (t + j) * split
            sums[:, at : at + split, :] = part[padded:].reshape(blocks, split, lanes)


def lift(vectors, scale, index, lifted, weights):
    count = weights.shape[1]
    slots = lax.broadcasted_iota(jnp.int32, (count, index.shape[1]), 0) + lax.axis_index(ROWS) * count
    hits = (index[...] == slots).astype(jnp.bfloat16)
    turned = vectors[...].T
    total = jnp.zeros(weights.shape, jnp.float32)
    for part in in_two(turned):
        total += lax.dot_general(part, hits, LAST, preferred_element_type=jnp.float32)
    lifted[...] = total.reshape(lifted.shape)
    column = jnp.broadcast_to(scale[...], (8, scale.shape[1])).T[:, :1]
    weights[...] = total * (step_rate * column)


def block_of(own, other, j):
    core, chip = j // own.shape[0], j % own.shape[0]
    return jnp.where(lax.axis_index(K) == core, own[chip], other[chip])


def gradient_of(own, other, labels, j, classes):
    rows, lanes = own.shape[1:]
    ids = lax.broadcasted_iota(jnp.int32, (rows, lanes), 0) + lax.axis_index(Y) * classes
    return block_of(own, other, j) - (labels[j] == ids).astype(jnp.float32)


def project(own, other, first, second, third, fourth, labels, projected, *, classes):
    blocks, split, lanes = first.shape
    groups = projected.shape[1] // split
    pieces = (first, second, third, fourth)[:groups]
    total = jnp.zeros(projected.shape[1:], jnp.float32)
    for t in range(0, blocks, 2):
        pair = (t, t + 1)
        lines = [jnp.concatenate([p[j] for j in pair], axis=1) for p in pieces]
        gradient = [gradient_of(own, other, labels, j, classes) for j in pair]
        total += product(
            in_two(jnp.concatenate(lines, axis=0)),
            in_two(jnp.concatenate(gradient, axis=1)),
            LAST,
        )
    for s in range(groups):
        at = pl.multiple_of(lax.rem(lax.axis_index(Y) + s, groups) * split, split)
        part = total[s * split : (s + 1) * split]
        projected[:, pl.ds(at, split), :] = jnp.broadcast_to(
            part[None], (projected.shape[0], *part.shape)
        )


def step_batch(own, other, labels, index, coefficients, output, updated):
    chips, rows, lanes = own.shape
    classes, count = coefficients.shape
    total = jnp.zeros((rows, count), jnp.float32)
    slots = lax.broadcasted_iota(jnp.int32, (count, lanes), 0) + lax.axis_index(ROWS) * count
    for t in range(0, 2 * chips, 2):
        pair = (t, t + 1)
        gradient = [gradient_of(own, other, labels, j, classes) for j in pair]
        hits = [(index[j] == slots).astype(jnp.float32) for j in pair]
        spots = jnp.concatenate(hits, axis=1).astype(jnp.bfloat16)
        for part in in_two(jnp.concatenate(gradient, axis=1)):
            total += lax.dot_general(part, spots, LAST, preferred_element_type=jnp.float32)
        for j in pair:
            output[:, j * lanes : (j + 1) * lanes] = block_of(own, other, j)[:classes]
    updated[...] = coefficients[...] - step_rate * total[:classes]


def correct(updated, projected, weights, result):
    classes = updated.shape[0]
    change = product(in_two(projected[...]), in_two(weights[...]), FIRST)
    result[...] = updated[...] + change[:classes]


def kernel(body, outs, name, scratch=(), limit=16, **settings):
    near = pl.BlockSpec(memory_space=pltpu.VMEM)

    def call(*operands):
        return pl.pallas_call(
            functools.partial(body, **settings),
            out_shape=outs,
            in_specs=[near for _ in operands],
            out_specs=jax.tree.map(lambda _: near, outs),
            scratch_shapes=scratch,
            compiler_params=pltpu.CompilerParams(vmem_limit_bytes=limit * 2**20),
            interpret=INTERPRET,
            name=name,
        )(*operands)

    return call


def from_others(value, axis):
    size = lax.axis_size(axis)
    pieces = [value]
    for s in range(1, size):
        pieces.append(lax.ppermute(value, axis, [((d + s) % size, d) for d in range(size)]))
    return pieces + [value] * (4 - size)


def shards(
    centers,
    coefficients,
    batch_features,
    batch_labels,
    batch_index,
    subset_index,
    eigen_vectors,
    eigen_scale,
):
    depth, chips, cores, groups = (lax.axis_size(a) for a in (Z, X, K, Y))
    blocks = chips * cores
    count = centers.shape[0]
    classes = coefficients.shape[0]
    vectors = eigen_vectors.shape[1]
    split = vectors // groups // blocks
    padded = -(-classes // 8) * 8
    while (padded + vectors // groups) % (8 * depth):
        padded += 8
    lines = padded + vectors // groups
    batch = blocks * LANES
    array = lambda *shape: jax.ShapeDtypeStruct(shape, jnp.float32)

    with jax.named_scope("centers_gather"):
        center_pieces = from_others(centers.T, Y)
    with jax.named_scope("batch_z"):
        batch_own = gathered(batch_features, Z)
    batch_own, center_pieces = lax.optimization_barrier((batch_own, center_pieces))
    rows, width = batch_features.shape
    granules = (depth * (2 * width // LANES) // 2, rows, LANES)
    copies = kernel(
        pack,
        jax.ShapeDtypeStruct((chips * groups, *granules), batch_own.dtype),
        "pack",
        (pltpu.VMEM(granules, batch_own.dtype),),
        limit=2,
    )(batch_own)
    with jax.named_scope("batch_xy"):
        batch_own = lax.all_to_all(copies, (X, Y), 0, 0, tiled=True)
    batch_own = batch_own.reshape(chips, groups, *granules)
    batch_other = from_others(batch_own, K)[1]

    lifted, weights = kernel(
        lift, (array(blocks, groups, split, count), array(vectors, count)), "lift", limit=4
    )(eigen_vectors, eigen_scale[None], subset_index[None])
    labels = batch_labels.reshape(blocks, 1, LANES)
    index = batch_index.reshape(blocks, 1, LANES)

    sums = kernel(
        kernel_products,
        array(blocks, lines, LANES),
        "kernel_products",
        (pltpu.VMEM((lines, count), jnp.float32),),
    )(
        batch_own,
        batch_other,
        *center_pieces,
        coefficients,
        lifted,
    )

    own = scattered(sums.reshape(cores, chips, lines, LANES), K)
    own = scattered(own, X)
    own = scattered(own.reshape(depth, lines // depth, LANES), Z)
    own = gathered(own, Z).reshape(lines, LANES)
    with jax.named_scope("basis_gather"):
        basis = from_others(own[padded:].reshape(blocks, split, LANES), Y)
    predicted, basis = lax.optimization_barrier((gathered(own[:padded], X), basis))
    predicted = from_others(predicted, K)[:2]

    copies = kernel(
        project, array(blocks, groups * split, padded), "project", classes=classes
    )(*predicted, *basis, labels)
    with jax.named_scope("projected_gather"):
        projected = lax.all_to_all(copies, (K, X), 0, 0, tiled=True).reshape(vectors, padded)

    output, updated = kernel(
        step_batch, (array(classes, batch), array(classes, count)), "step_batch"
    )(*predicted, labels, index, coefficients)
    result = kernel(correct, array(classes, count), "correct")(updated, projected, weights)
    return (output, result)


def solution(mesh, shape=(16, 4, 2)):
    finer = Mesh(mesh.devices.reshape(*shape, mesh.shape["cls"]), (*ROWS, Y))
    placed = (P(ROWS, Y), P(Y, ROWS), P(ROWS, Y), P(), P(), P(ROWS), P(ROWS, None), P())
    return jax.shard_map(
        shards,
        mesh=finer,
        in_specs=placed,
        out_specs=(P(Y, None), P(Y, ROWS)),
        check_vma=False,
    )
```

time: 186 us -> 175 us (0.941)
  blocking collectives: 95 us -> 87.5 us
  Pallas kernels: 10.9 us -> 8.47 us
  waiting for transfers between devices: 15.1 us -> 17.4 us
    all_to_all x3 -> x1, blocking collectives: 52.4 us -> 20.7 us  [gathered(): return lax.all_to_all(copies, axis, 0, 0, tiled=True)]
    all_to_all x0 -> x1, blocking collectives: none -> 24.1 us  [shards(): batch_own = lax.all_to_all(copies, (X, Y), 0, 0, tiled=True)]
    all_to_all x3 -> x2, starting transfers between devices: 28.6 us -> 19.2 us  [gathered(): return lax.all_to_all(copies, axis, 0, 0, tiled=True)]
    ppermute x7 -> x8, starting transfers between devices: 25.3 us -> 33 us  [from_others(): lax.ppermute(value, axis, [((d + s) % size, d) for d in range(size)])]
    ppermute x7 -> x8, waiting for transfers between devices: 6.12 us -> 9.59 us  [from_others(): lax.ppermute(value, axis, [((d + s) % size, d) for d in range(size)])]
    pallas_call x4 -> x6, Pallas kernels: 10.9 us -> 8.47 us  [call(): pl.pallas_call(functools.partial(body, **settings), out_shape=outs, in_sp...]
  transfers between devices with their start and end apart: 11 -> 11, of which waited for: 5 -> 6; matrix products, arithmetic and copies ran while one was open for 1% -> 0% of each run, Pallas kernels for 1% -> 1%
where the time goes in v3:
time: 175 us; the launch traced here: 174 us
  blocking collectives  87.5 us (50%)
  starting transfers between devices  57.3 us (33%)
  waiting for transfers between devices  17.4 us (10%)
  Pallas kernels  8.47 us (5%)
  local copies, waits for them, and re-layouts  2.24 us (1%)
    all_to_all x3, blocking collectives, scattered(): return jnp.sum(lax.all_to_all(tiles, axis, 0, 0, tiled=True), axis=0)  42.6 us
    ppermute x8, starting transfers between devices, from_others(): lax.ppermute(value, axis, [((d + s) % size, d) for d in range(size)])  33 us
    all_to_all x1, blocking collectives, shards(): batch_own = lax.all_to_all(copies, (X, Y), 0, 0, tiled=True)  24.1 us
    all_to_all x1, blocking collectives, gathered(): return lax.all_to_all(copies, axis, 0, 0, tiled=True)  20.7 us
    all_to_all x2, starting transfers between devices, gathered(): return lax.all_to_all(copies, axis, 0, 0, tiled=True)  19.2 us
    ppermute x8, waiting for transfers between devices, from_others(): lax.ppermute(value, axis, [((d + s) % size, d) for d in range(size)])  9.59 us
    pallas_call x6, Pallas kernels, call(): pl.pallas_call(functools.partial(body, **settings), out_shape=outs, in_sp...  8.47 us
    all_to_all x1, waiting for transfers between devices, shards(): lax.all_to_all(copies, (K, X), 0, 0, tiled=True).reshape(vectors, padded)  7.82 us
  transfers between devices with their start and end apart: 11, of which 6 were waited for; matrix products, arithmetic and copies ran while one was open for 0% of the time, Pallas kernels for 1%

profile of v3, /device:TPU:1, one launch (start us, length us, event | category | flops | bytes accessed | tf_op | source)
XLA Modules:
  0.0 174.0 jit_solution(10456118168788958426)
XLA Ops:
  0.6 1.3 broadcast_in_dim.15
  2.0 15.7 %all-to-all-start = ((bf16[16,8,320]{2,1,0:T(8,128)(2,1)}), bf16[16,8,320]{2,1,0:T(8,128)(2,1)S(1)}, u32[]{:S(2)}, u32[]{:S(2)}) async-start(bf16[16,8,320]{2,1,0:T(8,128)(2,1)} %broadcast_in_dim.15), calls=%async_computation | async-start | bytes 196608 | tf_op jit(solution)/shard_map/batch_z/all_to_all | solution.py:26
  17.7 3.2 %collective-permute-start.2 = (bf16[320,256]{1,0:T(8,128)(2,1)}, bf16[320,256]{1,0:T(8,128)(2,1)S(1)}, u32[]{:S(2)}, u32[]{:S(2)}) collective-permute-start(bf16[320,256]{1,0:T(8,128)(2,1)} %bitcast.19), channel_id=1, source_target_pairs={{3,0},{0,1},{1,2},{2,3},{7,4},{4,5},{5,6},{6,7},{11,8},{8,9},{9,10... | collective-permute-start | bytes 491528 | tf_op jit(solution)/shard_map/centers_gather/ppermute | solution.py:221
  20.9 4.5 %collective-permute-start.1 = (bf16[320,256]{1,0:T(8,128)(2,1)}, bf16[320,256]{1,0:T(8,128)(2,1)S(1)}, u32[]{:S(2)}, u32[]{:S(2)}) collective-permute-start(bf16[320,256]{1,0:T(8,128)(2,1)} %bitcast.20), channel_id=1, source_target_pairs={{2,0},{3,1},{0,2},{1,3},{6,4},{7,5},{4,6},{5,7},{10,8},{11,9},{8,1... | collective-permute-start | bytes 491528 | tf_op jit(solution)/shard_map/centers_gather/ppermute | solution.py:221
  25.5 3.0 %collective-permute-start = (bf16[320,256]{1,0:T(8,128)(2,1)}, bf16[320,256]{1,0:T(8,128)(2,1)S(1)}, u32[]{:S(2)}, u32[]{:S(2)}) collective-permute-start(bf16[320,256]{1,0:T(8,128)(2,1)} %bitcast.21), channel_id=1, source_target_pairs={{1,0},{2,1},{3,2},{0,3},{5,4},{6,5},{7,6},{4,7},{9,8},{10,9},{11,1... | collective-permute-start | bytes 491528 | tf_op jit(solution)/shard_map/centers_gather/ppermute | solution.py:221
  28.5 0.0 collective-permute-done.2.fourth
  28.5 2.3 %collective-permute-done.1.third = bf16[320,256]{1,0:T(8,128)(2,1)S(1)} collective-permute-done((bf16[320,256]{1,0:T(8,128)(2,1)}, bf16[320,256]{1,0:T(8,128)(2,1)S(1)}, u32[]{:S(2)}, u32[]{:S(2)}) %collective-permute-start.1) | collective-permute-done | bytes 163872 | tf_op jit(solution)/shard_map/centers_gather/ppermute | solution.py:221
  30.8 1.2 collective-permute-done.second
  32.0 0.0 all-to-all-done.batch
  32.0 0.2 pack.1
  32.2 0.0 copy-start.2
  32.2 0.0 copy-start.5
  32.2 0.0 copy-start.6
  32.2 0.0 copy-start
  32.3 0.0 copy-start.1
  32.3 24.1 %all_to_all.40 = bf16[16,40,8,128]{3,2,1,0:T(8,128)(2,1)S(1)} all-to-all(bf16[16,40,8,128]{3,2,1,0:T(8,128)(2,1)S(1)} %pack.1), channel_id=1, replica_groups=mesh['rows_z'=16,'rows_x'=4,'rows_k'=2,'cls'=4] {'rows_x','cls'}, dimensions={0} | all-to-all | bytes 2621440 | tf_op jit(solution)/shard_map/batch_xy/all_to_all | solution.py:263
  56.4 5.3 %collective-permute-start.3 = (bf16[4,4,40,8,128]{4,3,2,1,0:T(8,128)(2,1)S(1)}, bf16[4,4,40,8,128]{4,3,2,1,0:T(8,128)(2,1)S(1)}, u32[]{:S(2)}, u32[]{:S(2)}) collective-permute-start(bf16[4,4,40,8,128]{4,3,2,1,0:T(8,128)(2,1)S(1)} %bitcast.12), channel_id=1, source_target_pairs={{4,0},{0,4},{5,1},{1,5},{6,2},{2,6},{7,3},{3,7},{12,8},{8,12},{13,... | collective-permute-start | bytes 3932168 | tf_op jit(solution)/shard_map/ppermute | solution.py:221
  61.6 0.0 copy-done.2
  61.6 0.0 copy-done.5
  61.7 0.0 copy-done.6
  61.7 0.4 lift.1
  62.1 2.2 %collective-permute-done.3.other = bf16[4,4,40,8,128]{4,3,2,1,0:T(8,128)(2,1)S(1)} collective-permute-done((bf16[4,4,40,8,128]{4,3,2,1,0:T(8,128)(2,1)S(1)}, bf16[4,4,40,8,128]{4,3,2,1,0:T(8,128)(2,1)S(1)}, u32[]{:S(2)}, u32[]{:S(2)}) %collective-permute-start.3) | collective-permute-done | bytes 1310752 | tf_op jit(solution)/shard_map/ppermute | solution.py:221
  64.3 0.0 copy-done
  64.3 3.8 %kernel_products.1 = f32[8,384,128]{2,1,0:T(8,128)S(1)} custom-call(bf16[4,4,40,8,128]{4,3,2,1,0:T(8,128)(2,1)S(1)} %bitcast.13, bf16[4,4,40,8,128]{4,3,2,1,0:T(8,128)(2,1)S(1)} %collective-permute-done.3.other, bf16[320,256]{1,0:T(8,128)(2,1)S(1)} %bitcast.22, bf16[320,256]{1,0:T(8,128)(2,1)S(1)} %collective-permute-done.second, ...), custom_call_target="tpu_custom_call" | custom-call | tf_op jit(solution)/shard_map/kernel_products/pallas_call | solution.py:203
  68.1 5.0 %all_to_all.41 = f32[2,4,384,128]{3,2,1,0:T(8,128)S(1)} all-to-all(f32[2,4,384,128]{3,2,1,0:T(8,128)S(1)} %bitcast.11), channel_id=1, replica_groups=mesh['rows_z'=16,'rows_x'=4,'rows_k'=2,'cls'=4] {'rows_k'}, dimensions={0} | all-to-all | bytes 3145728 | tf_op jit(solution)/shard_map/all_to_all | solution.py:30
  73.1 0.2 reduce_sum.27
  73.2 14.4 %all_to_all.42 = f32[4,384,128]{2,1,0:T(8,128)S(1)} all-to-all(f32[4,384,128]{2,1,0:T(8,128)S(1)} %reduce_sum.27), channel_id=1, replica_groups=mesh['rows_z'=16,'rows_x'=4,'rows_k'=2,'cls'=4] {'rows_x'}, dimensions={0} | all-to-all | bytes 1572864 | tf_op jit(solution)/shard_map/all_to_all | solution.py:30
  87.7 23.2 %all_to_all.43 = f32[16,24,128]{2,1,0:T(8,128)S(1)} all-to-all(f32[16,24,128]{2,1,0:T(8,128)S(1)} %bitcast.28), channel_id=1, replica_groups=mesh['rows_z'=16,'rows_x'=4,'rows_k'=2,'cls'=4] {'rows_z'}, dimensions={0} | all-to-all | bytes 393216 | tf_op jit(solution)/shard_map/all_to_all | solution.py:30
  110.9 0.0 copy-start.3
  111.0 20.7 %all_to_all.44 = f32[16,24,128]{2,1,0:T(8,128)S(1)} all-to-all(f32[16,24,128]{2,1,0:T(8,128)S(1)} %broadcast_in_dim.18), channel_id=1, replica_groups=mesh['rows_z'=16,'rows_x'=4,'rows_k'=2,'cls'=4] {'rows_z'}, dimensions={0} | all-to-all | bytes 393216 | tf_op jit(solution)/shard_map/all_to_all | solution.py:26
  131.7 0.8 broadcast_in_dim.19
  132.6 3.5 %all-to-all-start.6 = ((f32[4,256,128]{2,1,0:T(8,128)}), f32[4,256,128]{2,1,0:T(8,128)S(1)}, u32[]{:S(2)}, u32[]{:S(2)}) async-start(f32[4,256,128]{2,1,0:T(8,128)} %broadcast_in_dim.19), calls=%async_computation.6 | async-start | bytes 1048576 | tf_op jit(solution)/shard_map/all_to_all | solution.py:26
  136.1 2.0 %collective-permute-start.6 = (f32[8,16,128]{2,1,0:T(8,128)S(1)}, f32[8,16,128]{2,1,0:T(8,128)S(1)}, u32[]{:S(2)}, u32[]{:S(2)}) collective-permute-start(f32[8,16,128]{2,1,0:T(8,128)S(1)} %bitcast.15), channel_id=1, source_target_pairs={{3,0},{0,1},{1,2},{2,3},{7,4},{4,5},{5,6},{6,7},{11,8},{8,9},{9,10... | collective-permute-start | bytes 196616 | tf_op jit(solution)/shard_map/basis_gather/ppermute | solution.py:221
  138.1 3.7 %collective-permute-start.5 = (f32[8,16,128]{2,1,0:T(8,128)S(1)}, f32[8,16,128]{2,1,0:T(8,128)S(1)}, u32[]{:S(2)}, u32[]{:S(2)}) collective-permute-start(f32[8,16,128]{2,1,0:T(8,128)S(1)} %bitcast.16), channel_id=1, source_target_pairs={{2,0},{3,1},{0,2},{1,3},{6,4},{7,5},{4,6},{5,7},{10,8},{11,9},{8,1... | collective-permute-start | bytes 196616 | tf_op jit(solution)/shard_map/basis_gather/ppermute | solution.py:221
  141.8 3.0 %collective-permute-start.4 = (f32[8,16,128]{2,1,0:T(8,128)S(1)}, f32[8,16,128]{2,1,0:T(8,128)S(1)}, u32[]{:S(2)}, u32[]{:S(2)}) collective-permute-start(f32[8,16,128]{2,1,0:T(8,128)S(1)} %bitcast.17), channel_id=1, source_target_pairs={{1,0},{2,1},{3,2},{0,3},{5,4},{6,5},{7,6},{4,7},{9,8},{10,9},{11,1... | collective-permute-start | bytes 196616 | tf_op jit(solution)/shard_map/basis_gather/ppermute | solution.py:221
  144.7 0.0 collective-permute-done.6.fourth
  144.7 0.0 collective-permute-done.5.third
  144.7 2.3 %collective-permute-done.4.second = f32[8,16,128]{2,1,0:T(8,128)S(1)} collective-permute-done((f32[8,16,128]{2,1,0:T(8,128)S(1)}, f32[8,16,128]{2,1,0:T(8,128)S(1)}, u32[]{:S(2)}, u32[]{:S(2)}) %collective-permute-start.4) | collective-permute-done | bytes 65568 | tf_op jit(solution)/shard_map/basis_gather/ppermute | solution.py:221
  147.1 0.0 all-to-all-done.6.own
  147.1 8.4 %collective-permute-start.7 = (f32[4,256,128]{2,1,0:T(8,128)S(1)}, f32[4,256,128]{2,1,0:T(8,128)S(1)}, u32[]{:S(2)}, u32[]{:S(2)}) collective-permute-start(f32[4,256,128]{2,1,0:T(8,128)S(1)} %all-to-all-done.6.own), channel_id=1, source_target_pairs={{4,0},{0,4},{5,1},{1,5},{6,2},{2,6},{7,3},{3,7},{12,8},{8,12},{13,... | collective-permute-start | bytes 1572872 | tf_op jit(solution)/shard_map/ppermute | solution.py:221
  155.5 1.5 collective-permute-done.7.other
  157.0 0.0 copy-done.3
  157.0 1.4 project.1
  158.4 5.1 %all-to-all-start.7 = ((f32[8,64,256]{2,1,0:T(8,128)}), f32[8,64,256]{2,1,0:T(8,128)S(1)}, u32[]{:S(2)}, u32[]{:S(2)}) async-start(f32[8,64,256]{2,1,0:T(8,128)} %project.1), calls=%async_computation.7 | async-start | bytes 1048576 | tf_op jit(solution)/shard_map/projected_gather/all_to_all | solution.py:299
  163.6 0.0 copy-done.4
  163.6 1.5 step_batch.1
  165.1 7.8 %all-to-all-done.7 = f32[8,64,256]{2,1,0:T(8,128)S(1)} async-done(((f32[8,64,256]{2,1,0:T(8,128)}), f32[8,64,256]{2,1,0:T(8,128)S(1)}, u32[]{:S(2)}, u32[]{:S(2)}) %all-to-all-start.7) | async-done | bytes 524320 | tf_op jit(solution)/shard_map/projected_gather/all_to_all | solution.py:299
  172.9 1.1 correct.1
  (7 shorter events, 0.1 us)
Async XLA Ops:
  2.0 30.0 %all-to-all-start = ((bf16[16,8,320]{2,1,0:T(8,128)(2,1)}), bf16[16,8,320]{2,1,0:T(8,128)(2,1)S(1)}, u32[]{:S(2)}, u32[]{:S(2)}) async-start(bf16[16,8,320]{2,1,0:T(8,128)(2,1)} %broadcast_in_dim.15), calls=%async_computation | async-start | bytes 196608 | tf_op jit(solution)/shard_map/batch_z/all_to_all | solution.py:26
  17.7 10.7 %collective-permute-start.2 = (bf16[320,256]{1,0:T(8,128)(2,1)}, bf16[320,256]{1,0:T(8,128)(2,1)S(1)}, u32[]{:S(2)}, u32[]{:S(2)}) collective-permute-start(bf16[320,256]{1,0:T(8,128)(2,1)} %bitcast.19), channel_id=1, source_target_pairs={{3,0},{0,1},{1,2},{2,3},{7,4},{4,5},{5,6},{6,7},{11,8},{8,9},{9,10... | collective-permute-start | bytes 491528 | tf_op jit(solution)/shard_map/centers_gather/ppermute | solution.py:221
  20.9 9.8 %collective-permute-start.1 = (bf16[320,256]{1,0:T(8,128)(2,1)}, bf16[320,256]{1,0:T(8,128)(2,1)S(1)}, u32[]{:S(2)}, u32[]{:S(2)}) collective-permute-start(bf16[320,256]{1,0:T(8,128)(2,1)} %bitcast.20), channel_id=1, source_target_pairs={{2,0},{3,1},{0,2},{1,3},{6,4},{7,5},{4,6},{5,7},{10,8},{11,9},{8,1... | collective-permute-start | bytes 491528 | tf_op jit(solution)/shard_map/centers_gather/ppermute | solution.py:221
  25.5 6.5 %collective-permute-start = (bf16[320,256]{1,0:T(8,128)(2,1)}, bf16[320,256]{1,0:T(8,128)(2,1)S(1)}, u32[]{:S(2)}, u32[]{:S(2)}) collective-permute-start(bf16[320,256]{1,0:T(8,128)(2,1)} %bitcast.21), channel_id=1, source_target_pairs={{1,0},{2,1},{3,2},{0,3},{5,4},{6,5},{7,6},{4,7},{9,8},{10,9},{11,1... | collective-permute-start | bytes 491528 | tf_op jit(solution)/shard_map/centers_gather/ppermute | solution.py:221
  32.2 29.4 %copy-start.2 = (f32[64,512]{1,0:T(8,128)S(1)}, f32[64,512]{1,0:T(8,128)}, u32[]{:S(2)}) copy-start(f32[64,512]{1,0:T(8,128)} %vectors.1) | copy-start | bytes 393220
  32.2 29.4 %copy-start.5 = (f32[512]{0:T(512)S(1)}, f32[512]{0:T(512)}, u32[]{:S(2)}) copy-start(f32[512]{0:T(512)} %param.15) | copy-start | bytes 6148
  32.2 29.4 %copy-start.6 = (s32[64]{0:T(128)S(1)}, s32[64]{0:T(128)}, u32[]{:S(2)}) copy-start(s32[64]{0:T(128)} %param.13) | copy-start | bytes 772
  32.2 32.0 %copy-start = (f32[250,256]{1,0:T(8,128)S(1)}, f32[250,256]{1,0:T(8,128)}, u32[]{:S(2)}) copy-start(f32[250,256]{1,0:T(8,128)} %coefficients.3) | copy-start | bytes 768004
  32.3 32.0 %copy-start.1 = (bf16[256,320]{0,1:T(8,128)(2,1)S(1)}, bf16[256,320]{0,1:T(8,128)(2,1)}, u32[]{:S(2)}) copy-start(bf16[256,320]{0,1:T(8,128)(2,1)} %param.8) | copy-start | bytes 491524
  56.4 7.9 %collective-permute-start.3 = (bf16[4,4,40,8,128]{4,3,2,1,0:T(8,128)(2,1)S(1)}, bf16[4,4,40,8,128]{4,3,2,1,0:T(8,128)(2,1)S(1)}, u32[]{:S(2)}, u32[]{:S(2)}) collective-permute-start(bf16[4,4,40,8,128]{4,3,2,1,0:T(8,128)(2,1)S(1)} %bitcast.12), channel_id=1, source_target_pairs={{4,0},{0,4},{5,1},{1,5},{6,2},{2,6},{7,3},{3,7},{12,8},{8,12},{13,... | collective-permute-start | bytes 3932168 | tf_op jit(solution)/shard_map/ppermute | solution.py:221
  110.9 46.0 %copy-start.3 = (s32[1024]{0:T(1024)S(1)}, s32[1024]{0:T(1024)}, u32[]{:S(2)}) copy-start(s32[1024]{0:T(1024)} %param.11) | copy-start | bytes 12292
  132.6 14.5 %all-to-all-start.6 = ((f32[4,256,128]{2,1,0:T(8,128)}), f32[4,256,128]{2,1,0:T(8,128)S(1)}, u32[]{:S(2)}, u32[]{:S(2)}) async-start(f32[4,256,128]{2,1,0:T(8,128)} %broadcast_in_dim.19), calls=%async_computation.6 | async-start | bytes 1048576 | tf_op jit(solution)/shard_map/all_to_all | solution.py:26
  136.1 8.7 %collective-permute-start.6 = (f32[8,16,128]{2,1,0:T(8,128)S(1)}, f32[8,16,128]{2,1,0:T(8,128)S(1)}, u32[]{:S(2)}, u32[]{:S(2)}) collective-permute-start(f32[8,16,128]{2,1,0:T(8,128)S(1)} %bitcast.15), channel_id=1, source_target_pairs={{3,0},{0,1},{1,2},{2,3},{7,4},{4,5},{5,6},{6,7},{11,8},{8,9},{9,10... | collective-permute-start | bytes 196616 | tf_op jit(solution)/shard_map/basis_gather/ppermute | solution.py:221
  138.1 6.6 %collective-permute-start.5 = (f32[8,16,128]{2,1,0:T(8,128)S(1)}, f32[8,16,128]{2,1,0:T(8,128)S(1)}, u32[]{:S(2)}, u32[]{:S(2)}) collective-permute-start(f32[8,16,128]{2,1,0:T(8,128)S(1)} %bitcast.16), channel_id=1, source_target_pairs={{2,0},{3,1},{0,2},{1,3},{6,4},{7,5},{4,6},{5,7},{10,8},{11,9},{8,1... | collective-permute-start | bytes 196616 | tf_op jit(solution)/shard_map/basis_gather/ppermute | solution.py:221
  141.8 5.3 %collective-permute-start.4 = (f32[8,16,128]{2,1,0:T(8,128)S(1)}, f32[8,16,128]{2,1,0:T(8,128)S(1)}, u32[]{:S(2)}, u32[]{:S(2)}) collective-permute-start(f32[8,16,128]{2,1,0:T(8,128)S(1)} %bitcast.17), channel_id=1, source_target_pairs={{1,0},{2,1},{3,2},{0,3},{5,4},{6,5},{7,6},{4,7},{9,8},{10,9},{11,1... | collective-permute-start | bytes 196616 | tf_op jit(solution)/shard_map/basis_gather/ppermute | solution.py:221
  147.1 9.9 %collective-permute-start.7 = (f32[4,256,128]{2,1,0:T(8,128)S(1)}, f32[4,256,128]{2,1,0:T(8,128)S(1)}, u32[]{:S(2)}, u32[]{:S(2)}) collective-permute-start(f32[4,256,128]{2,1,0:T(8,128)S(1)} %all-to-all-done.6.own), channel_id=1, source_target_pairs={{4,0},{0,4},{5,1},{1,5},{6,2},{2,6},{7,3},{3,7},{12,8},{8,12},{13,... | collective-permute-start | bytes 1572872 | tf_op jit(solution)/shard_map/ppermute | solution.py:221
  157.0 6.6 %copy-start.4 = (s32[1024]{0:T(1024)S(1)}, s32[1024]{0:T(1024)}, u32[]{:S(2)}) copy-start(s32[1024]{0:T(1024)} %param.12) | copy-start | bytes 12292
  158.4 14.5 %all-to-all-start.7 = ((f32[8,64,256]{2,1,0:T(8,128)}), f32[8,64,256]{2,1,0:T(8,128)S(1)}, u32[]{:S(2)}, u32[]{:S(2)}) async-start(f32[8,64,256]{2,1,0:T(8,128)} %project.1), calls=%async_computation.7 | async-start | bytes 1048576 | tf_op jit(solution)/shard_map/projected_gather/all_to_all | solution.py:299

commit v4 on v3

--- a/solution.py
+++ b/solution.py
@@ -40,6 +40,16 @@
     (a, b), (c, d) = left, right
     one = lambda u, v: lax.dot_general(u, v, dims, preferred_element_type=jnp.float32)
     return one(a, d) + one(b, c) + one(a, c)
+
+
+def fan(value, copies):
+    copies[...] = jnp.broadcast_to(value[...][None], copies.shape)
+
+
+def part(sums, copies, basis):
+    padded = copies.shape[1]
+    copies[...] = jnp.broadcast_to(sums[:padded][None], copies.shape)
+    basis[...] = sums[padded:].reshape(basis.shape)
 
 
 def pack(batch, copies, granules):
@@ -245,11 +255,22 @@
     batch = blocks * LANES
     array = lambda *shape: jax.ShapeDtypeStruct(shape, jnp.float32)
 
+    with jax.named_scope("batch_z"):
+        batch_own = lax.all_to_all(
+            kernel(
+                fan,
+                jax.ShapeDtypeStruct((depth, *batch_features.shape), batch_features.dtype),
+                "fan",
+                limit=2,
+            )(batch_features),
+            Z,
+            0,
+            0,
+            tiled=True,
+        )
+    batch_own, turned = lax.optimization_barrier((batch_own, centers.T))
     with jax.named_scope("centers_gather"):
-        center_pieces = from_others(centers.T, Y)
-    with jax.named_scope("batch_z"):
-        batch_own = gathered(batch_features, Z)
-    batch_own, center_pieces = lax.optimization_barrier((batch_own, center_pieces))
+        center_pieces = from_others(turned, Y)
     rows, width = batch_features.shape
     granules = (depth * (2 * width // LANES) // 2, rows, LANES)
     copies = kernel(
@@ -261,6 +282,7 @@
     )(batch_own)
     with jax.named_scope("batch_xy"):
         batch_own = lax.all_to_all(copies, (X, Y), 0, 0, tiled=True)
+    batch_own, center_pieces = lax.optimization_barrier((batch_own, center_pieces))
     batch_own = batch_own.reshape(chips, groups, *granules)
     batch_other = from_others(batch_own, K)[1]
 
@@ -287,9 +309,13 @@
     own = scattered(own, X)
     own = scattered(own.reshape(depth, lines // depth, LANES), Z)
     own = gathered(own, Z).reshape(lines, LANES)
+    copies, basis = kernel(
+        part, (array(chips, padded, LANES), array(blocks, split, LANES)), "part", limit=4
+    )(own)
     with jax.named_scope("basis_gather"):
-        basis = from_others(own[padded:].reshape(blocks, split, LANES), Y)
-    predicted, basis = lax.optimization_barrier((gathered(own[:padded], X), basis))
+        basis = from_others(basis, Y)
+    predicted = lax.all_to_all(copies, X, 0, 0, tiled=True)
+    predicted, basis = lax.optimization_barrier((predicted, basis))
     predicted = from_others(predicted, K)[:2]
 
     copies = kernel(

time: 175 us -> 173 us (0.989)
  waiting for transfers between devices: 17.4 us -> 27.7 us
  starting transfers between devices: 57.3 us -> 48.7 us
  blocking collectives: 87.5 us -> 83.4 us
  Pallas kernels: 8.47 us -> 10.4 us
    ppermute x8, waiting for transfers between devices: 9.59 us -> 19.9 us  [from_others(): lax.ppermute(value, axis, [((d + s) % size, d) for d in range(size)])]
    all_to_all x2, starting transfers between devices: 19.2 us -> 10.4 us  [the longest x1 6.9 us: shards(): batch_own = lax.all_to_all(copies, (X, Y), 0, 0, tiled=True)]
    all_to_all x3, blocking collectives: 42.6 us -> 36 us  [scattered(): return jnp.sum(lax.all_to_all(tiles, axis, 0, 0, tiled=True), axis=0)]
    all_to_all x1, blocking collectives: 24.1 us -> 27.4 us  [shards(): lax.all_to_all(kernel(fan, jax.ShapeDtypeStruct((depth, *batch_features.s...]
    broadcast_in_dim x3 -> x1, local copies, waits for them, and re-layouts: 2.18 us -> 0.01 us  [gathered(): copies = jnp.broadcast_to(value, (lax.axis_size(axis), *value.shape))]
    pallas_call x6 -> x8, Pallas kernels: 8.47 us -> 10.4 us  [call(): pl.pallas_call(functools.partial(body, **settings), out_shape=outs, in_sp...]
where the time goes in v4:
time: 173 us; the launch traced here: 172 us
  blocking collectives  83.4 us (48%)
  starting transfers between devices  48.7 us (28%)
  waiting for transfers between devices  27.7 us (16%)
  Pallas kernels  10.4 us (6%)
    all_to_all x3, blocking collectives, scattered(): return jnp.sum(lax.all_to_all(tiles, axis, 0, 0, tiled=True), axis=0)  36 us
    ppermute x8, starting transfers between devices, from_others(): lax.ppermute(value, axis, [((d + s) % size, d) for d in range(size)])  33.2 us
    all_to_all x1, blocking collectives, shards(): lax.all_to_all(kernel(fan, jax.ShapeDtypeStruct((depth, *batch_features.s...  27.4 us
    all_to_all x1, blocking collectives, gathered(): return lax.all_to_all(copies, axis, 0, 0, tiled=True)  20 us
    ppermute x8, waiting for transfers between devices, from_others(): lax.ppermute(value, axis, [((d + s) % size, d) for d in range(size)])  19.9 us
    pallas_call x8, Pallas kernels, call(): pl.pallas_call(functools.partial(body, **settings), out_shape=outs, in_sp...  10.4 us
    all_to_all x1, waiting for transfers between devices, shards(): lax.all_to_all(copies, (K, X), 0, 0, tiled=True).reshape(vectors, padded)  7.82 us
    all_to_all x1, starting transfers between devices, shards(): batch_own = lax.all_to_all(copies, (X, Y), 0, 0, tiled=True)  6.9 us
  transfers between devices with their start and end apart: 11, of which 6 were waited for; matrix products, arithmetic and copies ran while one was open for 0% of the time, Pallas kernels for 1%

profile of v4, /device:TPU:1, one launch (start us, length us, event | category | flops | bytes accessed | tf_op | source)
XLA Modules:
  0.0 172.0 jit_solution(12793341771842047178)
XLA Ops:
  0.6 0.0 copy-start.4
  0.6 0.7 copy-done.4
  1.3 27.4 %all_to_all.40.batch = bf16[16,8,320]{2,1,0:T(8,128)(2,1)S(1)} all-to-all(bf16[16,8,320]{2,1,0:T(8,128)(2,1)S(1)} %fan.1), channel_id=1, replica_groups=mesh['rows_z'=16,'rows_x'=4,'rows_k'=2,'cls'=4] {'rows_z'}, dimensions={0} | all-to-all | bytes 163840 | tf_op jit(solution)/shard_map/batch_z/all_to_all | solution.py:259
  28.7 1.3 pack.1
  30.0 0.0 copy-start.1
  30.0 0.0 copy-start.2
  30.0 0.0 copy-start
  30.0 6.9 %all-to-all-start.1 = ((bf16[16,40,8,128]{3,2,1,0:T(8,128)(2,1)}), bf16[16,40,8,128]{3,2,1,0:T(8,128)(2,1)S(1)}, u32[]{:S(2)}, u32[]{:S(2)}) async-start(bf16[16,40,8,128]{3,2,1,0:T(8,128)(2,1)} %pack.1), calls=%async_computation.1 | async-start | bytes 2621440 | tf_op jit(solution)/shard_map/batch_xy/all_to_all | solution.py:284
  36.9 0.0 copy-done.1
  36.9 3.3 %collective-permute-start.2 = (bf16[320,256]{1,0:T(8,128)(2,1)S(1)}, bf16[320,256]{1,0:T(8,128)(2,1)S(1)}, u32[]{:S(2)}, u32[]{:S(2)}) collective-permute-start(bf16[320,256]{1,0:T(8,128)(2,1)S(1)} %bitcast.15), channel_id=1, source_target_pairs={{3,0},{0,1},{1,2},{2,3},{7,4},{4,5},{5,6},{6,7},{11,8},{8,9},{9,10... | collective-permute-start | bytes 491528 | tf_op jit(solution)/shard_map/centers_gather/ppermute | solution.py:231
  40.2 4.3 %collective-permute-start.1 = (bf16[320,256]{1,0:T(8,128)(2,1)S(1)}, bf16[320,256]{1,0:T(8,128)(2,1)S(1)}, u32[]{:S(2)}, u32[]{:S(2)}) collective-permute-start(bf16[320,256]{1,0:T(8,128)(2,1)S(1)} %bitcast.16), channel_id=1, source_target_pairs={{2,0},{3,1},{0,2},{1,3},{6,4},{7,5},{4,6},{5,7},{10,8},{11,9},{8,1... | collective-permute-start | bytes 491528 | tf_op jit(solution)/shard_map/centers_gather/ppermute | solution.py:231
  44.5 3.1 %collective-permute-start = (bf16[320,256]{1,0:T(8,128)(2,1)S(1)}, bf16[320,256]{1,0:T(8,128)(2,1)S(1)}, u32[]{:S(2)}, u32[]{:S(2)}) collective-permute-start(bf16[320,256]{1,0:T(8,128)(2,1)S(1)} %bitcast.17), channel_id=1, source_target_pairs={{1,0},{2,1},{3,2},{0,3},{5,4},{6,5},{7,6},{4,7},{9,8},{10,9},{11,1... | collective-permute-start | bytes 491528 | tf_op jit(solution)/shard_map/centers_gather/ppermute | solution.py:231
  47.6 7.0 %collective-permute-done.2.fourth = bf16[320,256]{1,0:T(8,128)(2,1)S(1)} collective-permute-done((bf16[320,256]{1,0:T(8,128)(2,1)S(1)}, bf16[320,256]{1,0:T(8,128)(2,1)S(1)}, u32[]{:S(2)}, u32[]{:S(2)}) %collective-permute-start.2) | collective-permute-done | bytes 163872 | tf_op jit(solution)/shard_map/centers_gather/ppermute | solution.py:231
  54.6 6.6 %collective-permute-done.1.third = bf16[320,256]{1,0:T(8,128)(2,1)S(1)} collective-permute-done((bf16[320,256]{1,0:T(8,128)(2,1)S(1)}, bf16[320,256]{1,0:T(8,128)(2,1)S(1)}, u32[]{:S(2)}, u32[]{:S(2)}) %collective-permute-start.1) | collective-permute-done | bytes 163872 | tf_op jit(solution)/shard_map/centers_gather/ppermute | solution.py:231
  61.2 0.0 collective-permute-done.second
  61.2 0.0 all-to-all-done.1
  61.2 4.6 %collective-permute-start.3 = (bf16[4,4,40,8,128]{4,3,2,1,0:T(8,128)(2,1)S(1)}, bf16[4,4,40,8,128]{4,3,2,1,0:T(8,128)(2,1)S(1)}, u32[]{:S(2)}, u32[]{:S(2)}) collective-permute-start(bf16[4,4,40,8,128]{4,3,2,1,0:T(8,128)(2,1)S(1)} %bitcast.11), channel_id=1, source_target_pairs={{4,0},{0,4},{5,1},{1,5},{6,2},{2,6},{7,3},{3,7},{12,8},{8,12},{13,... | collective-permute-start | bytes 3932168 | tf_op jit(solution)/shard_map/ppermute | solution.py:231
  65.8 0.0 copy-done.2
  65.8 0.0 copy-done.6
  65.8 0.0 copy-done.7
  65.8 0.4 lift.1
  66.2 2.2 %collective-permute-done.3.other = bf16[4,4,40,8,128]{4,3,2,1,0:T(8,128)(2,1)S(1)} collective-permute-done((bf16[4,4,40,8,128]{4,3,2,1,0:T(8,128)(2,1)S(1)}, bf16[4,4,40,8,128]{4,3,2,1,0:T(8,128)(2,1)S(1)}, u32[]{:S(2)}, u32[]{:S(2)}) %collective-permute-start.3) | collective-permute-done | bytes 1310752 | tf_op jit(solution)/shard_map/ppermute | solution.py:231
  68.4 0.0 copy-done
  68.4 3.8 %kernel_products.1 = f32[8,384,128]{2,1,0:T(8,128)S(1)} custom-call(bf16[4,4,40,8,128]{4,3,2,1,0:T(8,128)(2,1)S(1)} %bitcast.12, bf16[4,4,40,8,128]{4,3,2,1,0:T(8,128)(2,1)S(1)} %collective-permute-done.3.other, bf16[320,256]{1,0:T(8,128)(2,1)S(1)} %bitcast.18, bf16[320,256]{1,0:T(8,128)(2,1)S(1)} %collective-permute-done.second, ...), custom_call_target="tpu_custom_call" | custom-call | tf_op jit(solution)/shard_map/kernel_products/pallas_call | solution.py:213
  72.2 5.0 %all_to_all.41 = f32[2,4,384,128]{3,2,1,0:T(8,128)S(1)} all-to-all(f32[2,4,384,128]{3,2,1,0:T(8,128)S(1)} %bitcast.10), channel_id=1, replica_groups=mesh['rows_z'=16,'rows_x'=4,'rows_k'=2,'cls'=4] {'rows_k'}, dimensions={0} | all-to-all | bytes 3145728 | tf_op jit(solution)/shard_map/all_to_all | solution.py:30
  77.2 0.2 reduce_sum.27
  77.4 14.0 %all_to_all.42 = f32[4,384,128]{2,1,0:T(8,128)S(1)} all-to-all(f32[4,384,128]{2,1,0:T(8,128)S(1)} %reduce_sum.27), channel_id=1, replica_groups=mesh['rows_z'=16,'rows_x'=4,'rows_k'=2,'cls'=4] {'rows_x'}, dimensions={0} | all-to-all | bytes 1572864 | tf_op jit(solution)/shard_map/all_to_all | solution.py:30
  91.5 0.0 copy-start.3
  91.5 16.9 %all_to_all.43 = f32[16,24,128]{2,1,0:T(8,128)S(1)} all-to-all(f32[16,24,128]{2,1,0:T(8,128)S(1)} %bitcast.24), channel_id=1, replica_groups=mesh['rows_z'=16,'rows_x'=4,'rows_k'=2,'cls'=4] {'rows_z'}, dimensions={0} | all-to-all | bytes 393216 | tf_op jit(solution)/shard_map/all_to_all | solution.py:30
  108.5 20.0 %all_to_all.44 = f32[16,24,128]{2,1,0:T(8,128)S(1)} all-to-all(f32[16,24,128]{2,1,0:T(8,128)S(1)} %broadcast_in_dim.11), channel_id=1, replica_groups=mesh['rows_z'=16,'rows_x'=4,'rows_k'=2,'cls'=4] {'rows_z'}, dimensions={0} | all-to-all | bytes 393216 | tf_op jit(solution)/shard_map/all_to_all | solution.py:26
  128.5 0.8 part.1
  129.3 3.5 %all-to-all-start.6 = ((f32[4,256,128]{2,1,0:T(8,128)}), f32[4,256,128]{2,1,0:T(8,128)S(1)}, u32[]{:S(2)}, u32[]{:S(2)}) async-start(f32[4,256,128]{2,1,0:T(8,128)} %get-tuple-element.28), calls=%async_computation.6 | async-start | bytes 1048576 | tf_op jit(solution)/shard_map/all_to_all | solution.py:317
  132.8 1.9 %collective-permute-start.6 = (f32[8,16,128]{2,1,0:T(8,128)S(1)}, f32[8,16,128]{2,1,0:T(8,128)S(1)}, u32[]{:S(2)}, u32[]{:S(2)}) collective-permute-start(f32[8,16,128]{2,1,0:T(8,128)S(1)} %get-tuple-element.33.first), channel_id=1, source_target_pairs={{3,0},{0,1},{1,2},{2,3},{7,4},{4,5},{5,6},{6,7},{11,8},{8,9},{9,10... | collective-permute-start | bytes 196616 | tf_op jit(solution)/shard_map/basis_gather/ppermute | solution.py:231
  134.7 4.5 %collective-permute-start.5 = (f32[8,16,128]{2,1,0:T(8,128)S(1)}, f32[8,16,128]{2,1,0:T(8,128)S(1)}, u32[]{:S(2)}, u32[]{:S(2)}) collective-permute-start(f32[8,16,128]{2,1,0:T(8,128)S(1)} %get-tuple-element.33.first), channel_id=1, source_target_pairs={{2,0},{3,1},{0,2},{1,3},{6,4},{7,5},{4,6},{5,7},{10,8},{11,9},{8,1... | collective-permute-start | bytes 196616 | tf_op jit(solution)/shard_map/basis_gather/ppermute | solution.py:231
  139.2 2.5 %collective-permute-start.4 = (f32[8,16,128]{2,1,0:T(8,128)S(1)}, f32[8,16,128]{2,1,0:T(8,128)S(1)}, u32[]{:S(2)}, u32[]{:S(2)}) collective-permute-start(f32[8,16,128]{2,1,0:T(8,128)S(1)} %get-tuple-element.33.first), channel_id=1, source_target_pairs={{1,0},{2,1},{3,2},{0,3},{5,4},{6,5},{7,6},{4,7},{9,8},{10,9},{11,1... | collective-permute-start | bytes 196616 | tf_op jit(solution)/shard_map/basis_gather/ppermute | solution.py:231
  141.7 0.0 collective-permute-done.6.fourth
  141.7 0.0 collective-permute-done.5.third
  141.7 2.6 %collective-permute-done.4.second = f32[8,16,128]{2,1,0:T(8,128)S(1)} collective-permute-done((f32[8,16,128]{2,1,0:T(8,128)S(1)}, f32[8,16,128]{2,1,0:T(8,128)S(1)}, u32[]{:S(2)}, u32[]{:S(2)}) %collective-permute-start.4) | collective-permute-done | bytes 65568 | tf_op jit(solution)/shard_map/basis_gather/ppermute | solution.py:231
  144.3 0.0 all-to-all-done.6.own
  144.3 9.1 %collective-permute-start.7 = (f32[4,256,128]{2,1,0:T(8,128)S(1)}, f32[4,256,128]{2,1,0:T(8,128)S(1)}, u32[]{:S(2)}, u32[]{:S(2)}) collective-permute-start(f32[4,256,128]{2,1,0:T(8,128)S(1)} %all-to-all-done.6.own), channel_id=1, source_target_pairs={{4,0},{0,4},{5,1},{1,5},{6,2},{2,6},{7,3},{3,7},{12,8},{8,12},{13,... | collective-permute-start | bytes 1572872 | tf_op jit(solution)/shard_map/ppermute | solution.py:231
  153.4 1.5 collective-permute-done.7.other
  154.9 0.0 copy-done.3
  154.9 1.5 project.1
  156.4 5.1 %all-to-all-start.7 = ((f32[8,64,256]{2,1,0:T(8,128)}), f32[8,64,256]{2,1,0:T(8,128)S(1)}, u32[]{:S(2)}, u32[]{:S(2)}) async-start(f32[8,64,256]{2,1,0:T(8,128)} %project.1), calls=%async_computation.7 | async-start | bytes 1048576 | tf_op jit(solution)/shard_map/projected_gather/all_to_all | solution.py:325
  161.5 0.0 copy-done.5
  161.5 1.5 step_batch.1
  163.0 7.8 %all-to-all-done.7 = f32[8,64,256]{2,1,0:T(8,128)S(1)} async-done(((f32[8,64,256]{2,1,0:T(8,128)}), f32[8,64,256]{2,1,0:T(8,128)S(1)}, u32[]{:S(2)}, u32[]{:S(2)}) %all-to-all-start.7) | async-done | bytes 524320 | tf_op jit(solution)/shard_map/projected_gather/all_to_all | solution.py:325
  170.8 1.1 correct.1
  (7 shorter events, 0.1 us)
Async XLA Ops:
  0.6 0.7 copy-start.4
  30.0 6.9 %copy-start.1 = (bf16[256,320]{0,1:T(8,128)(2,1)S(1)}, bf16[256,320]{0,1:T(8,128)(2,1)}, u32[]{:S(2)}) copy-start(bf16[256,320]{0,1:T(8,128)(2,1)} %param.8) | copy-start | bytes 491524
  30.0 35.8 %copy-start.2 = (f32[64,512]{1,0:T(8,128)S(1)}, f32[64,512]{1,0:T(8,128)}, u32[]{:S(2)}) copy-start(f32[64,512]{1,0:T(8,128)} %vectors.1) | copy-start | bytes 393220
  30.0 35.8 %copy-start.6 = (f32[512]{0:T(512)S(1)}, f32[512]{0:T(512)}, u32[]{:S(2)}) copy-start(f32[512]{0:T(512)} %param.15) | copy-start | bytes 6148
  30.0 35.8 %copy-start.7 = (s32[64]{0:T(128)S(1)}, s32[64]{0:T(128)}, u32[]{:S(2)}) copy-start(s32[64]{0:T(128)} %param.13) | copy-start | bytes 772
  30.0 38.4 %copy-start = (f32[250,256]{1,0:T(8,128)S(1)}, f32[250,256]{1,0:T(8,128)}, u32[]{:S(2)}) copy-start(f32[250,256]{1,0:T(8,128)} %coefficients.3) | copy-start | bytes 768004
  30.0 31.2 %all-to-all-start.1 = ((bf16[16,40,8,128]{3,2,1,0:T(8,128)(2,1)}), bf16[16,40,8,128]{3,2,1,0:T(8,128)(2,1)S(1)}, u32[]{:S(2)}, u32[]{:S(2)}) async-start(bf16[16,40,8,128]{3,2,1,0:T(8,128)(2,1)} %pack.1), calls=%async_computation.1 | async-start | bytes 2621440 | tf_op jit(solution)/shard_map/batch_xy/all_to_all | solution.py:284
  36.9 17.7 %collective-permute-start.2 = (bf16[320,256]{1,0:T(8,128)(2,1)S(1)}, bf16[320,256]{1,0:T(8,128)(2,1)S(1)}, u32[]{:S(2)}, u32[]{:S(2)}) collective-permute-start(bf16[320,256]{1,0:T(8,128)(2,1)S(1)} %bitcast.15), channel_id=1, source_target_pairs={{3,0},{0,1},{1,2},{2,3},{7,4},{4,5},{5,6},{6,7},{11,8},{8,9},{9,10... | collective-permute-start | bytes 491528 | tf_op jit(solution)/shard_map/centers_gather/ppermute | solution.py:231
  40.2 21.0 %collective-permute-start.1 = (bf16[320,256]{1,0:T(8,128)(2,1)S(1)}, bf16[320,256]{1,0:T(8,128)(2,1)S(1)}, u32[]{:S(2)}, u32[]{:S(2)}) collective-permute-start(bf16[320,256]{1,0:T(8,128)(2,1)S(1)} %bitcast.16), channel_id=1, source_target_pairs={{2,0},{3,1},{0,2},{1,3},{6,4},{7,5},{4,6},{5,7},{10,8},{11,9},{8,1... | collective-permute-start | bytes 491528 | tf_op jit(solution)/shard_map/centers_gather/ppermute | solution.py:231
  44.5 16.7 %collective-permute-start = (bf16[320,256]{1,0:T(8,128)(2,1)S(1)}, bf16[320,256]{1,0:T(8,128)(2,1)S(1)}, u32[]{:S(2)}, u32[]{:S(2)}) collective-permute-start(bf16[320,256]{1,0:T(8,128)(2,1)S(1)} %bitcast.17), channel_id=1, source_target_pairs={{1,0},{2,1},{3,2},{0,3},{5,4},{6,5},{7,6},{4,7},{9,8},{10,9},{11,1... | collective-permute-start | bytes 491528 | tf_op jit(solution)/shard_map/centers_gather/ppermute | solution.py:231
  61.2 7.2 %collective-permute-start.3 = (bf16[4,4,40,8,128]{4,3,2,1,0:T(8,128)(2,1)S(1)}, bf16[4,4,40,8,128]{4,3,2,1,0:T(8,128)(2,1)S(1)}, u32[]{:S(2)}, u32[]{:S(2)}) collective-permute-start(bf16[4,4,40,8,128]{4,3,2,1,0:T(8,128)(2,1)S(1)} %bitcast.11), channel_id=1, source_target_pairs={{4,0},{0,4},{5,1},{1,5},{6,2},{2,6},{7,3},{3,7},{12,8},{8,12},{13,... | collective-permute-start | bytes 3932168 | tf_op jit(solution)/shard_map/ppermute | solution.py:231
  91.5 63.5 %copy-start.3 = (s32[1024]{0:T(1024)S(1)}, s32[1024]{0:T(1024)}, u32[]{:S(2)}) copy-start(s32[1024]{0:T(1024)} %param.11) | copy-start | bytes 12292
  129.3 15.0 %all-to-all-start.6 = ((f32[4,256,128]{2,1,0:T(8,128)}), f32[4,256,128]{2,1,0:T(8,128)S(1)}, u32[]{:S(2)}, u32[]{:S(2)}) async-start(f32[4,256,128]{2,1,0:T(8,128)} %get-tuple-element.28), calls=%async_computation.6 | async-start | bytes 1048576 | tf_op jit(solution)/shard_map/all_to_all | solution.py:317
  132.8 8.9 %collective-permute-start.6 = (f32[8,16,128]{2,1,0:T(8,128)S(1)}, f32[8,16,128]{2,1,0:T(8,128)S(1)}, u32[]{:S(2)}, u32[]{:S(2)}) collective-permute-start(f32[8,16,128]{2,1,0:T(8,128)S(1)} %get-tuple-element.33.first), channel_id=1, source_target_pairs={{3,0},{0,1},{1,2},{2,3},{7,4},{4,5},{5,6},{6,7},{11,8},{8,9},{9,10... | collective-permute-start | bytes 196616 | tf_op jit(solution)/shard_map/basis_gather/ppermute | solution.py:231
  134.7 7.0 %collective-permute-start.5 = (f32[8,16,128]{2,1,0:T(8,128)S(1)}, f32[8,16,128]{2,1,0:T(8,128)S(1)}, u32[]{:S(2)}, u32[]{:S(2)}) collective-permute-start(f32[8,16,128]{2,1,0:T(8,128)S(1)} %get-tuple-element.33.first), channel_id=1, source_target_pairs={{2,0},{3,1},{0,2},{1,3},{6,4},{7,5},{4,6},{5,7},{10,8},{11,9},{8,1... | collective-permute-start | bytes 196616 | tf_op jit(solution)/shard_map/basis_gather/ppermute | solution.py:231
  139.2 5.1 %collective-permute-start.4 = (f32[8,16,128]{2,1,0:T(8,128)S(1)}, f32[8,16,128]{2,1,0:T(8,128)S(1)}, u32[]{:S(2)}, u32[]{:S(2)}) collective-permute-start(f32[8,16,128]{2,1,0:T(8,128)S(1)} %get-tuple-element.33.first), channel_id=1, source_target_pairs={{1,0},{2,1},{3,2},{0,3},{5,4},{6,5},{7,6},{4,7},{9,8},{10,9},{11,1... | collective-permute-start | bytes 196616 | tf_op jit(solution)/shard_map/basis_gather/ppermute | solution.py:231
  144.3 10.6 %collective-permute-start.7 = (f32[4,256,128]{2,1,0:T(8,128)S(1)}, f32[4,256,128]{2,1,0:T(8,128)S(1)}, u32[]{:S(2)}, u32[]{:S(2)}) collective-permute-start(f32[4,256,128]{2,1,0:T(8,128)S(1)} %all-to-all-done.6.own), channel_id=1, source_target_pairs={{4,0},{0,4},{5,1},{1,5},{6,2},{2,6},{7,3},{3,7},{12,8},{8,12},{13,... | collective-permute-start | bytes 1572872 | tf_op jit(solution)/shard_map/ppermute | solution.py:231
  154.9 6.6 %copy-start.5 = (s32[1024]{0:T(1024)S(1)}, s32[1024]{0:T(1024)}, u32[]{:S(2)}) copy-start(s32[1024]{0:T(1024)} %param.12) | copy-start | bytes 12292
  156.4 14.5 %all-to-all-start.7 = ((f32[8,64,256]{2,1,0:T(8,128)}), f32[8,64,256]{2,1,0:T(8,128)S(1)}, u32[]{:S(2)}, u32[]{:S(2)}) async-start(f32[8,64,256]{2,1,0:T(8,128)} %project.1), calls=%async_computation.7 | async-start | bytes 1048576 | tf_op jit(solution)/shard_map/projected_gather/all_to_all | solution.py:325

commit v5 on v4

--- a/solution.py
+++ b/solution.py
@@ -200,9 +200,11 @@
     updated[...] = coefficients[...] - step_rate * total[:classes]
 
 
-def correct(updated, projected, weights, result):
-    classes = updated.shape[0]
-    change = product(in_two(projected[...]), in_two(weights[...]), FIRST)
+def correct(updated, own, other, weights, result):
+    classes, count = updated.shape
+    lines = [block_of(own, other, j) for j in range(2 * own.shape[0])]
+    projected = jnp.concatenate(lines, axis=0)
+    change = product(in_two(projected), in_two(weights[...]), FIRST)
     result[...] = updated[...] + change[:classes]
 
 
@@ -222,6 +224,11 @@
         )(*operands)
 
     return call
+
+
+def from_next(value, axis):
+    size = lax.axis_size(axis)
+    return lax.ppermute(value, axis, [((d + 1) % size, d) for d in range(size)])
 
 
 def from_others(value, axis):
@@ -268,9 +275,13 @@
             0,
             tiled=True,
         )
-    batch_own, turned = lax.optimization_barrier((batch_own, centers.T))
     with jax.named_scope("centers_gather"):
-        center_pieces = from_others(turned, Y)
+        center_pieces = [centers.T, from_next(centers.T, Y)]
+    batch_own, center_pieces = lax.optimization_barrier((batch_own, center_pieces))
+    with jax.named_scope("centers_gather"):
+        for _ in range(groups - 2):
+            center_pieces.append(from_next(center_pieces[-1], Y))
+    center_pieces += center_pieces[:1] * (4 - groups)
     rows, width = batch_features.shape
     granules = (depth * (2 * width // LANES) // 2, rows, LANES)
     copies = kernel(
@@ -319,15 +330,16 @@
     predicted = from_others(predicted, K)[:2]
 
     copies = kernel(
-        project, array(blocks, groups * split, padded), "project", classes=classes
+        project, array(chips, groups * split, padded), "project", classes=classes
     )(*predicted, *basis, labels)
     with jax.named_scope("projected_gather"):
-        projected = lax.all_to_all(copies, (K, X), 0, 0, tiled=True).reshape(vectors, padded)
+        projected = lax.all_to_all(copies, X, 0, 0, tiled=True)
+        projected = from_others(projected, K)[:2]
 
     output, updated = kernel(
         step_batch, (array(classes, batch), array(classes, count)), "step_batch"
     )(*predicted, labels, index, coefficients)
-    result = kernel(correct, array(classes, count), "correct")(updated, projected, weights)
+    result = kernel(correct, array(classes, count), "correct")(updated, *projected, weights)
     return (output, result)
 
 

time: 173 us -> 181 us (1.046)
  starting transfers between devices: 48.7 us -> 67.9 us
  blocking collectives: 83.4 us -> 69.4 us
  waiting for transfers between devices: 27.7 us -> 30.6 us
    ppermute x0 -> x3, waiting for transfers between devices: none -> 19.5 us  [from_next(): return lax.ppermute(value, axis, [((d + 1) % size, d) for d in range(size)])]
    all_to_all x1, blocking collectives: 27.4 us -> 10.2 us  [shards(): projected = lax.all_to_all(copies, X, 0, 0, tiled=True)]
    ppermute x0 -> x3, starting transfers between devices: none -> 14.6 us  [from_next(): return lax.ppermute(value, axis, [((d + 1) % size, d) for d in range(size)])]
    ppermute x8 -> x6, waiting for transfers between devices: 19.9 us -> 6.79 us  [from_others(): lax.ppermute(value, axis, [((d + s) % size, d) for d in range(size)])]
    all_to_all x1, starting transfers between devices: 5.13 us -> 15.7 us  [shards(): lax.all_to_all(kernel(fan, jax.ShapeDtypeStruct((depth, *batch_features.s...]
    ppermute x8 -> x6, starting transfers between devices: 33.2 us -> 27.3 us  [from_others(): lax.ppermute(value, axis, [((d + s) % size, d) for d in range(size)])]
    all_to_all x1, waiting for transfers between devices: 7.82 us -> 4.3 us  [shards(): lax.all_to_all(kernel(fan, jax.ShapeDtypeStruct((depth, *batch_features.s...]
    all_to_all x3, blocking collectives: 36 us -> 39.2 us  [scattered(): return jnp.sum(lax.all_to_all(tiles, axis, 0, 0, tiled=True), axis=0)]
  transfers between devices with their start and end apart: 11 -> 12, of which waited for: 6 -> 7; matrix products, arithmetic and copies ran while one was open for 0% -> 0% of each run, Pallas kernels for 1% -> 1%
where the time goes in v5:
time: 181 us; the launch traced here: 180 us
  blocking collectives  69.4 us (38%)
  starting transfers between devices  67.9 us (38%)
  waiting for transfers between devices  30.6 us (17%)
  Pallas kernels  10.3 us (6%)
    all_to_all x3, blocking collectives, scattered(): return jnp.sum(lax.all_to_all(tiles, axis, 0, 0, tiled=True), axis=0)  39.2 us
    ppermute x6, starting transfers between devices, from_others(): lax.ppermute(value, axis, [((d + s) % size, d) for d in range(size)])  27.3 us
    all_to_all x1, blocking collectives, gathered(): return lax.all_to_all(copies, axis, 0, 0, tiled=True)  20 us
    ppermute x3, waiting for transfers between devices, from_next(): return lax.ppermute(value, axis, [((d + 1) % size, d) for d in range(size)])  19.5 us
    all_to_all x1, starting transfers between devices, shards(): lax.all_to_all(kernel(fan, jax.ShapeDtypeStruct((depth, *batch_features.s...  15.7 us
    ppermute x3, starting transfers between devices, from_next(): return lax.ppermute(value, axis, [((d + 1) % size, d) for d in range(size)])  14.6 us
    pallas_call x8, Pallas kernels, call(): pl.pallas_call(functools.partial(body, **settings), out_shape=outs, in_sp...  10.3 us
    all_to_all x1, blocking collectives, shards(): projected = lax.all_to_all(copies, X, 0, 0, tiled=True)  10.2 us
  transfers between devices with their start and end apart: 12, of which 7 were waited for; matrix products, arithmetic and copies ran while one was open for 0% of the time, Pallas kernels for 1%

profile of v5, /device:TPU:1, one launch (start us, length us, event | category | flops | bytes accessed | tf_op | source)
XLA Modules:
  0.0 180.1 jit_solution(3751076927889828972)
XLA Ops:
  0.6 0.0 copy-start.4
  0.6 0.7 copy-done.4
  1.3 0.6 fan.1
  2.0 15.7 %all-to-all-start = ((bf16[16,8,320]{2,1,0:T(8,128)(2,1)}), bf16[16,8,320]{2,1,0:T(8,128)(2,1)S(1)}, u32[]{:S(2)}, u32[]{:S(2)}) async-start(bf16[16,8,320]{2,1,0:T(8,128)(2,1)} %fan.1), calls=%async_computation | async-start | bytes 196608 | tf_op jit(solution)/shard_map/batch_z/all_to_all | solution.py:266
  17.7 4.6 %collective-permute-start = (bf16[320,256]{1,0:T(8,128)(2,1)}, bf16[320,256]{1,0:T(8,128)(2,1)S(1)}, u32[]{:S(2)}, u32[]{:S(2)}) collective-permute-start(bf16[320,256]{1,0:T(8,128)(2,1)} %bitcast.13), channel_id=1, source_target_pairs={{1,0},{2,1},{3,2},{0,3},{5,4},{6,5},{7,6},{4,7},{9,8},{10,9},{11,1... | collective-permute-start | bytes 491528 | tf_op jit(solution)/shard_map/centers_gather/ppermute | solution.py:231
  22.4 2.9 %collective-permute-done.second = bf16[320,256]{1,0:T(8,128)(2,1)S(1)} collective-permute-done((bf16[320,256]{1,0:T(8,128)(2,1)}, bf16[320,256]{1,0:T(8,128)(2,1)S(1)}, u32[]{:S(2)}, u32[]{:S(2)}) %collective-permute-start) | collective-permute-done | bytes 163872 | tf_op jit(solution)/shard_map/centers_gather/ppermute | solution.py:231
  25.3 4.3 %all-to-all-done.batch = bf16[16,8,320]{2,1,0:T(8,128)(2,1)S(1)} async-done(((bf16[16,8,320]{2,1,0:T(8,128)(2,1)}), bf16[16,8,320]{2,1,0:T(8,128)(2,1)S(1)}, u32[]{:S(2)}, u32[]{:S(2)}) %all-to-all-start) | async-done | bytes 81952 | tf_op jit(solution)/shard_map/batch_z/all_to_all | solution.py:266
  29.6 1.3 pack.1
  30.9 0.0 copy-start.1
  30.9 6.9 %all-to-all-start.1 = ((bf16[16,40,8,128]{3,2,1,0:T(8,128)(2,1)}), bf16[16,40,8,128]{3,2,1,0:T(8,128)(2,1)S(1)}, u32[]{:S(2)}, u32[]{:S(2)}) async-start(bf16[16,40,8,128]{3,2,1,0:T(8,128)(2,1)} %pack.1), calls=%async_computation.1 | async-start | bytes 2621440 | tf_op jit(solution)/shard_map/batch_xy/all_to_all | solution.py:295
  37.8 4.5 %collective-permute-start.1 = (bf16[320,256]{1,0:T(8,128)(2,1)S(1)}, bf16[320,256]{1,0:T(8,128)(2,1)S(1)}, u32[]{:S(2)}, u32[]{:S(2)}) collective-permute-start(bf16[320,256]{1,0:T(8,128)(2,1)S(1)} %collective-permute-done.second), channel_id=1, source_target_pairs={{1,0},{2,1},{3,2},{0,3},{5,4},{6,5},{7,6},{4,7},{9,8},{10,9},{11,1... | collective-permute-start | bytes 491528 | tf_op jit(solution)/shard_map/centers_gather/ppermute | solution.py:231
  42.3 14.4 %collective-permute-done.1.third = bf16[320,256]{1,0:T(8,128)(2,1)S(1)} collective-permute-done((bf16[320,256]{1,0:T(8,128)(2,1)S(1)}, bf16[320,256]{1,0:T(8,128)(2,1)S(1)}, u32[]{:S(2)}, u32[]{:S(2)}) %collective-permute-start.1) | collective-permute-done | bytes 163872 | tf_op jit(solution)/shard_map/centers_gather/ppermute | solution.py:231
  56.7 5.5 %collective-permute-start.2 = (bf16[320,256]{1,0:T(8,128)(2,1)S(1)}, bf16[320,256]{1,0:T(8,128)(2,1)S(1)}, u32[]{:S(2)}, u32[]{:S(2)}) collective-permute-start(bf16[320,256]{1,0:T(8,128)(2,1)S(1)} %collective-permute-done.1.third), channel_id=1, source_target_pairs={{1,0},{2,1},{3,2},{0,3},{5,4},{6,5},{7,6},{4,7},{9,8},{10,9},{11,1... | collective-permute-start | bytes 491528 | tf_op jit(solution)/shard_map/centers_gather/ppermute | solution.py:231
  62.1 2.2 %collective-permute-done.2.fourth = bf16[320,256]{1,0:T(8,128)(2,1)S(1)} collective-permute-done((bf16[320,256]{1,0:T(8,128)(2,1)S(1)}, bf16[320,256]{1,0:T(8,128)(2,1)S(1)}, u32[]{:S(2)}, u32[]{:S(2)}) %collective-permute-start.2) | collective-permute-done | bytes 163872 | tf_op jit(solution)/shard_map/centers_gather/ppermute | solution.py:231
  64.4 0.0 all-to-all-done.1
  64.4 4.0 %collective-permute-start.3 = (bf16[4,4,40,8,128]{4,3,2,1,0:T(8,128)(2,1)S(1)}, bf16[4,4,40,8,128]{4,3,2,1,0:T(8,128)(2,1)S(1)}, u32[]{:S(2)}, u32[]{:S(2)}) collective-permute-start(bf16[4,4,40,8,128]{4,3,2,1,0:T(8,128)(2,1)S(1)} %bitcast.10), channel_id=1, source_target_pairs={{4,0},{0,4},{5,1},{1,5},{6,2},{2,6},{7,3},{3,7},{12,8},{8,12},{13,... | collective-permute-start | bytes 3932168 | tf_op jit(solution)/shard_map/ppermute | solution.py:238
  68.4 0.0 copy-done.2
  68.4 0.0 copy-done.6
  68.4 0.0 copy-done.7
  68.4 0.4 lift.1
  68.8 2.2 %collective-permute-done.3.other = bf16[4,4,40,8,128]{4,3,2,1,0:T(8,128)(2,1)S(1)} collective-permute-done((bf16[4,4,40,8,128]{4,3,2,1,0:T(8,128)(2,1)S(1)}, bf16[4,4,40,8,128]{4,3,2,1,0:T(8,128)(2,1)S(1)}, u32[]{:S(2)}, u32[]{:S(2)}) %collective-permute-start.3) | collective-permute-done | bytes 1310752 | tf_op jit(solution)/shard_map/ppermute | solution.py:238
  71.1 0.0 copy-done.1
  71.1 3.8 %kernel_products.1 = f32[8,384,128]{2,1,0:T(8,128)S(1)} custom-call(bf16[4,4,40,8,128]{4,3,2,1,0:T(8,128)(2,1)S(1)} %bitcast.11, bf16[4,4,40,8,128]{4,3,2,1,0:T(8,128)(2,1)S(1)} %collective-permute-done.3.other, bf16[320,256]{1,0:T(8,128)(2,1)S(1)} %bitcast.14, bf16[320,256]{1,0:T(8,128)(2,1)S(1)} %collective-permute-done.second, ...), custom_call_target="tpu_custom_call" | custom-call | tf_op jit(solution)/shard_map/kernel_products/pallas_call | solution.py:215
  74.9 5.0 %all_to_all.40 = f32[2,4,384,128]{3,2,1,0:T(8,128)S(1)} all-to-all(f32[2,4,384,128]{3,2,1,0:T(8,128)S(1)} %bitcast.9), channel_id=1, replica_groups=mesh['rows_z'=16,'rows_x'=4,'rows_k'=2,'cls'=4] {'rows_k'}, dimensions={0} | all-to-all | bytes 3145728 | tf_op jit(solution)/shard_map/all_to_all | solution.py:30
  79.9 0.2 reduce_sum.27
  80.0 14.8 %all_to_all.41 = f32[4,384,128]{2,1,0:T(8,128)S(1)} all-to-all(f32[4,384,128]{2,1,0:T(8,128)S(1)} %reduce_sum.27), channel_id=1, replica_groups=mesh['rows_z'=16,'rows_x'=4,'rows_k'=2,'cls'=4] {'rows_x'}, dimensions={0} | all-to-all | bytes 1572864 | tf_op jit(solution)/shard_map/all_to_all | solution.py:30
  94.9 0.0 copy-start.3
  94.9 19.4 %all_to_all.42 = f32[16,24,128]{2,1,0:T(8,128)S(1)} all-to-all(f32[16,24,128]{2,1,0:T(8,128)S(1)} %bitcast.20), channel_id=1, replica_groups=mesh['rows_z'=16,'rows_x'=4,'rows_k'=2,'cls'=4] {'rows_z'}, dimensions={0} | all-to-all | bytes 393216 | tf_op jit(solution)/shard_map/all_to_all | solution.py:30
  114.4 20.0 %all_to_all.43 = f32[16,24,128]{2,1,0:T(8,128)S(1)} all-to-all(f32[16,24,128]{2,1,0:T(8,128)S(1)} %broadcast_in_dim.11), channel_id=1, replica_groups=mesh['rows_z'=16,'rows_x'=4,'rows_k'=2,'cls'=4] {'rows_z'}, dimensions={0} | all-to-all | bytes 393216 | tf_op jit(solution)/shard_map/all_to_all | solution.py:26
  134.4 0.8 part.1
  135.2 3.5 %all-to-all-start.6 = ((f32[4,256,128]{2,1,0:T(8,128)}), f32[4,256,128]{2,1,0:T(8,128)S(1)}, u32[]{:S(2)}, u32[]{:S(2)}) async-start(f32[4,256,128]{2,1,0:T(8,128)} %get-tuple-element.30), calls=%async_computation.6 | async-start | bytes 1048576 | tf_op jit(solution)/shard_map/all_to_all | solution.py:328
  138.7 0.0 copy-start.5
  138.7 2.7 %collective-permute-start.6 = (f32[8,16,128]{2,1,0:T(8,128)S(1)}, f32[8,16,128]{2,1,0:T(8,128)S(1)}, u32[]{:S(2)}, u32[]{:S(2)}) collective-permute-start(f32[8,16,128]{2,1,0:T(8,128)S(1)} %get-tuple-element.35.first), channel_id=1, source_target_pairs={{3,0},{0,1},{1,2},{2,3},{7,4},{4,5},{5,6},{6,7},{11,8},{8,9},{9,10... | collective-permute-start | bytes 196616 | tf_op jit(solution)/shard_map/basis_gather/ppermute | solution.py:238
  141.4 5.7 %collective-permute-start.5 = (f32[8,16,128]{2,1,0:T(8,128)S(1)}, f32[8,16,128]{2,1,0:T(8,128)S(1)}, u32[]{:S(2)}, u32[]{:S(2)}) collective-permute-start(f32[8,16,128]{2,1,0:T(8,128)S(1)} %get-tuple-element.35.first), channel_id=1, source_target_pairs={{2,0},{3,1},{0,2},{1,3},{6,4},{7,5},{4,6},{5,7},{10,8},{11,9},{8,1... | collective-permute-start | bytes 196616 | tf_op jit(solution)/shard_map/basis_gather/ppermute | solution.py:238
  147.1 1.9 %collective-permute-start.4 = (f32[8,16,128]{2,1,0:T(8,128)S(1)}, f32[8,16,128]{2,1,0:T(8,128)S(1)}, u32[]{:S(2)}, u32[]{:S(2)}) collective-permute-start(f32[8,16,128]{2,1,0:T(8,128)S(1)} %get-tuple-element.35.first), channel_id=1, source_target_pairs={{1,0},{2,1},{3,2},{0,3},{5,4},{6,5},{7,6},{4,7},{9,8},{10,9},{11,1... | collective-permute-start | bytes 196616 | tf_op jit(solution)/shard_map/basis_gather/ppermute | solution.py:238
  149.1 0.0 collective-permute-done.6.fourth
  149.1 0.0 collective-permute-done.5.third
  149.1 3.1 %collective-permute-done.4.second = f32[8,16,128]{2,1,0:T(8,128)S(1)} collective-permute-done((f32[8,16,128]{2,1,0:T(8,128)S(1)}, f32[8,16,128]{2,1,0:T(8,128)S(1)}, u32[]{:S(2)}, u32[]{:S(2)}) %collective-permute-start.4) | collective-permute-done | bytes 65568 | tf_op jit(solution)/shard_map/basis_gather/ppermute | solution.py:238
  152.1 0.0 all-to-all-done.6.own
  152.1 9.2 %collective-permute-start.7 = (f32[4,256,128]{2,1,0:T(8,128)S(1)}, f32[4,256,128]{2,1,0:T(8,128)S(1)}, u32[]{:S(2)}, u32[]{:S(2)}) collective-permute-start(f32[4,256,128]{2,1,0:T(8,128)S(1)} %all-to-all-done.6.own), channel_id=1, source_target_pairs={{4,0},{0,4},{5,1},{1,5},{6,2},{2,6},{7,3},{3,7},{12,8},{8,12},{13,... | collective-permute-start | bytes 1572872 | tf_op jit(solution)/shard_map/ppermute | solution.py:238
  161.3 1.5 collective-permute-done.7.other
  162.8 0.6 project.1
  163.5 10.2 %all_to_all.44.own = f32[4,64,256]{2,1,0:T(8,128)S(1)} all-to-all(f32[4,64,256]{2,1,0:T(8,128)S(1)} %project.1), channel_id=1, replica_groups=mesh['rows_z'=16,'rows_x'=4,'rows_k'=2,'cls'=4] {'rows_x'}, dimensions={0} | all-to-all | bytes 524288 | tf_op jit(solution)/shard_map/projected_gather/all_to_all | solution.py:336
  173.7 3.7 %collective-permute-start.8 = (f32[4,64,256]{2,1,0:T(8,128)S(1)}, f32[4,64,256]{2,1,0:T(8,128)S(1)}, u32[]{:S(2)}, u32[]{:S(2)}) collective-permute-start(f32[4,64,256]{2,1,0:T(8,128)S(1)} %all_to_all.44.own), channel_id=1, source_target_pairs={{4,0},{0,4},{5,1},{1,5},{6,2},{2,6},{7,3},{3,7},{12,8},{8,12},{13,... | collective-permute-start | bytes 786440 | tf_op jit(solution)/shard_map/projected_gather/ppermute | solution.py:238
  177.4 0.0 copy-done.5
  177.4 1.5 step_batch.1
  179.0 0.0 collective-permute-done.8.other
  179.0 1.1 correct.1
  (9 shorter events, 0.1 us)
Async XLA Ops:
  0.6 0.7 copy-start.4
  2.0 27.6 %all-to-all-start = ((bf16[16,8,320]{2,1,0:T(8,128)(2,1)}), bf16[16,8,320]{2,1,0:T(8,128)(2,1)S(1)}, u32[]{:S(2)}, u32[]{:S(2)}) async-start(bf16[16,8,320]{2,1,0:T(8,128)(2,1)} %fan.1), calls=%async_computation | async-start | bytes 196608 | tf_op jit(solution)/shard_map/batch_z/all_to_all | solution.py:266
  17.7 7.5 %collective-permute-start = (bf16[320,256]{1,0:T(8,128)(2,1)}, bf16[320,256]{1,0:T(8,128)(2,1)S(1)}, u32[]{:S(2)}, u32[]{:S(2)}) collective-permute-start(bf16[320,256]{1,0:T(8,128)(2,1)} %bitcast.13), channel_id=1, source_target_pairs={{1,0},{2,1},{3,2},{0,3},{5,4},{6,5},{7,6},{4,7},{9,8},{10,9},{11,1... | collective-permute-start | bytes 491528 | tf_op jit(solution)/shard_map/centers_gather/ppermute | solution.py:231
  30.8 37.6 %copy-start.2 = (f32[64,512]{1,0:T(8,128)S(1)}, f32[64,512]{1,0:T(8,128)}, u32[]{:S(2)}) copy-start(f32[64,512]{1,0:T(8,128)} %vectors.1) | copy-start | bytes 393220
  30.9 37.6 %copy-start.6 = (f32[512]{0:T(512)S(1)}, f32[512]{0:T(512)}, u32[]{:S(2)}) copy-start(f32[512]{0:T(512)} %param.15) | copy-start | bytes 6148
  30.9 37.6 %copy-start.7 = (s32[64]{0:T(128)S(1)}, s32[64]{0:T(128)}, u32[]{:S(2)}) copy-start(s32[64]{0:T(128)} %param.13) | copy-start | bytes 772
  30.9 40.2 %copy-start = (f32[250,256]{1,0:T(8,128)S(1)}, f32[250,256]{1,0:T(8,128)}, u32[]{:S(2)}) copy-start(f32[250,256]{1,0:T(8,128)} %coefficients.3) | copy-start | bytes 768004
  30.9 40.2 %copy-start.1 = (bf16[256,320]{0,1:T(8,128)(2,1)S(1)}, bf16[256,320]{0,1:T(8,128)(2,1)}, u32[]{:S(2)}) copy-start(bf16[256,320]{0,1:T(8,128)(2,1)} %param.8) | copy-start | bytes 491524
  30.9 33.5 %all-to-all-start.1 = ((bf16[16,40,8,128]{3,2,1,0:T(8,128)(2,1)}), bf16[16,40,8,128]{3,2,1,0:T(8,128)(2,1)S(1)}, u32[]{:S(2)}, u32[]{:S(2)}) async-start(bf16[16,40,8,128]{3,2,1,0:T(8,128)(2,1)} %pack.1), calls=%async_computation.1 | async-start | bytes 2621440 | tf_op jit(solution)/shard_map/batch_xy/all_to_all | solution.py:295
  37.8 18.9 %collective-permute-start.1 = (bf16[320,256]{1,0:T(8,128)(2,1)S(1)}, bf16[320,256]{1,0:T(8,128)(2,1)S(1)}, u32[]{:S(2)}, u32[]{:S(2)}) collective-permute-start(bf16[320,256]{1,0:T(8,128)(2,1)S(1)} %collective-permute-done.second), channel_id=1, source_target_pairs={{1,0},{2,1},{3,2},{0,3},{5,4},{6,5},{7,6},{4,7},{9,8},{10,9},{11,1... | collective-permute-start | bytes 491528 | tf_op jit(solution)/shard_map/centers_gather/ppermute | solution.py:231
  56.7 7.7 %collective-permute-start.2 = (bf16[320,256]{1,0:T(8,128)(2,1)S(1)}, bf16[320,256]{1,0:T(8,128)(2,1)S(1)}, u32[]{:S(2)}, u32[]{:S(2)}) collective-permute-start(bf16[320,256]{1,0:T(8,128)(2,1)S(1)} %collective-permute-done.1.third), channel_id=1, source_target_pairs={{1,0},{2,1},{3,2},{0,3},{5,4},{6,5},{7,6},{4,7},{9,8},{10,9},{11,1... | collective-permute-start | bytes 491528 | tf_op jit(solution)/shard_map/centers_gather/ppermute | solution.py:231
  64.4 6.7 %collective-permute-start.3 = (bf16[4,4,40,8,128]{4,3,2,1,0:T(8,128)(2,1)S(1)}, bf16[4,4,40,8,128]{4,3,2,1,0:T(8,128)(2,1)S(1)}, u32[]{:S(2)}, u32[]{:S(2)}) collective-permute-start(bf16[4,4,40,8,128]{4,3,2,1,0:T(8,128)(2,1)S(1)} %bitcast.10), channel_id=1, source_target_pairs={{4,0},{0,4},{5,1},{1,5},{6,2},{2,6},{7,3},{3,7},{12,8},{8,12},{13,... | collective-permute-start | bytes 3932168 | tf_op jit(solution)/shard_map/ppermute | solution.py:238
  94.9 67.9 %copy-start.3 = (s32[1024]{0:T(1024)S(1)}, s32[1024]{0:T(1024)}, u32[]{:S(2)}) copy-start(s32[1024]{0:T(1024)} %param.11) | copy-start | bytes 12292
  135.2 16.9 %all-to-all-start.6 = ((f32[4,256,128]{2,1,0:T(8,128)}), f32[4,256,128]{2,1,0:T(8,128)S(1)}, u32[]{:S(2)}, u32[]{:S(2)}) async-start(f32[4,256,128]{2,1,0:T(8,128)} %get-tuple-element.30), calls=%async_computation.6 | async-start | bytes 1048576 | tf_op jit(solution)/shard_map/all_to_all | solution.py:328
  138.7 38.7 %copy-start.5 = (s32[1024]{0:T(1024)S(1)}, s32[1024]{0:T(1024)}, u32[]{:S(2)}) copy-start(s32[1024]{0:T(1024)} %param.12) | copy-start | bytes 12292
  138.7 10.4 %collective-permute-start.6 = (f32[8,16,128]{2,1,0:T(8,128)S(1)}, f32[8,16,128]{2,1,0:T(8,128)S(1)}, u32[]{:S(2)}, u32[]{:S(2)}) collective-permute-start(f32[8,16,128]{2,1,0:T(8,128)S(1)} %get-tuple-element.35.first), channel_id=1, source_target_pairs={{3,0},{0,1},{1,2},{2,3},{7,4},{4,5},{5,6},{6,7},{11,8},{8,9},{9,10... | collective-permute-start | bytes 196616 | tf_op jit(solution)/shard_map/basis_gather/ppermute | solution.py:238
  141.4 7.7 %collective-permute-start.5 = (f32[8,16,128]{2,1,0:T(8,128)S(1)}, f32[8,16,128]{2,1,0:T(8,128)S(1)}, u32[]{:S(2)}, u32[]{:S(2)}) collective-permute-start(f32[8,16,128]{2,1,0:T(8,128)S(1)} %get-tuple-element.35.first), channel_id=1, source_target_pairs={{2,0},{3,1},{0,2},{1,3},{6,4},{7,5},{4,6},{5,7},{10,8},{11,9},{8,1... | collective-permute-start | bytes 196616 | tf_op jit(solution)/shard_map/basis_gather/ppermute | solution.py:238
  147.1 5.0 %collective-permute-start.4 = (f32[8,16,128]{2,1,0:T(8,128)S(1)}, f32[8,16,128]{2,1,0:T(8,128)S(1)}, u32[]{:S(2)}, u32[]{:S(2)}) collective-permute-start(f32[8,16,128]{2,1,0:T(8,128)S(1)} %get-tuple-element.35.first), channel_id=1, source_target_pairs={{1,0},{2,1},{3,2},{0,3},{5,4},{6,5},{7,6},{4,7},{9,8},{10,9},{11,1... | collective-permute-start | bytes 196616 | tf_op jit(solution)/shard_map/basis_gather/ppermute | solution.py:238
  152.1 10.7 %collective-permute-start.7 = (f32[4,256,128]{2,1,0:T(8,128)S(1)}, f32[4,256,128]{2,1,0:T(8,128)S(1)}, u32[]{:S(2)}, u32[]{:S(2)}) collective-permute-start(f32[4,256,128]{2,1,0:T(8,128)S(1)} %all-to-all-done.6.own), channel_id=1, source_target_pairs={{4,0},{0,4},{5,1},{1,5},{6,2},{2,6},{7,3},{3,7},{12,8},{8,12},{13,... | collective-permute-start | bytes 1572872 | tf_op jit(solution)/shard_map/ppermute | solution.py:238
  173.7 5.3 %collective-permute-start.8 = (f32[4,64,256]{2,1,0:T(8,128)S(1)}, f32[4,64,256]{2,1,0:T(8,128)S(1)}, u32[]{:S(2)}, u32[]{:S(2)}) collective-permute-start(f32[4,64,256]{2,1,0:T(8,128)S(1)} %all_to_all.44.own), channel_id=1, source_target_pairs={{4,0},{0,4},{5,1},{1,5},{6,2},{2,6},{7,3},{3,7},{12,8},{8,12},{13,... | collective-permute-start | bytes 786440 | tf_op jit(solution)/shard_map/projected_gather/ppermute | solution.py:238

commit v6 on v4

--- a/solution.py
+++ b/solution.py
@@ -66,20 +66,16 @@
     copies[...] = jnp.broadcast_to(granules[...][None], copies.shape)
 
 
-def kernel_products(
-    own, other, first, second, third, fourth, coefficients, basis, sums, stacked
-):
-    chips, groups, granules, rows, lanes = own.shape
+def kernel_products(batch, first, second, third, fourth, high, low, sums, *, padded):
+    chips, groups, granules, rows, lanes = batch.shape
     blocks, lines, _ = sums.shape
-    classes, count = coefficients.shape
+    count = high.shape[1]
     full, rest = first.shape[0] // lanes, first.shape[0] % lanes
     depth = 2 * granules // (2 * full + 1)
     half = depth // 2
-    split = basis.shape[2]
-    padded = lines - blocks * split
     near = depth // blocks
+    split = (lines - padded) // blocks
     centers = (first, second, third, fourth)[:groups]
-    is_low = lax.axis_index(K) == 0
 
     center_norm = jnp.zeros((1, count), jnp.float32)
     tails = []
@@ -90,10 +86,6 @@
     none = jnp.zeros((rest, count), tails[0].dtype)
     low_tail = jnp.concatenate([v for t in tails for v in (t, none)], axis=0)
     high_tail = jnp.concatenate([v for t in tails for v in (none, t)], axis=0)
-    stacked[padded - 8 : padded, :] = jnp.zeros((8, count), jnp.float32)
-    stacked[:classes, :] = coefficients[...]
-    stacked[padded:, :] = basis[:, pl.ds(lax.axis_index(Y), 1)].reshape(-1, count)
-    weights = in_two(stacked[...])
     lane = lax.broadcasted_iota(jnp.int32, (2 * lanes, lanes), 1)
 
     for t in range(0, blocks, 2):
@@ -109,9 +101,7 @@
                 pieces = []
                 for z in range(t * near, (t + 2) * near):
                     at = z * full + h if h < full else depth * full + z % half
-                    for x in range(chips):
-                        a, b = own[x, y, at], other[x, y, at]
-                        pieces += [jnp.where(is_low, a, b), jnp.where(is_low, b, a)]
+                    pieces += [batch[x, y, at] for x in range(chips)]
                 columns.append(jnp.concatenate(pieces, axis=0))
                 wide = columns[h].astype(jnp.float32)
                 wide = wide if h < full else jnp.where(is_own, wide, 0.0)
@@ -129,7 +119,7 @@
         )
         squared = center_norm + batch_norm - 2.0 * inner
         values = jnp.exp(-jnp.sqrt(jnp.maximum(squared, 0.0)) / spread)
-        out = product(weights, in_two(values), LAST)
+        out = product((high[...], low[...]), in_two(values), LAST)
         for j in range(2):
             part = out[:, j * lanes : (j + 1) * lanes]
             sums[t + j, :padded, :] = part[:padded]
@@ -137,39 +127,61 @@
             sums[:, at : at + split, :] = part[padded:].reshape(blocks, split, lanes)
 
 
-def lift(vectors, scale, index, lifted, weights):
-    count = weights.shape[1]
-    slots = lax.broadcasted_iota(jnp.int32, (count, index.shape[1]), 0) + lax.axis_index(ROWS) * count
-    hits = (index[...] == slots).astype(jnp.bfloat16)
+def lift(vectors, scale, index, coefficients, high, low, weights, stacked):
+    classes, count = coefficients.shape
+    lines, groups = stacked.shape[0], lax.axis_size(Y)
+    own = weights.shape[0] // groups
+    padded = lines - own
+    split = own // lax.axis_size(X)
+    slots = lax.broadcasted_iota(jnp.int32, (count, index.shape[1]), 0)
+    hits = index[...] == slots + lax.axis_index(ROWS) * count
+    hits = hits.astype(jnp.float32).astype(jnp.bfloat16)
     turned = vectors[...].T
     total = jnp.zeros(weights.shape, jnp.float32)
     for part in in_two(turned):
         total += lax.dot_general(part, hits, LAST, preferred_element_type=jnp.float32)
-    lifted[...] = total.reshape(lifted.shape)
     column = jnp.broadcast_to(scale[...], (8, scale.shape[1])).T[:, :1]
+    stacked[padded - 8 : padded, :] = jnp.zeros((8, count), jnp.float32)
+    stacked[:classes, :] = coefficients[...]
+    weights[...] = total
+    for x in range(lax.axis_size(X)):
+        at = pl.multiple_of((x * groups + lax.axis_index(Y)) * split, split)
+        stacked[padded + x * split : padded + (x + 1) * split, :] = weights[pl.ds(at, split), :]
+    high[...], low[...] = in_two(stacked[...])
     weights[...] = total * (step_rate * column)
 
 
-def block_of(own, other, j):
-    core, chip = j // own.shape[0], j % own.shape[0]
-    return jnp.where(lax.axis_index(K) == core, own[chip], other[chip])
-
-
-def gradient_of(own, other, labels, j, classes):
-    rows, lanes = own.shape[1:]
-    ids = lax.broadcasted_iota(jnp.int32, (rows, lanes), 0) + lax.axis_index(Y) * classes
-    return block_of(own, other, j) - (labels[j] == ids).astype(jnp.float32)
-
-
-def project(own, other, first, second, third, fourth, labels, projected, *, classes):
+def add(own, other, total):
+    total[...] = own[...] + other[...]
+
+
+def join(own, other, copies):
+    copies[...] = jnp.broadcast_to((own[...] + other[...])[None], copies.shape)
+
+
+def targets_of(labels, j, rows, classes):
+    ids = lax.broadcasted_iota(jnp.int32, (rows, 2 * LANES), 0) + lax.axis_index(Y) * classes
+    return (labels[j] == ids).astype(jnp.float32)
+
+
+def project(own, first, second, third, fourth, labels, projected, *, classes, rows_each):
     blocks, split, lanes = first.shape
-    groups = projected.shape[1] // split
+    rows = own.shape[1]
+    groups = projected.shape[0] // split
     pieces = (first, second, third, fourth)[:groups]
-    total = jnp.zeros(projected.shape[1:], jnp.float32)
+    side = 1 - lax.axis_index(K)
+    spot = lax.broadcasted_iota(jnp.int32, (lanes, 2 * lanes), 0)
+    lane = lax.broadcasted_iota(jnp.int32, (lanes, 2 * lanes), 1)
+    line = spot // rows_each * (2 * rows_each) + side * rows_each + spot % rows_each
+    picks = (lane == line).astype(jnp.float32).astype(jnp.bfloat16)
+    total = jnp.zeros(projected.shape, jnp.float32)
     for t in range(0, blocks, 2):
-        pair = (t, t + 1)
-        lines = [jnp.concatenate([p[j] for j in pair], axis=1) for p in pieces]
-        gradient = [gradient_of(own, other, labels, j, classes) for j in pair]
+        lines = [jnp.concatenate([p[t], p[t + 1]], axis=1) for p in pieces]
+        gradient = []
+        for j in (t, t + 1):
+            targets = targets_of(labels, j, rows, classes).astype(jnp.bfloat16)
+            hits = lax.dot_general(targets, picks, LAST, preferred_element_type=jnp.float32)
+            gradient.append(own[j] - hits)
         total += product(
             in_two(jnp.concatenate(lines, axis=0)),
             in_two(jnp.concatenate(gradient, axis=1)),
@@ -177,26 +189,32 @@
         )
     for s in range(groups):
         at = pl.multiple_of(lax.rem(lax.axis_index(Y) + s, groups) * split, split)
-        part = total[s * split : (s + 1) * split]
-        projected[:, pl.ds(at, split), :] = jnp.broadcast_to(
-            part[None], (projected.shape[0], *part.shape)
-        )
-
-
-def step_batch(own, other, labels, index, coefficients, output, updated):
-    chips, rows, lanes = own.shape
+        projected[pl.ds(at, split), :] = total[s * split : (s + 1) * split]
+
+
+def step_batch(own, other, labels, index, coefficients, output, updated, *, rows_each):
+    blocks, rows, lanes = own.shape
     classes, count = coefficients.shape
     total = jnp.zeros((rows, count), jnp.float32)
-    slots = lax.broadcasted_iota(jnp.int32, (count, lanes), 0) + lax.axis_index(ROWS) * count
-    for t in range(0, 2 * chips, 2):
-        pair = (t, t + 1)
-        gradient = [gradient_of(own, other, labels, j, classes) for j in pair]
-        hits = [(index[j] == slots).astype(jnp.float32) for j in pair]
-        spots = jnp.concatenate(hits, axis=1).astype(jnp.bfloat16)
-        for part in in_two(jnp.concatenate(gradient, axis=1)):
-            total += lax.dot_general(part, spots, LAST, preferred_element_type=jnp.float32)
-        for j in pair:
-            output[:, j * lanes : (j + 1) * lanes] = block_of(own, other, j)[:classes]
+    slots = lax.broadcasted_iota(jnp.int32, (count, 2 * lanes), 0)
+    slots += lax.axis_index(ROWS) * count
+    spot = lax.broadcasted_iota(jnp.int32, (2 * lanes, 2 * lanes), 0)
+    lane = lax.broadcasted_iota(jnp.int32, (2 * lanes, 2 * lanes), 1)
+    core = jnp.where(spot < lanes, 1 - lax.axis_index(K), lax.axis_index(K))
+    place = spot % lanes
+    line = place // rows_each * (2 * rows_each) + core * rows_each + place % rows_each
+    picks = (lane == line).astype(jnp.float32).astype(jnp.bfloat16)
+    for j in range(blocks):
+        rest = jnp.concatenate([own[j], other[j]], axis=1)
+        predicted = jnp.zeros((rows, 2 * lanes), jnp.float32)
+        for _ in range(3):
+            part = rest.astype(jnp.bfloat16)
+            predicted += jnp.dot(part, picks, preferred_element_type=jnp.float32)
+            rest = rest - part.astype(jnp.float32)
+        output[:, 2 * j * lanes : 2 * (j + 1) * lanes] = predicted[:classes]
+        hits = (index[j] == slots).astype(jnp.float32).astype(jnp.bfloat16)
+        for part in in_two(predicted - targets_of(labels, j, rows, classes)):
+            total += lax.dot_general(part, hits, LAST, preferred_element_type=jnp.float32)
     updated[...] = coefficients[...] - step_rate * total[:classes]
 
 
@@ -242,17 +260,16 @@
     eigen_vectors,
     eigen_scale,
 ):
-    depth, chips, cores, groups = (lax.axis_size(a) for a in (Z, X, K, Y))
-    blocks = chips * cores
+    depth, chips, groups = (lax.axis_size(a) for a in (Z, X, Y))
     count = centers.shape[0]
     classes = coefficients.shape[0]
     vectors = eigen_vectors.shape[1]
-    split = vectors // groups // blocks
+    split = vectors // groups // chips
     padded = -(-classes // 8) * 8
     while (padded + vectors // groups) % (8 * depth):
         padded += 8
     lines = padded + vectors // groups
-    batch = blocks * LANES
+    batch = batch_labels.shape[0]
     array = lambda *shape: jax.ShapeDtypeStruct(shape, jnp.float32)
 
     with jax.named_scope("batch_z"):
@@ -286,47 +303,54 @@
     batch_own = batch_own.reshape(chips, groups, *granules)
     batch_other = from_others(batch_own, K)[1]
 
-    lifted, weights = kernel(
-        lift, (array(blocks, groups, split, count), array(vectors, count)), "lift", limit=4
-    )(eigen_vectors, eigen_scale[None], subset_index[None])
-    labels = batch_labels.reshape(blocks, 1, LANES)
-    index = batch_index.reshape(blocks, 1, LANES)
-
-    sums = kernel(
-        kernel_products,
-        array(blocks, lines, LANES),
-        "kernel_products",
+    high, low, weights = kernel(
+        lift,
+        (
+            jax.ShapeDtypeStruct((lines, count), jnp.bfloat16),
+            jax.ShapeDtypeStruct((lines, count), jnp.bfloat16),
+            array(vectors, count),
+        ),
+        "lift",
         (pltpu.VMEM((lines, count), jnp.float32),),
-    )(
-        batch_own,
-        batch_other,
-        *center_pieces,
-        coefficients,
-        lifted,
+        limit=6,
+    )(eigen_vectors, eigen_scale[None], subset_index[None], coefficients)
+    labels = batch_labels.reshape(chips, 1, 2 * LANES)
+    index = batch_index.reshape(chips, 1, 2 * LANES)
+
+    products = kernel(
+        kernel_products, array(chips, lines, LANES), "kernel_products", limit=12, padded=padded
     )
-
-    own = scattered(sums.reshape(cores, chips, lines, LANES), K)
+    sent = from_others(products(batch_own, *center_pieces, high, low), K)[1]
+    kept = products(batch_other, *center_pieces, high, low)
+    own = kernel(add, array(chips, lines, LANES), "add", limit=6)(kept, sent)
+
     own = scattered(own, X)
     own = scattered(own.reshape(depth, lines // depth, LANES), Z)
     own = gathered(own, Z).reshape(lines, LANES)
     copies, basis = kernel(
-        part, (array(chips, padded, LANES), array(blocks, split, LANES)), "part", limit=4
+        part, (array(chips, padded, LANES), array(chips, split, LANES)), "part", limit=4
     )(own)
     with jax.named_scope("basis_gather"):
         basis = from_others(basis, Y)
     predicted = lax.all_to_all(copies, X, 0, 0, tiled=True)
     predicted, basis = lax.optimization_barrier((predicted, basis))
-    predicted = from_others(predicted, K)[:2]
-
-    copies = kernel(
-        project, array(blocks, groups * split, padded), "project", classes=classes
-    )(*predicted, *basis, labels)
+
+    half = kernel(
+        project, array(groups * split, padded), "project", classes=classes, rows_each=rows
+    )(predicted, *basis, labels)
+    copies = kernel(join, array(chips, groups * split, padded), "join", limit=4)(
+        *from_others(half, K)[:2]
+    )
+    copies, late = lax.optimization_barrier((copies, predicted))
     with jax.named_scope("projected_gather"):
-        projected = lax.all_to_all(copies, (K, X), 0, 0, tiled=True).reshape(vectors, padded)
+        projected = lax.all_to_all(copies, X, 0, 0, tiled=True).reshape(vectors, padded)
 
     output, updated = kernel(
-        step_batch, (array(classes, batch), array(classes, count)), "step_batch"
-    )(*predicted, labels, index, coefficients)
+        step_batch,
+        (array(classes, batch), array(classes, count)),
+        "step_batch",
+        rows_each=rows,
+    )(*from_others(late, K)[:2], labels, index, coefficients)
     result = kernel(correct, array(classes, count), "correct")(updated, projected, weights)
     return (output, result)
 

time: 173 us -> 171 us (0.988)
  blocking collectives: 83.4 us -> 79.2 us
  waiting for transfers between devices: 27.7 us -> 29.8 us
    all_to_all x3 -> x2, blocking collectives: 36 us -> 31.3 us  [scattered(): return jnp.sum(lax.all_to_all(tiles, axis, 0, 0, tiled=True), axis=0)]
    ppermute x8 -> x10, waiting for transfers between devices: 19.9 us -> 22.5 us  [from_others(): lax.ppermute(value, axis, [((d + s) % size, d) for d in range(size)])]
    pallas_call x8 -> x11, Pallas kernels: 10.4 us -> 11.4 us  [call(): pl.pallas_call(functools.partial(body, **settings), out_shape=outs, in_sp...]
    ppermute x8 -> x10, starting transfers between devices: 33.2 us -> 33 us  [from_others(): lax.ppermute(value, axis, [((d + s) % size, d) for d in range(size)])]
  transfers between devices with their start and end apart: 11 -> 13, of which waited for: 6 -> 8; matrix products, arithmetic and copies ran while one was open for 0% -> 0% of each run, Pallas kernels for 1% -> 4%
where the time goes in v6:
time: 171 us; the launch traced here: 170 us
  blocking collectives  79.2 us (46%)
  starting transfers between devices  47.8 us (28%)
  waiting for transfers between devices  29.8 us (17%)
  Pallas kernels  11.4 us (7%)
    ppermute x10, starting transfers between devices, from_others(): lax.ppermute(value, axis, [((d + s) % size, d) for d in range(size)])  33 us
    all_to_all x2, blocking collectives, scattered(): return jnp.sum(lax.all_to_all(tiles, axis, 0, 0, tiled=True), axis=0)  31.3 us
    all_to_all x1, blocking collectives, shards(): lax.all_to_all(kernel(fan, jax.ShapeDtypeStruct((depth, *batch_features.s...  27.4 us
    ppermute x10, waiting for transfers between devices, from_others(): lax.ppermute(value, axis, [((d + s) % size, d) for d in range(size)])  22.5 us
    all_to_all x1, blocking collectives, gathered(): return lax.all_to_all(copies, axis, 0, 0, tiled=True)  20.4 us
    pallas_call x11, Pallas kernels, call(): pl.pallas_call(functools.partial(body, **settings), out_shape=outs, in_sp...  11.4 us
    all_to_all x1, waiting for transfers between devices, shards(): lax.all_to_all(copies, X, 0, 0, tiled=True).reshape(vectors, padded)  7.23 us
    all_to_all x1, starting transfers between devices, shards(): batch_own = lax.all_to_all(copies, (X, Y), 0, 0, tiled=True)  6.9 us
  transfers between devices with their start and end apart: 13, of which 8 were waited for; matrix products, arithmetic and copies ran while one was open for 0% of the time, Pallas kernels for 4%

profile of v6, /device:TPU:1, one launch (start us, length us, event | category | flops | bytes accessed | tf_op | source)
XLA Modules:
  0.0 169.8 jit_solution(4961644675970423478)
XLA Ops:
  0.6 0.0 copy-start.4
  0.6 0.7 copy-done.4
  1.3 27.4 %all_to_all.35.batch = bf16[16,8,320]{2,1,0:T(8,128)(2,1)S(1)} all-to-all(bf16[16,8,320]{2,1,0:T(8,128)(2,1)S(1)} %fan.1), channel_id=1, replica_groups=mesh['rows_z'=16,'rows_x'=4,'rows_k'=2,'cls'=4] {'rows_z'}, dimensions={0} | all-to-all | bytes 163840 | tf_op jit(solution)/shard_map/batch_z/all_to_all | solution.py:276
  28.7 1.3 pack.1
  30.0 0.0 copy-start.7
  30.0 6.9 %all-to-all-start.1 = ((bf16[16,40,8,128]{3,2,1,0:T(8,128)(2,1)}), bf16[16,40,8,128]{3,2,1,0:T(8,128)(2,1)S(1)}, u32[]{:S(2)}, u32[]{:S(2)}) async-start(bf16[16,40,8,128]{3,2,1,0:T(8,128)(2,1)} %pack.1), calls=%async_computation.1 | async-start | bytes 2621440 | tf_op jit(solution)/shard_map/batch_xy/all_to_all | solution.py:301
  36.9 0.0 copy-done.1
  36.9 4.5 %collective-permute-start = (bf16[320,256]{1,0:T(8,128)(2,1)S(1)}, bf16[320,256]{1,0:T(8,128)(2,1)S(1)}, u32[]{:S(2)}, u32[]{:S(2)}) collective-permute-start(bf16[320,256]{1,0:T(8,128)(2,1)S(1)} %bitcast.13), channel_id=1, source_target_pairs={{1,0},{2,1},{3,2},{0,3},{5,4},{6,5},{7,6},{4,7},{9,8},{10,9},{11,1... | collective-permute-start | bytes 491528 | tf_op jit(solution)/shard_map/centers_gather/ppermute | solution.py:249
  41.4 2.5 %collective-permute-start.1 = (bf16[320,256]{1,0:T(8,128)(2,1)S(1)}, bf16[320,256]{1,0:T(8,128)(2,1)S(1)}, u32[]{:S(2)}, u32[]{:S(2)}) collective-permute-start(bf16[320,256]{1,0:T(8,128)(2,1)S(1)} %bitcast.14), channel_id=1, source_target_pairs={{2,0},{3,1},{0,2},{1,3},{6,4},{7,5},{4,6},{5,7},{10,8},{11,9},{8,1... | collective-permute-start | bytes 491528 | tf_op jit(solution)/shard_map/centers_gather/ppermute | solution.py:249
  43.9 2.5 %collective-permute-start.2 = (bf16[320,256]{1,0:T(8,128)(2,1)S(1)}, bf16[320,256]{1,0:T(8,128)(2,1)S(1)}, u32[]{:S(2)}, u32[]{:S(2)}) collective-permute-start(bf16[320,256]{1,0:T(8,128)(2,1)S(1)} %bitcast.15), channel_id=1, source_target_pairs={{3,0},{0,1},{1,2},{2,3},{7,4},{4,5},{5,6},{6,7},{11,8},{8,9},{9,10... | collective-permute-start | bytes 491528 | tf_op jit(solution)/shard_map/centers_gather/ppermute | solution.py:249
  46.4 11.1 %collective-permute-done.second = bf16[320,256]{1,0:T(8,128)(2,1)S(1)} collective-permute-done((bf16[320,256]{1,0:T(8,128)(2,1)S(1)}, bf16[320,256]{1,0:T(8,128)(2,1)S(1)}, u32[]{:S(2)}, u32[]{:S(2)}) %collective-permute-start) | collective-permute-done | bytes 163872 | tf_op jit(solution)/shard_map/centers_gather/ppermute | solution.py:249
  57.6 2.7 %collective-permute-done.1.third = bf16[320,256]{1,0:T(8,128)(2,1)S(1)} collective-permute-done((bf16[320,256]{1,0:T(8,128)(2,1)S(1)}, bf16[320,256]{1,0:T(8,128)(2,1)S(1)}, u32[]{:S(2)}, u32[]{:S(2)}) %collective-permute-start.1) | collective-permute-done | bytes 163872 | tf_op jit(solution)/shard_map/centers_gather/ppermute | solution.py:249
  60.2 2.9 %collective-permute-done.2.fourth = bf16[320,256]{1,0:T(8,128)(2,1)S(1)} collective-permute-done((bf16[320,256]{1,0:T(8,128)(2,1)S(1)}, bf16[320,256]{1,0:T(8,128)(2,1)S(1)}, u32[]{:S(2)}, u32[]{:S(2)}) %collective-permute-start.2) | collective-permute-done | bytes 163872 | tf_op jit(solution)/shard_map/centers_gather/ppermute | solution.py:249
  63.1 0.0 all-to-all-done.1
  63.1 2.4 %collective-permute-start.3 = (bf16[4,4,40,8,128]{4,3,2,1,0:T(8,128)(2,1)S(1)}, bf16[4,4,40,8,128]{4,3,2,1,0:T(8,128)(2,1)S(1)}, u32[]{:S(2)}, u32[]{:S(2)}) collective-permute-start(bf16[4,4,40,8,128]{4,3,2,1,0:T(8,128)(2,1)S(1)} %bitcast.9), channel_id=1, source_target_pairs={{4,0},{0,4},{5,1},{1,5},{6,2},{2,6},{7,3},{3,7},{12,8},{8,12},{13,... | collective-permute-start | bytes 3932168 | tf_op jit(solution)/shard_map/ppermute | solution.py:249
  65.6 0.0 copy-done
  65.6 0.0 copy-done.2
  65.6 0.0 copy-done.6
  65.6 0.5 lift.1
  66.1 2.0 %kernel_products.3 = f32[4,384,128]{2,1,0:T(8,128)S(1)} custom-call(bf16[4,4,40,8,128]{4,3,2,1,0:T(8,128)(2,1)S(1)} %bitcast.10, bf16[320,256]{1,0:T(8,128)(2,1)S(1)} %bitcast.16, bf16[320,256]{1,0:T(8,128)(2,1)S(1)} %collective-permute-done.second, bf16[320,256]{1,0:T(8,128)(2,1)S(1)} %collective-permute-done.1.third, ...), custom_call_target="tpu_custom_call" | custom-call | tf_op jit(solution)/shard_map/kernel_products/pallas_call | solution.py:231
  68.0 1.9 %collective-permute-start.4 = (f32[4,384,128]{2,1,0:T(8,128)S(1)}, f32[4,384,128]{2,1,0:T(8,128)S(1)}, u32[]{:S(2)}, u32[]{:S(2)}) collective-permute-start(f32[4,384,128]{2,1,0:T(8,128)S(1)} %kernel_products.3), channel_id=1, source_target_pairs={{4,0},{0,4},{5,1},{1,5},{6,2},{2,6},{7,3},{3,7},{12,8},{8,12},{13,... | collective-permute-start | bytes 2359304 | tf_op jit(solution)/shard_map/ppermute | solution.py:249
  70.0 0.0 collective-permute-done.3.batch
  70.0 2.0 %kernel_products.2.own = f32[4,384,128]{2,1,0:T(8,128)S(1)} custom-call(bf16[4,4,40,8,128]{4,3,2,1,0:T(8,128)(2,1)S(1)} %collective-permute-done.3.batch, bf16[320,256]{1,0:T(8,128)(2,1)S(1)} %bitcast.17, bf16[320,256]{1,0:T(8,128)(2,1)S(1)} %collective-permute-done.second, bf16[320,256]{1,0:T(8,128)(2,1)S(1)} %collective-permute-done.1.third, ...), custom_call_target="tpu_custom_call" | custom-call | tf_op jit(solution)/shard_map/kernel_products/pallas_call | solution.py:231
  72.0 0.3 collective-permute-done.4.other
  72.2 0.1 add.1
  72.3 14.4 %all_to_all.36 = f32[4,384,128]{2,1,0:T(8,128)S(1)} all-to-all(f32[4,384,128]{2,1,0:T(8,128)S(1)} %add.1), channel_id=1, replica_groups=mesh['rows_z'=16,'rows_x'=4,'rows_k'=2,'cls'=4] {'rows_x'}, dimensions={0} | all-to-all | bytes 1572864 | tf_op jit(solution)/shard_map/all_to_all | solution.py:30
  86.7 0.0 copy-start.3
  86.7 16.9 %all_to_all.37 = f32[16,24,128]{2,1,0:T(8,128)S(1)} all-to-all(f32[16,24,128]{2,1,0:T(8,128)S(1)} %bitcast.23), channel_id=1, replica_groups=mesh['rows_z'=16,'rows_x'=4,'rows_k'=2,'cls'=4] {'rows_z'}, dimensions={0} | all-to-all | bytes 393216 | tf_op jit(solution)/shard_map/all_to_all | solution.py:30
  103.7 20.4 %all_to_all.38 = f32[16,24,128]{2,1,0:T(8,128)S(1)} all-to-all(f32[16,24,128]{2,1,0:T(8,128)S(1)} %broadcast_in_dim.11), channel_id=1, replica_groups=mesh['rows_z'=16,'rows_x'=4,'rows_k'=2,'cls'=4] {'rows_z'}, dimensions={0} | all-to-all | bytes 393216 | tf_op jit(solution)/shard_map/all_to_all | solution.py:26
  124.2 0.8 part.1
  125.0 3.5 %all-to-all-start.5 = ((f32[4,256,128]{2,1,0:T(8,128)}), f32[4,256,128]{2,1,0:T(8,128)S(1)}, u32[]{:S(2)}, u32[]{:S(2)}) async-start(f32[4,256,128]{2,1,0:T(8,128)} %get-tuple-element.32), calls=%async_computation.5 | async-start | bytes 1048576 | tf_op jit(solution)/shard_map/all_to_all | solution.py:335
  128.5 3.3 %collective-permute-start.5 = (f32[4,32,128]{2,1,0:T(8,128)S(1)}, f32[4,32,128]{2,1,0:T(8,128)S(1)}, u32[]{:S(2)}, u32[]{:S(2)}) collective-permute-start(f32[4,32,128]{2,1,0:T(8,128)S(1)} %get-tuple-element.35.first), channel_id=1, source_target_pairs={{1,0},{2,1},{3,2},{0,3},{5,4},{6,5},{7,6},{4,7},{9,8},{10,9},{11,1... | collective-permute-start | bytes 196616 | tf_op jit(solution)/shard_map/basis_gather/ppermute | solution.py:249
  131.8 3.1 %collective-permute-start.6 = (f32[4,32,128]{2,1,0:T(8,128)S(1)}, f32[4,32,128]{2,1,0:T(8,128)S(1)}, u32[]{:S(2)}, u32[]{:S(2)}) collective-permute-start(f32[4,32,128]{2,1,0:T(8,128)S(1)} %get-tuple-element.35.first), channel_id=1, source_target_pairs={{2,0},{3,1},{0,2},{1,3},{6,4},{7,5},{4,6},{5,7},{10,8},{11,9},{8,1... | collective-permute-start | bytes 196616 | tf_op jit(solution)/shard_map/basis_gather/ppermute | solution.py:249
  134.9 1.9 %collective-permute-start.7 = (f32[4,32,128]{2,1,0:T(8,128)S(1)}, f32[4,32,128]{2,1,0:T(8,128)S(1)}, u32[]{:S(2)}, u32[]{:S(2)}) collective-permute-start(f32[4,32,128]{2,1,0:T(8,128)S(1)} %get-tuple-element.35.first), channel_id=1, source_target_pairs={{3,0},{0,1},{1,2},{2,3},{7,4},{4,5},{5,6},{6,7},{11,8},{8,9},{9,10... | collective-permute-start | bytes 196616 | tf_op jit(solution)/shard_map/basis_gather/ppermute | solution.py:249
  136.8 0.0 collective-permute-done.5.second
  136.8 1.5 collective-permute-done.6.third
  138.3 3.1 %collective-permute-done.7.fourth = f32[4,32,128]{2,1,0:T(8,128)S(1)} collective-permute-done((f32[4,32,128]{2,1,0:T(8,128)S(1)}, f32[4,32,128]{2,1,0:T(8,128)S(1)}, u32[]{:S(2)}, u32[]{:S(2)}) %collective-permute-start.7) | collective-permute-done | bytes 65568 | tf_op jit(solution)/shard_map/basis_gather/ppermute | solution.py:249
  141.4 0.0 all-to-all-done.5.own
  141.4 0.9 project.1.own
  142.3 8.6 %collective-permute-start.8 = (f32[128,256]{1,0:T(8,128)S(1)}, f32[128,256]{1,0:T(8,128)S(1)}, u32[]{:S(2)}, u32[]{:S(2)}) collective-permute-start(f32[128,256]{1,0:T(8,128)S(1)} %project.1.own), channel_id=1, source_target_pairs={{4,0},{0,4},{5,1},{1,5},{6,2},{2,6},{7,3},{3,7},{12,8},{8,12},{13,... | collective-permute-start | bytes 393224 | tf_op jit(solution)/shard_map/ppermute | solution.py:249
  150.9 1.0 collective-permute-done.8.other
  151.9 0.8 join.1
  152.8 2.3 %collective-permute-start.9 = (f32[4,256,128]{2,1,0:T(8,128)S(1)}, f32[4,256,128]{2,1,0:T(8,128)S(1)}, u32[]{:S(2)}, u32[]{:S(2)}) collective-permute-start(f32[4,256,128]{2,1,0:T(8,128)S(1)} %all-to-all-done.5.own), channel_id=1, source_target_pairs={{4,0},{0,4},{5,1},{1,5},{6,2},{2,6},{7,3},{3,7},{12,8},{8,12},{13,... | collective-permute-start | bytes 1572872 | tf_op jit(solution)/shard_map/ppermute | solution.py:249
  155.0 4.5 %all-to-all-start.6 = ((f32[4,128,256]{2,1,0:T(8,128)}), f32[4,128,256]{2,1,0:T(8,128)S(1)}, u32[]{:S(2)}, u32[]{:S(2)}) async-start(f32[4,128,256]{2,1,0:T(8,128)} %join.1), calls=%async_computation.6 | async-start | bytes 1048576 | tf_op jit(solution)/shard_map/projected_gather/all_to_all | solution.py:346
  159.5 0.0 collective-permute-done.9.other
  159.5 1.9 %step_batch.1 = (f32[250,1024]{1,0:T(8,128)}, f32[250,256]{1,0:T(8,128)S(1)}) custom-call(f32[4,256,128]{2,1,0:T(8,128)S(1)} %all-to-all-done.5.own, f32[4,256,128]{2,1,0:T(8,128)S(1)} %collective-permute-done.9.other, s32[4,1,256]{2,1,0:T(1,128)S(1)} %bitcast.19, s32[4,1,256]{2,1,0:T(1,128)S(1)} %bitcast.20, f32[250,256]{1,0:T(8,128)S(1)} %copy-done), custom_call_target="tpu_custom_call" | custom-call | tf_op jit(solution)/shard_map/step_batch/pallas_call | solution.py:231
  161.4 7.2 %all-to-all-done.6 = f32[4,128,256]{2,1,0:T(8,128)S(1)} async-done(((f32[4,128,256]{2,1,0:T(8,128)}), f32[4,128,256]{2,1,0:T(8,128)S(1)}, u32[]{:S(2)}, u32[]{:S(2)}) %all-to-all-start.6) | async-done | bytes 524320 | tf_op jit(solution)/shard_map/projected_gather/all_to_all | solution.py:346
  168.7 1.1 correct.1
  (12 shorter events, 0.1 us)
Async XLA Ops:
  0.6 0.7 copy-start.4
  30.0 6.9 %copy-start.1 = (bf16[256,320]{0,1:T(8,128)(2,1)S(1)}, bf16[256,320]{0,1:T(8,128)(2,1)}, u32[]{:S(2)}) copy-start(bf16[256,320]{0,1:T(8,128)(2,1)} %param.8) | copy-start | bytes 491524
  30.0 35.6 %copy-start = (f32[250,256]{1,0:T(8,128)S(1)}, f32[250,256]{1,0:T(8,128)}, u32[]{:S(2)}) copy-start(f32[250,256]{1,0:T(8,128)} %coefficients.3) | copy-start | bytes 768004
  30.0 35.6 %copy-start.2 = (f32[64,512]{1,0:T(8,128)S(1)}, f32[64,512]{1,0:T(8,128)}, u32[]{:S(2)}) copy-start(f32[64,512]{1,0:T(8,128)} %vectors.1) | copy-start | bytes 393220
  30.0 35.6 %copy-start.6 = (f32[512]{0:T(512)S(1)}, f32[512]{0:T(512)}, u32[]{:S(2)}) copy-start(f32[512]{0:T(512)} %param.15) | copy-start | bytes 6148
  30.0 35.6 %copy-start.7 = (s32[64]{0:T(128)S(1)}, s32[64]{0:T(128)}, u32[]{:S(2)}) copy-start(s32[64]{0:T(128)} %param.13) | copy-start | bytes 772
  30.0 33.1 %all-to-all-start.1 = ((bf16[16,40,8,128]{3,2,1,0:T(8,128)(2,1)}), bf16[16,40,8,128]{3,2,1,0:T(8,128)(2,1)S(1)}, u32[]{:S(2)}, u32[]{:S(2)}) async-start(bf16[16,40,8,128]{3,2,1,0:T(8,128)(2,1)} %pack.1), calls=%async_computation.1 | async-start | bytes 2621440 | tf_op jit(solution)/shard_map/batch_xy/all_to_all | solution.py:301
  36.9 20.6 %collective-permute-start = (bf16[320,256]{1,0:T(8,128)(2,1)S(1)}, bf16[320,256]{1,0:T(8,128)(2,1)S(1)}, u32[]{:S(2)}, u32[]{:S(2)}) collective-permute-start(bf16[320,256]{1,0:T(8,128)(2,1)S(1)} %bitcast.13), channel_id=1, source_target_pairs={{1,0},{2,1},{3,2},{0,3},{5,4},{6,5},{7,6},{4,7},{9,8},{10,9},{11,1... | collective-permute-start | bytes 491528 | tf_op jit(solution)/shard_map/centers_gather/ppermute | solution.py:249
  41.4 18.8 %collective-permute-start.1 = (bf16[320,256]{1,0:T(8,128)(2,1)S(1)}, bf16[320,256]{1,0:T(8,128)(2,1)S(1)}, u32[]{:S(2)}, u32[]{:S(2)}) collective-permute-start(bf16[320,256]{1,0:T(8,128)(2,1)S(1)} %bitcast.14), channel_id=1, source_target_pairs={{2,0},{3,1},{0,2},{1,3},{6,4},{7,5},{4,6},{5,7},{10,8},{11,9},{8,1... | collective-permute-start | bytes 491528 | tf_op jit(solution)/shard_map/centers_gather/ppermute | solution.py:249
  43.9 19.2 %collective-permute-start.2 = (bf16[320,256]{1,0:T(8,128)(2,1)S(1)}, bf16[320,256]{1,0:T(8,128)(2,1)S(1)}, u32[]{:S(2)}, u32[]{:S(2)}) collective-permute-start(bf16[320,256]{1,0:T(8,128)(2,1)S(1)} %bitcast.15), channel_id=1, source_target_pairs={{3,0},{0,1},{1,2},{2,3},{7,4},{4,5},{5,6},{6,7},{11,8},{8,9},{9,10... | collective-permute-start | bytes 491528 | tf_op jit(solution)/shard_map/centers_gather/ppermute | solution.py:249
  63.1 6.8 %collective-permute-start.3 = (bf16[4,4,40,8,128]{4,3,2,1,0:T(8,128)(2,1)S(1)}, bf16[4,4,40,8,128]{4,3,2,1,0:T(8,128)(2,1)S(1)}, u32[]{:S(2)}, u32[]{:S(2)}) collective-permute-start(bf16[4,4,40,8,128]{4,3,2,1,0:T(8,128)(2,1)S(1)} %bitcast.9), channel_id=1, source_target_pairs={{4,0},{0,4},{5,1},{1,5},{6,2},{2,6},{7,3},{3,7},{12,8},{8,12},{13,... | collective-permute-start | bytes 3932168 | tf_op jit(solution)/shard_map/ppermute | solution.py:249
  68.0 4.2 %collective-permute-start.4 = (f32[4,384,128]{2,1,0:T(8,128)S(1)}, f32[4,384,128]{2,1,0:T(8,128)S(1)}, u32[]{:S(2)}, u32[]{:S(2)}) collective-permute-start(f32[4,384,128]{2,1,0:T(8,128)S(1)} %kernel_products.3), channel_id=1, source_target_pairs={{4,0},{0,4},{5,1},{1,5},{6,2},{2,6},{7,3},{3,7},{12,8},{8,12},{13,... | collective-permute-start | bytes 2359304 | tf_op jit(solution)/shard_map/ppermute | solution.py:249
  86.7 54.7 %copy-start.3 = (s32[1024]{0:T(1024)S(1)}, s32[1024]{0:T(1024)}, u32[]{:S(2)}) copy-start(s32[1024]{0:T(1024)} %param.11) | copy-start | bytes 12292
  125.0 16.4 %all-to-all-start.5 = ((f32[4,256,128]{2,1,0:T(8,128)}), f32[4,256,128]{2,1,0:T(8,128)S(1)}, u32[]{:S(2)}, u32[]{:S(2)}) async-start(f32[4,256,128]{2,1,0:T(8,128)} %get-tuple-element.32), calls=%async_computation.5 | async-start | bytes 1048576 | tf_op jit(solution)/shard_map/all_to_all | solution.py:335
  128.5 8.3 %collective-permute-start.5 = (f32[4,32,128]{2,1,0:T(8,128)S(1)}, f32[4,32,128]{2,1,0:T(8,128)S(1)}, u32[]{:S(2)}, u32[]{:S(2)}) collective-permute-start(f32[4,32,128]{2,1,0:T(8,128)S(1)} %get-tuple-element.35.first), channel_id=1, source_target_pairs={{1,0},{2,1},{3,2},{0,3},{5,4},{6,5},{7,6},{4,7},{9,8},{10,9},{11,1... | collective-permute-start | bytes 196616 | tf_op jit(solution)/shard_map/basis_gather/ppermute | solution.py:249
  131.8 6.5 %collective-permute-start.6 = (f32[4,32,128]{2,1,0:T(8,128)S(1)}, f32[4,32,128]{2,1,0:T(8,128)S(1)}, u32[]{:S(2)}, u32[]{:S(2)}) collective-permute-start(f32[4,32,128]{2,1,0:T(8,128)S(1)} %get-tuple-element.35.first), channel_id=1, source_target_pairs={{2,0},{3,1},{0,2},{1,3},{6,4},{7,5},{4,6},{5,7},{10,8},{11,9},{8,1... | collective-permute-start | bytes 196616 | tf_op jit(solution)/shard_map/basis_gather/ppermute | solution.py:249
  134.9 6.5 %collective-permute-start.7 = (f32[4,32,128]{2,1,0:T(8,128)S(1)}, f32[4,32,128]{2,1,0:T(8,128)S(1)}, u32[]{:S(2)}, u32[]{:S(2)}) collective-permute-start(f32[4,32,128]{2,1,0:T(8,128)S(1)} %get-tuple-element.35.first), channel_id=1, source_target_pairs={{3,0},{0,1},{1,2},{2,3},{7,4},{4,5},{5,6},{6,7},{11,8},{8,9},{9,10... | collective-permute-start | bytes 196616 | tf_op jit(solution)/shard_map/basis_gather/ppermute | solution.py:249
  141.4 18.1 %copy-start.5 = (s32[1024]{0:T(1024)S(1)}, s32[1024]{0:T(1024)}, u32[]{:S(2)}) copy-start(s32[1024]{0:T(1024)} %param.12) | copy-start | bytes 12292
  142.3 9.6 %collective-permute-start.8 = (f32[128,256]{1,0:T(8,128)S(1)}, f32[128,256]{1,0:T(8,128)S(1)}, u32[]{:S(2)}, u32[]{:S(2)}) collective-permute-start(f32[128,256]{1,0:T(8,128)S(1)} %project.1.own), channel_id=1, source_target_pairs={{4,0},{0,4},{5,1},{1,5},{6,2},{2,6},{7,3},{3,7},{12,8},{8,12},{13,... | collective-permute-start | bytes 393224 | tf_op jit(solution)/shard_map/ppermute | solution.py:249
  152.8 6.8 %collective-permute-start.9 = (f32[4,256,128]{2,1,0:T(8,128)S(1)}, f32[4,256,128]{2,1,0:T(8,128)S(1)}, u32[]{:S(2)}, u32[]{:S(2)}) collective-permute-start(f32[4,256,128]{2,1,0:T(8,128)S(1)} %all-to-all-done.5.own), channel_id=1, source_target_pairs={{4,0},{0,4},{5,1},{1,5},{6,2},{2,6},{7,3},{3,7},{12,8},{8,12},{13,... | collective-permute-start | bytes 1572872 | tf_op jit(solution)/shard_map/ppermute | solution.py:249
  155.0 13.6 %all-to-all-start.6 = ((f32[4,128,256]{2,1,0:T(8,128)}), f32[4,128,256]{2,1,0:T(8,128)S(1)}, u32[]{:S(2)}, u32[]{:S(2)}) async-start(f32[4,128,256]{2,1,0:T(8,128)} %join.1), calls=%async_computation.6 | async-start | bytes 1048576 | tf_op jit(solution)/shard_map/projected_gather/all_to_all | solution.py:346

commit v7 on v6

--- a/solution.py
+++ b/solution.py
@@ -50,6 +50,17 @@
     padded = copies.shape[1]
     copies[...] = jnp.broadcast_to(sums[:padded][None], copies.shape)
     basis[...] = sums[padded:].reshape(basis.shape)
+
+
+def pair(own, other, both):
+    both[0] = own[...]
+    both[1] = other[...]
+
+
+def group_of(s):
+    y, groups = lax.axis_index(Y), lax.axis_size(Y)
+    y = y if s < 2 else groups - 1 - y
+    return y + (1 - 2 * lax.rem(y, 2)) if s % 2 else y
 
 
 def pack(batch, copies, granules):
@@ -66,16 +77,16 @@
     copies[...] = jnp.broadcast_to(granules[...][None], copies.shape)
 
 
-def kernel_products(batch, first, second, third, fourth, high, low, sums, *, padded):
+def kernel_products(batch, near_pair, far_pair, high, low, sums, *, padded):
     chips, groups, granules, rows, lanes = batch.shape
     blocks, lines, _ = sums.shape
     count = high.shape[1]
-    full, rest = first.shape[0] // lanes, first.shape[0] % lanes
+    full, rest = near_pair.shape[1] // lanes, near_pair.shape[1] % lanes
     depth = 2 * granules // (2 * full + 1)
     half = depth // 2
     near = depth // blocks
     split = (lines - padded) // blocks
-    centers = (first, second, third, fourth)[:groups]
+    centers = [p.at[i] for p in (near_pair, far_pair) for i in range(2)][:groups]
 
     center_norm = jnp.zeros((1, count), jnp.float32)
     tails = []
@@ -95,7 +106,7 @@
         is_own = (lane >= rest) if is_high else (lane < rest)
         ends = []
         for s in range(groups):
-            y = lax.rem(lax.axis_index(Y) + s, groups)
+            y = group_of(s)
             columns = []
             for h in range(full + 1):
                 pieces = []
@@ -164,11 +175,11 @@
     return (labels[j] == ids).astype(jnp.float32)
 
 
-def project(own, first, second, third, fourth, labels, projected, *, classes, rows_each):
-    blocks, split, lanes = first.shape
+def project(own, near_pair, far_pair, labels, projected, *, classes, rows_each):
+    _, blocks, split, lanes = near_pair.shape
     rows = own.shape[1]
     groups = projected.shape[0] // split
-    pieces = (first, second, third, fourth)[:groups]
+    pieces = [p.at[i] for p in (near_pair, far_pair) for i in range(2)][:groups]
     side = 1 - lax.axis_index(K)
     spot = lax.broadcasted_iota(jnp.int32, (lanes, 2 * lanes), 0)
     lane = lax.broadcasted_iota(jnp.int32, (lanes, 2 * lanes), 1)
@@ -188,7 +199,7 @@
             LAST,
         )
     for s in range(groups):
-        at = pl.multiple_of(lax.rem(lax.axis_index(Y) + s, groups) * split, split)
+        at = pl.multiple_of(group_of(s) * split, split)
         projected[pl.ds(at, split), :] = total[s * split : (s + 1) * split]
 
 
@@ -242,12 +253,15 @@
     return call
 
 
-def from_others(value, axis):
+def swapped(value, axis, mirrored=False):
     size = lax.axis_size(axis)
-    pieces = [value]
-    for s in range(1, size):
-        pieces.append(lax.ppermute(value, axis, [((d + s) % size, d) for d in range(size)]))
-    return pieces + [value] * (4 - size)
+    other = (lambda d: size - 1 - d) if mirrored else (lambda d: d ^ 1)
+    return lax.ppermute(value, axis, [(other(d), d) for d in range(size)])
+
+
+def paired(own, other):
+    out = jax.ShapeDtypeStruct((2, *own.shape), own.dtype)
+    return kernel(pair, out, "pair", limit=2)(own, other)
 
 
 def shards(
@@ -285,9 +299,11 @@
             0,
             tiled=True,
         )
-    batch_own, turned = lax.optimization_barrier((batch_own, centers.T))
     with jax.named_scope("centers_gather"):
-        center_pieces = from_others(turned, Y)
+        near_centers = paired(centers.T, swapped(centers.T, Y))
+    batch_own, near_centers = lax.optimization_barrier((batch_own, near_centers))
+    with jax.named_scope("centers_gather"):
+        far_centers = swapped(near_centers, Y, True)
     rows, width = batch_features.shape
     granules = (depth * (2 * width // LANES) // 2, rows, LANES)
     copies = kernel(
@@ -299,9 +315,9 @@
     )(batch_own)
     with jax.named_scope("batch_xy"):
         batch_own = lax.all_to_all(copies, (X, Y), 0, 0, tiled=True)
-    batch_own, center_pieces = lax.optimization_barrier((batch_own, center_pieces))
+    batch_own, far_centers = lax.optimization_barrier((batch_own, far_centers))
     batch_own = batch_own.reshape(chips, groups, *granules)
-    batch_other = from_others(batch_own, K)[1]
+    batch_other = swapped(batch_own, K)
 
     high, low, weights = kernel(
         lift,
@@ -320,8 +336,8 @@
     products = kernel(
         kernel_products, array(chips, lines, LANES), "kernel_products", limit=12, padded=padded
     )
-    sent = from_others(products(batch_own, *center_pieces, high, low), K)[1]
-    kept = products(batch_other, *center_pieces, high, low)
+    sent = swapped(products(batch_own, near_centers, far_centers, high, low), K)
+    kept = products(batch_other, near_centers, far_centers, high, low)
     own = kernel(add, array(chips, lines, LANES), "add", limit=6)(kept, sent)
 
     own = scattered(own, X)
@@ -331,7 +347,8 @@
         part, (array(chips, padded, LANES), array(chips, split, LANES)), "part", limit=4
     )(own)
     with jax.named_scope("basis_gather"):
-        basis = from_others(basis, Y)
+        basis = paired(basis, swapped(basis, Y))
+        basis = (basis, swapped(basis, Y, True))
     predicted = lax.all_to_all(copies, X, 0, 0, tiled=True)
     predicted, basis = lax.optimization_barrier((predicted, basis))
 
@@ -339,7 +356,7 @@
         project, array(groups * split, padded), "project", classes=classes, rows_each=rows
     )(predicted, *basis, labels)
     copies = kernel(join, array(chips, groups * split, padded), "join", limit=4)(
-        *from_others(half, K)[:2]
+        half, swapped(half, K)
     )
     copies, late = lax.optimization_barrier((copies, predicted))
     with jax.named_scope("projected_gather"):
@@ -350,7 +367,7 @@
         (array(classes, batch), array(classes, count)),
         "step_batch",
         rows_each=rows,
-    )(*from_others(late, K)[:2], labels, index, coefficients)
+    )(late, swapped(late, K), labels, index, coefficients)
     result = kernel(correct, array(classes, count), "correct")(updated, projected, weights)
     return (output, result)
 

time: 171 us -> 174 us (1.018)
  blocking collectives: 79.2 us -> 55.3 us
  starting transfers between devices: 47.8 us -> 61.2 us
  waiting for transfers between devices: 29.8 us -> 41.7 us
    all_to_all x1 -> x0, blocking collectives: 27.4 us -> none  [shards(): lax.all_to_all(kernel(fan, jax.ShapeDtypeStruct((depth, *batch_features.s...]
    all_to_all x0 -> x1, starting transfers between devices: none -> 15.7 us  [shards(): lax.all_to_all(kernel(fan, jax.ShapeDtypeStruct((depth, *batch_features.s...]
    ppermute x10 -> x8, waiting for transfers between devices: 22.5 us -> 30.5 us  [swapped(): return lax.ppermute(value, axis, [(other(d), d) for d in range(size)])]
    all_to_all x0 -> x1, waiting for transfers between devices: none -> 4 us  [shards(): lax.all_to_all(kernel(fan, jax.ShapeDtypeStruct((depth, *batch_features.s...]
    all_to_all x2, blocking collectives: 31.3 us -> 34.9 us  [scattered(): return jnp.sum(lax.all_to_all(tiles, axis, 0, 0, tiled=True), axis=0)]
    ppermute x10 -> x8, starting transfers between devices: 33 us -> 30.6 us  [swapped(): return lax.ppermute(value, axis, [(other(d), d) for d in range(size)])]
    pallas_call x11 -> x13, Pallas kernels: 11.4 us -> 12 us  [call(): pl.pallas_call(functools.partial(body, **settings), out_shape=outs, in_sp...]
  transfers between devices with their start and end apart: 13 -> 12, of which waited for: 8 -> 8; matrix products, arithmetic and copies ran while one was open for 0% -> 0% of each run, Pallas kernels for 4% -> 4%
where the time goes in v7:
time: 174 us; the launch traced here: 173 us
  starting transfers between devices  61.2 us (35%)
  blocking collectives  55.3 us (32%)
  waiting for transfers between devices  41.7 us (24%)
  Pallas kernels  12 us (7%)
    all_to_all x2, blocking collectives, scattered(): return jnp.sum(lax.all_to_all(tiles, axis, 0, 0, tiled=True), axis=0)  34.9 us
    ppermute x8, starting transfers between devices, swapped(): return lax.ppermute(value, axis, [(other(d), d) for d in range(size)])  30.6 us
    ppermute x8, waiting for transfers between devices, swapped(): return lax.ppermute(value, axis, [(other(d), d) for d in range(size)])  30.5 us
    all_to_all x1, blocking collectives, gathered(): return lax.all_to_all(copies, axis, 0, 0, tiled=True)  20.4 us
    all_to_all x1, starting transfers between devices, shards(): lax.all_to_all(kernel(fan, jax.ShapeDtypeStruct((depth, *batch_features.s...  15.7 us
    pallas_call x13, Pallas kernels, call(): pl.pallas_call(functools.partial(body, **settings), out_shape=outs, in_sp...  12 us
    all_to_all x1, waiting for transfers between devices, shards(): lax.all_to_all(copies, X, 0, 0, tiled=True).reshape(vectors, padded)  7.23 us
    all_to_all x1, starting transfers between devices, shards(): batch_own = lax.all_to_all(copies, (X, Y), 0, 0, tiled=True)  6.9 us
  transfers between devices with their start and end apart: 12, of which 8 were waited for; matrix products, arithmetic and copies ran while one was open for 0% of the time, Pallas kernels for 4%

profile of v7, /device:TPU:1, one launch (start us, length us, event | category | flops | bytes accessed | tf_op | source)
XLA Modules:
  0.0 172.9 jit_solution(1896153351619077915)
XLA Ops:
  0.6 0.0 copy-start.4
  0.6 0.7 copy-done.4
  1.3 0.6 fan.1
  2.0 15.7 %all-to-all-start = ((bf16[16,8,320]{2,1,0:T(8,128)(2,1)}), bf16[16,8,320]{2,1,0:T(8,128)(2,1)S(1)}, u32[]{:S(2)}, u32[]{:S(2)}) async-start(bf16[16,8,320]{2,1,0:T(8,128)(2,1)} %fan.1), calls=%async_computation | async-start | bytes 196608 | tf_op jit(solution)/shard_map/batch_z/all_to_all | solution.py:290
  17.7 3.2 %collective-permute-start = (bf16[320,256]{1,0:T(8,128)(2,1)}, bf16[320,256]{1,0:T(8,128)(2,1)S(1)}, u32[]{:S(2)}, u32[]{:S(2)}) collective-permute-start(bf16[320,256]{1,0:T(8,128)(2,1)} %bitcast.13), channel_id=1, source_target_pairs={{1,0},{0,1},{3,2},{2,3},{5,4},{4,5},{7,6},{6,7},{9,8},{8,9},{11,10... | collective-permute-start | bytes 491528 | tf_op jit(solution)/shard_map/centers_gather/ppermute | solution.py:259
  20.9 3.7 %collective-permute-done.other = bf16[320,256]{1,0:T(8,128)(2,1)S(1)} collective-permute-done((bf16[320,256]{1,0:T(8,128)(2,1)}, bf16[320,256]{1,0:T(8,128)(2,1)S(1)}, u32[]{:S(2)}, u32[]{:S(2)}) %collective-permute-start) | collective-permute-done | bytes 163872 | tf_op jit(solution)/shard_map/centers_gather/ppermute | solution.py:259
  24.6 0.9 copy-done.1
  25.6 4.0 %all-to-all-done.batch = bf16[16,8,320]{2,1,0:T(8,128)(2,1)S(1)} async-done(((bf16[16,8,320]{2,1,0:T(8,128)(2,1)}), bf16[16,8,320]{2,1,0:T(8,128)(2,1)S(1)}, u32[]{:S(2)}, u32[]{:S(2)}) %all-to-all-start) | async-done | bytes 81952 | tf_op jit(solution)/shard_map/batch_z/all_to_all | solution.py:290
  29.6 1.3 pack.1
  30.9 6.9 %all-to-all-start.1 = ((bf16[16,40,8,128]{3,2,1,0:T(8,128)(2,1)}), bf16[16,40,8,128]{3,2,1,0:T(8,128)(2,1)S(1)}, u32[]{:S(2)}, u32[]{:S(2)}) async-start(bf16[16,40,8,128]{3,2,1,0:T(8,128)(2,1)} %pack.1), calls=%async_computation.1 | async-start | bytes 2621440 | tf_op jit(solution)/shard_map/batch_xy/all_to_all | solution.py:317
  37.8 4.5 %collective-permute-start.1 = (bf16[2,320,256]{2,1,0:T(8,128)(2,1)S(1)}, bf16[2,320,256]{2,1,0:T(8,128)(2,1)S(1)}, u32[]{:S(2)}, u32[]{:S(2)}) collective-permute-start(bf16[2,320,256]{2,1,0:T(8,128)(2,1)S(1)} %pair.2.near_pair), channel_id=1, source_target_pairs={{3,0},{2,1},{1,2},{0,3},{7,4},{6,5},{5,6},{4,7},{11,8},{10,9},{9,1... | collective-permute-start | bytes 983048 | tf_op jit(solution)/shard_map/centers_gather/ppermute | solution.py:259
  42.2 18.5 %collective-permute-done.1.far_pair = bf16[2,320,256]{2,1,0:T(8,128)(2,1)S(1)} collective-permute-done((bf16[2,320,256]{2,1,0:T(8,128)(2,1)S(1)}, bf16[2,320,256]{2,1,0:T(8,128)(2,1)S(1)}, u32[]{:S(2)}, u32[]{:S(2)}) %collective-permute-start.1) | collective-permute-done | bytes 327712 | tf_op jit(solution)/shard_map/centers_gather/ppermute | solution.py:259
  60.7 0.0 all-to-all-done.1
  60.7 4.5 %collective-permute-start.2 = (bf16[4,4,40,8,128]{4,3,2,1,0:T(8,128)(2,1)S(1)}, bf16[4,4,40,8,128]{4,3,2,1,0:T(8,128)(2,1)S(1)}, u32[]{:S(2)}, u32[]{:S(2)}) collective-permute-start(bf16[4,4,40,8,128]{4,3,2,1,0:T(8,128)(2,1)S(1)} %bitcast.9), channel_id=1, source_target_pairs={{4,0},{0,4},{5,1},{1,5},{6,2},{2,6},{7,3},{3,7},{12,8},{8,12},{13,... | collective-permute-start | bytes 3932168 | tf_op jit(solution)/shard_map/ppermute | solution.py:259
  65.2 0.0 copy-done
  65.2 0.0 copy-done.2
  65.2 0.0 copy-done.6
  65.2 0.0 copy-done.7
  65.2 0.5 lift.1
  65.7 2.0 %kernel_products.3 = f32[4,384,128]{2,1,0:T(8,128)S(1)} custom-call(bf16[4,4,40,8,128]{4,3,2,1,0:T(8,128)(2,1)S(1)} %bitcast.10, bf16[2,320,256]{2,1,0:T(8,128)(2,1)S(1)} %pair.2.near_pair, bf16[2,320,256]{2,1,0:T(8,128)(2,1)S(1)} %collective-permute-done.1.far_pair, bf16[384,256]{1,0:T(8,128)(2,1)S(1)} %get-tuple-element.22.high, ...), custom_call_target="tpu_custom_call" | custom-call | tf_op jit(solution)/shard_map/kernel_products/pallas_call | solution.py:242
  67.7 1.9 %collective-permute-start.3 = (f32[4,384,128]{2,1,0:T(8,128)S(1)}, f32[4,384,128]{2,1,0:T(8,128)S(1)}, u32[]{:S(2)}, u32[]{:S(2)}) collective-permute-start(f32[4,384,128]{2,1,0:T(8,128)S(1)} %kernel_products.3), channel_id=1, source_target_pairs={{4,0},{0,4},{5,1},{1,5},{6,2},{2,6},{7,3},{3,7},{12,8},{8,12},{13,... | collective-permute-start | bytes 2359304 | tf_op jit(solution)/shard_map/ppermute | solution.py:259
  69.6 0.0 collective-permute-done.2.batch
  69.6 2.0 %kernel_products.2.own = f32[4,384,128]{2,1,0:T(8,128)S(1)} custom-call(bf16[4,4,40,8,128]{4,3,2,1,0:T(8,128)(2,1)S(1)} %collective-permute-done.2.batch, bf16[2,320,256]{2,1,0:T(8,128)(2,1)S(1)} %pair.2.near_pair, bf16[2,320,256]{2,1,0:T(8,128)(2,1)S(1)} %collective-permute-done.1.far_pair, bf16[384,256]{1,0:T(8,128)(2,1)S(1)} %get-tuple-element.22.high, ...), custom_call_target="tpu_custom_call" | custom-call | tf_op jit(solution)/shard_map/kernel_products/pallas_call | solution.py:242
  71.6 0.3 collective-permute-done.3.other
  71.8 0.1 add.1
  71.9 15.6 %all_to_all.35 = f32[4,384,128]{2,1,0:T(8,128)S(1)} all-to-all(f32[4,384,128]{2,1,0:T(8,128)S(1)} %add.1), channel_id=1, replica_groups=mesh['rows_z'=16,'rows_x'=4,'rows_k'=2,'cls'=4] {'rows_x'}, dimensions={0} | all-to-all | bytes 1572864 | tf_op jit(solution)/shard_map/all_to_all | solution.py:30
  87.6 0.0 copy-start.3
  87.6 19.3 %all_to_all.36 = f32[16,24,128]{2,1,0:T(8,128)S(1)} all-to-all(f32[16,24,128]{2,1,0:T(8,128)S(1)} %bitcast.20), channel_id=1, replica_groups=mesh['rows_z'=16,'rows_x'=4,'rows_k'=2,'cls'=4] {'rows_z'}, dimensions={0} | all-to-all | bytes 393216 | tf_op jit(solution)/shard_map/all_to_all | solution.py:30
  106.9 20.4 %all_to_all.37 = f32[16,24,128]{2,1,0:T(8,128)S(1)} all-to-all(f32[16,24,128]{2,1,0:T(8,128)S(1)} %broadcast_in_dim.11), channel_id=1, replica_groups=mesh['rows_z'=16,'rows_x'=4,'rows_k'=2,'cls'=4] {'rows_z'}, dimensions={0} | all-to-all | bytes 393216 | tf_op jit(solution)/shard_map/all_to_all | solution.py:26
  127.3 0.8 part.1
  128.2 3.5 %all-to-all-start.5 = ((f32[4,256,128]{2,1,0:T(8,128)}), f32[4,256,128]{2,1,0:T(8,128)S(1)}, u32[]{:S(2)}, u32[]{:S(2)}) async-start(f32[4,256,128]{2,1,0:T(8,128)} %get-tuple-element.24), calls=%async_computation.5 | async-start | bytes 1048576 | tf_op jit(solution)/shard_map/all_to_all | solution.py:352
  131.7 1.9 %collective-permute-start.4 = (f32[4,32,128]{2,1,0:T(8,128)S(1)}, f32[4,32,128]{2,1,0:T(8,128)S(1)}, u32[]{:S(2)}, u32[]{:S(2)}) collective-permute-start(f32[4,32,128]{2,1,0:T(8,128)S(1)} %get-tuple-element.25.own), channel_id=1, source_target_pairs={{1,0},{0,1},{3,2},{2,3},{5,4},{4,5},{7,6},{6,7},{9,8},{8,9},{11,10... | collective-permute-start | bytes 196616 | tf_op jit(solution)/shard_map/basis_gather/ppermute | solution.py:259
  133.6 3.1 %collective-permute-done.4.other = f32[4,32,128]{2,1,0:T(8,128)S(1)} collective-permute-done((f32[4,32,128]{2,1,0:T(8,128)S(1)}, f32[4,32,128]{2,1,0:T(8,128)S(1)}, u32[]{:S(2)}, u32[]{:S(2)}) %collective-permute-start.4) | collective-permute-done | bytes 65568 | tf_op jit(solution)/shard_map/basis_gather/ppermute | solution.py:259
  136.7 3.2 %collective-permute-start.5 = (f32[2,4,32,128]{3,2,1,0:T(8,128)S(1)}, f32[2,4,32,128]{3,2,1,0:T(8,128)S(1)}, u32[]{:S(2)}, u32[]{:S(2)}) collective-permute-start(f32[2,4,32,128]{3,2,1,0:T(8,128)S(1)} %pair.3.near_pair), channel_id=1, source_target_pairs={{3,0},{2,1},{1,2},{0,3},{7,4},{6,5},{5,6},{4,7},{11,8},{10,9},{9,1... | collective-permute-start | bytes 393224 | tf_op jit(solution)/shard_map/basis_gather/ppermute | solution.py:259
  139.9 4.0 %collective-permute-done.5.far_pair = f32[2,4,32,128]{3,2,1,0:T(8,128)S(1)} collective-permute-done((f32[2,4,32,128]{3,2,1,0:T(8,128)S(1)}, f32[2,4,32,128]{3,2,1,0:T(8,128)S(1)}, u32[]{:S(2)}, u32[]{:S(2)}) %collective-permute-start.5) | collective-permute-done | bytes 131104 | tf_op jit(solution)/shard_map/basis_gather/ppermute | solution.py:259
  143.9 0.0 all-to-all-done.5.own
  143.9 0.0 copy-done.3
  143.9 0.9 project.1.own
  144.8 9.2 %collective-permute-start.6 = (f32[128,256]{1,0:T(8,128)S(1)}, f32[128,256]{1,0:T(8,128)S(1)}, u32[]{:S(2)}, u32[]{:S(2)}) collective-permute-start(f32[128,256]{1,0:T(8,128)S(1)} %project.1.own), channel_id=1, source_target_pairs={{4,0},{0,4},{5,1},{1,5},{6,2},{2,6},{7,3},{3,7},{12,8},{8,12},{13,... | collective-permute-start | bytes 393224 | tf_op jit(solution)/shard_map/ppermute | solution.py:259
  154.0 1.0 collective-permute-done.6.other
  155.0 0.8 join.1
  155.8 2.3 %collective-permute-start.7 = (f32[4,256,128]{2,1,0:T(8,128)S(1)}, f32[4,256,128]{2,1,0:T(8,128)S(1)}, u32[]{:S(2)}, u32[]{:S(2)}) collective-permute-start(f32[4,256,128]{2,1,0:T(8,128)S(1)} %all-to-all-done.5.own), channel_id=1, source_target_pairs={{4,0},{0,4},{5,1},{1,5},{6,2},{2,6},{7,3},{3,7},{12,8},{8,12},{13,... | collective-permute-start | bytes 1572872 | tf_op jit(solution)/shard_map/ppermute | solution.py:259
  158.1 4.5 %all-to-all-start.6 = ((f32[4,128,256]{2,1,0:T(8,128)}), f32[4,128,256]{2,1,0:T(8,128)S(1)}, u32[]{:S(2)}, u32[]{:S(2)}) async-start(f32[4,128,256]{2,1,0:T(8,128)} %join.1), calls=%async_computation.6 | async-start | bytes 1048576 | tf_op jit(solution)/shard_map/projected_gather/all_to_all | solution.py:363
  162.6 0.0 collective-permute-done.7.other
  162.6 0.0 copy-done.5
  162.6 1.9 %step_batch.1 = (f32[250,1024]{1,0:T(8,128)}, f32[250,256]{1,0:T(8,128)S(1)}) custom-call(f32[4,256,128]{2,1,0:T(8,128)S(1)} %all-to-all-done.5.own, f32[4,256,128]{2,1,0:T(8,128)S(1)} %collective-permute-done.7.other, s32[4,1,256]{2,1,0:T(1,128)S(1)} %bitcast.16, s32[4,1,256]{2,1,0:T(1,128)S(1)} %bitcast.17, f32[250,256]{1,0:T(8,128)S(1)} %copy-done), custom_call_target="tpu_custom_call" | custom-call | tf_op jit(solution)/shard_map/step_batch/pallas_call | solution.py:242
  164.5 7.2 %all-to-all-done.6 = f32[4,128,256]{2,1,0:T(8,128)S(1)} async-done(((f32[4,128,256]{2,1,0:T(8,128)}), f32[4,128,256]{2,1,0:T(8,128)S(1)}, u32[]{:S(2)}, u32[]{:S(2)}) %all-to-all-start.6) | async-done | bytes 524320 | tf_op jit(solution)/shard_map/projected_gather/all_to_all | solution.py:363
  171.7 1.1 correct.1
  (11 shorter events, 0.1 us)
Async XLA Ops:
  0.6 0.7 copy-start.4
  2.0 27.6 %all-to-all-start = ((bf16[16,8,320]{2,1,0:T(8,128)(2,1)}), bf16[16,8,320]{2,1,0:T(8,128)(2,1)S(1)}, u32[]{:S(2)}, u32[]{:S(2)}) async-start(bf16[16,8,320]{2,1,0:T(8,128)(2,1)} %fan.1), calls=%async_computation | async-start | bytes 196608 | tf_op jit(solution)/shard_map/batch_z/all_to_all | solution.py:290
  17.7 6.9 %collective-permute-start = (bf16[320,256]{1,0:T(8,128)(2,1)}, bf16[320,256]{1,0:T(8,128)(2,1)S(1)}, u32[]{:S(2)}, u32[]{:S(2)}) collective-permute-start(bf16[320,256]{1,0:T(8,128)(2,1)} %bitcast.13), channel_id=1, source_target_pairs={{1,0},{0,1},{3,2},{2,3},{5,4},{4,5},{7,6},{6,7},{9,8},{8,9},{11,10... | collective-permute-start | bytes 491528 | tf_op jit(solution)/shard_map/centers_gather/ppermute | solution.py:259
  24.6 0.9 copy-start.1
  30.8 34.3 %copy-start = (f32[250,256]{1,0:T(8,128)S(1)}, f32[250,256]{1,0:T(8,128)}, u32[]{:S(2)}) copy-start(f32[250,256]{1,0:T(8,128)} %coefficients.3) | copy-start | bytes 768004
  30.8 34.4 %copy-start.2 = (f32[64,512]{1,0:T(8,128)S(1)}, f32[64,512]{1,0:T(8,128)}, u32[]{:S(2)}) copy-start(f32[64,512]{1,0:T(8,128)} %vectors.1) | copy-start | bytes 393220
  30.9 34.4 %copy-start.6 = (f32[512]{0:T(512)S(1)}, f32[512]{0:T(512)}, u32[]{:S(2)}) copy-start(f32[512]{0:T(512)} %param.15) | copy-start | bytes 6148
  30.9 34.4 %copy-start.7 = (s32[64]{0:T(128)S(1)}, s32[64]{0:T(128)}, u32[]{:S(2)}) copy-start(s32[64]{0:T(128)} %param.13) | copy-start | bytes 772
  30.9 29.9 %all-to-all-start.1 = ((bf16[16,40,8,128]{3,2,1,0:T(8,128)(2,1)}), bf16[16,40,8,128]{3,2,1,0:T(8,128)(2,1)S(1)}, u32[]{:S(2)}, u32[]{:S(2)}) async-start(bf16[16,40,8,128]{3,2,1,0:T(8,128)(2,1)} %pack.1), calls=%async_computation.1 | async-start | bytes 2621440 | tf_op jit(solution)/shard_map/batch_xy/all_to_all | solution.py:317
  37.8 22.9 %collective-permute-start.1 = (bf16[2,320,256]{2,1,0:T(8,128)(2,1)S(1)}, bf16[2,320,256]{2,1,0:T(8,128)(2,1)S(1)}, u32[]{:S(2)}, u32[]{:S(2)}) collective-permute-start(bf16[2,320,256]{2,1,0:T(8,128)(2,1)S(1)} %pair.2.near_pair), channel_id=1, source_target_pairs={{3,0},{2,1},{1,2},{0,3},{7,4},{6,5},{5,6},{4,7},{11,8},{10,9},{9,1... | collective-permute-start | bytes 983048 | tf_op jit(solution)/shard_map/centers_gather/ppermute | solution.py:259
  60.7 8.9 %collective-permute-start.2 = (bf16[4,4,40,8,128]{4,3,2,1,0:T(8,128)(2,1)S(1)}, bf16[4,4,40,8,128]{4,3,2,1,0:T(8,128)(2,1)S(1)}, u32[]{:S(2)}, u32[]{:S(2)}) collective-permute-start(bf16[4,4,40,8,128]{4,3,2,1,0:T(8,128)(2,1)S(1)} %bitcast.9), channel_id=1, source_target_pairs={{4,0},{0,4},{5,1},{1,5},{6,2},{2,6},{7,3},{3,7},{12,8},{8,12},{13,... | collective-permute-start | bytes 3932168 | tf_op jit(solution)/shard_map/ppermute | solution.py:259
  67.7 4.2 %collective-permute-start.3 = (f32[4,384,128]{2,1,0:T(8,128)S(1)}, f32[4,384,128]{2,1,0:T(8,128)S(1)}, u32[]{:S(2)}, u32[]{:S(2)}) collective-permute-start(f32[4,384,128]{2,1,0:T(8,128)S(1)} %kernel_products.3), channel_id=1, source_target_pairs={{4,0},{0,4},{5,1},{1,5},{6,2},{2,6},{7,3},{3,7},{12,8},{8,12},{13,... | collective-permute-start | bytes 2359304 | tf_op jit(solution)/shard_map/ppermute | solution.py:259
  87.6 56.3 %copy-start.3 = (s32[1024]{0:T(1024)S(1)}, s32[1024]{0:T(1024)}, u32[]{:S(2)}) copy-start(s32[1024]{0:T(1024)} %param.11) | copy-start | bytes 12292
  128.2 15.7 %all-to-all-start.5 = ((f32[4,256,128]{2,1,0:T(8,128)}), f32[4,256,128]{2,1,0:T(8,128)S(1)}, u32[]{:S(2)}, u32[]{:S(2)}) async-start(f32[4,256,128]{2,1,0:T(8,128)} %get-tuple-element.24), calls=%async_computation.5 | async-start | bytes 1048576 | tf_op jit(solution)/shard_map/all_to_all | solution.py:352
  131.7 5.0 %collective-permute-start.4 = (f32[4,32,128]{2,1,0:T(8,128)S(1)}, f32[4,32,128]{2,1,0:T(8,128)S(1)}, u32[]{:S(2)}, u32[]{:S(2)}) collective-permute-start(f32[4,32,128]{2,1,0:T(8,128)S(1)} %get-tuple-element.25.own), channel_id=1, source_target_pairs={{1,0},{0,1},{3,2},{2,3},{5,4},{4,5},{7,6},{6,7},{9,8},{8,9},{11,10... | collective-permute-start | bytes 196616 | tf_op jit(solution)/shard_map/basis_gather/ppermute | solution.py:259
  136.7 7.2 %collective-permute-start.5 = (f32[2,4,32,128]{3,2,1,0:T(8,128)S(1)}, f32[2,4,32,128]{3,2,1,0:T(8,128)S(1)}, u32[]{:S(2)}, u32[]{:S(2)}) collective-permute-start(f32[2,4,32,128]{3,2,1,0:T(8,128)S(1)} %pair.3.near_pair), channel_id=1, source_target_pairs={{3,0},{2,1},{1,2},{0,3},{7,4},{6,5},{5,6},{4,7},{11,8},{10,9},{9,1... | collective-permute-start | bytes 393224 | tf_op jit(solution)/shard_map/basis_gather/ppermute | solution.py:259
  143.9 18.7 %copy-start.5 = (s32[1024]{0:T(1024)S(1)}, s32[1024]{0:T(1024)}, u32[]{:S(2)}) copy-start(s32[1024]{0:T(1024)} %param.12) | copy-start | bytes 12292
  144.8 10.2 %collective-permute-start.6 = (f32[128,256]{1,0:T(8,128)S(1)}, f32[128,256]{1,0:T(8,128)S(1)}, u32[]{:S(2)}, u32[]{:S(2)}) collective-permute-start(f32[128,256]{1,0:T(8,128)S(1)} %project.1.own), channel_id=1, source_target_pairs={{4,0},{0,4},{5,1},{1,5},{6,2},{2,6},{7,3},{3,7},{12,8},{8,12},{13,... | collective-permute-start | bytes 393224 | tf_op jit(solution)/shard_map/ppermute | solution.py:259
  155.8 6.8 %collective-permute-start.7 = (f32[4,256,128]{2,1,0:T(8,128)S(1)}, f32[4,256,128]{2,1,0:T(8,128)S(1)}, u32[]{:S(2)}, u32[]{:S(2)}) collective-permute-start(f32[4,256,128]{2,1,0:T(8,128)S(1)} %all-to-all-done.5.own), channel_id=1, source_target_pairs={{4,0},{0,4},{5,1},{1,5},{6,2},{2,6},{7,3},{3,7},{12,8},{8,12},{13,... | collective-permute-start | bytes 1572872 | tf_op jit(solution)/shard_map/ppermute | solution.py:259
  158.1 13.6 %all-to-all-start.6 = ((f32[4,128,256]{2,1,0:T(8,128)}), f32[4,128,256]{2,1,0:T(8,128)S(1)}, u32[]{:S(2)}, u32[]{:S(2)}) async-start(f32[4,128,256]{2,1,0:T(8,128)} %join.1), calls=%async_computation.6 | async-start | bytes 1048576 | tf_op jit(solution)/shard_map/projected_gather/all_to_all | solution.py:363

commit v8 on v6

--- a/solution.py
+++ b/solution.py
@@ -8,15 +8,17 @@
 from jax.sharding import Mesh
 from jax.sharding import PartitionSpec as P
 
+
 Z, X, K, Y = "rows_z", "rows_x", "rows_k", "cls"
 ROWS = (Z, X, K)
 LANES = 128
 INTERPRET = False
 
+CODES = 32767.0
+
 spread = 4.0
 step_rate = 0.5
 
-HIGHEST = lax.Precision.HIGHEST
 LAST = (((1,), (1,)), ((), ()))
 FIRST = (((0,), (0,)), ((), ()))
 
@@ -53,7 +55,7 @@
 
 
 def pack(batch, copies, granules):
-    depth, rows, width = batch.shape
+    depth, _, width = batch.shape
     full, rest = width // LANES, width % LANES
     half = depth // 2
     for z in range(depth):
@@ -67,7 +69,7 @@
 
 
 def kernel_products(batch, first, second, third, fourth, high, low, sums, *, padded):
-    chips, groups, granules, rows, lanes = batch.shape
+    chips, groups, granules, _, lanes = batch.shape
     blocks, lines, _ = sums.shape
     count = high.shape[1]
     full, rest = first.shape[0] // lanes, first.shape[0] % lanes
@@ -155,8 +157,27 @@
     total[...] = own[...] + other[...]
 
 
-def join(own, other, copies):
-    copies[...] = jnp.broadcast_to((own[...] + other[...])[None], copies.shape)
+def join(own, other, copies, *, classes):
+    total = own[...] + other[...]
+    _, lanes = total.shape
+    lane = lax.broadcasted_iota(jnp.int32, total.shape, 1)
+    total = jnp.where(lane < classes, total, 0.0)
+    largest = jnp.maximum(jnp.max(jnp.abs(total), axis=1, keepdims=True), 1e-30)
+    power = jnp.clip(jnp.ceil(jnp.log2(largest)), -100.0, 100.0)
+    factor = jnp.ceil(largest * jnp.exp2(-power) * 16384.0) + 1.0
+    steps = jnp.floor(total * (CODES / (factor * jnp.exp2(power) / 16384.0)) + 0.5)
+    steps = jnp.clip(steps, -CODES, CODES)
+    steps = jnp.where(lane == lanes - 2, factor, jnp.where(lane == lanes - 1, power, steps))
+    codes = steps.astype(jnp.int32).astype(jnp.int16)
+    copies[...] = jnp.broadcast_to(codes[None], copies.shape)
+
+
+def decoded(codes):
+    steps = codes.astype(jnp.int32).astype(jnp.float32)
+    lanes = steps.shape[1]
+    lane = lax.broadcasted_iota(jnp.int32, steps.shape, 1)
+    pick = lambda n: jnp.sum(jnp.where(lane == n, steps, 0.0), axis=1, keepdims=True)
+    return steps * (pick(lanes - 2) * jnp.exp2(pick(lanes - 1)) / 16384.0 / CODES)
 
 
 def targets_of(labels, j, rows, classes):
@@ -220,11 +241,11 @@
 
 def correct(updated, projected, weights, result):
     classes = updated.shape[0]
-    change = product(in_two(projected[...]), in_two(weights[...]), FIRST)
+    change = product(in_two(decoded(projected[...])), in_two(weights[...]), FIRST)
     result[...] = updated[...] + change[:classes]
 
 
-def kernel(body, outs, name, scratch=(), limit=16, **settings):
+def kernel(body, outs, scratch=(), limit=16, **settings):
     near = pl.BlockSpec(memory_space=pltpu.VMEM)
 
     def call(*operands):
@@ -236,7 +257,6 @@
             scratch_shapes=scratch,
             compiler_params=pltpu.CompilerParams(vmem_limit_bytes=limit * 2**20),
             interpret=INTERPRET,
-            name=name,
         )(*operands)
 
     return call
@@ -266,39 +286,32 @@
     vectors = eigen_vectors.shape[1]
     split = vectors // groups // chips
     padded = -(-classes // 8) * 8
-    while (padded + vectors // groups) % (8 * depth):
+    while padded < classes + 2 or (padded + vectors // groups) % (8 * depth):
         padded += 8
     lines = padded + vectors // groups
     batch = batch_labels.shape[0]
     array = lambda *shape: jax.ShapeDtypeStruct(shape, jnp.float32)
 
-    with jax.named_scope("batch_z"):
-        batch_own = lax.all_to_all(
-            kernel(
-                fan,
-                jax.ShapeDtypeStruct((depth, *batch_features.shape), batch_features.dtype),
-                "fan",
-                limit=2,
-            )(batch_features),
-            Z,
-            0,
-            0,
-            tiled=True,
-        )
+    batch_own = lax.all_to_all(
+        kernel(
+            fan, jax.ShapeDtypeStruct((depth, *batch_features.shape), batch_features.dtype), limit=2
+        )(batch_features),
+        Z,
+        0,
+        0,
+        tiled=True,
+    )
     batch_own, turned = lax.optimization_barrier((batch_own, centers.T))
-    with jax.named_scope("centers_gather"):
-        center_pieces = from_others(turned, Y)
+    center_pieces = from_others(turned, Y)
     rows, width = batch_features.shape
     granules = (depth * (2 * width // LANES) // 2, rows, LANES)
     copies = kernel(
         pack,
         jax.ShapeDtypeStruct((chips * groups, *granules), batch_own.dtype),
-        "pack",
         (pltpu.VMEM(granules, batch_own.dtype),),
         limit=2,
     )(batch_own)
-    with jax.named_scope("batch_xy"):
-        batch_own = lax.all_to_all(copies, (X, Y), 0, 0, tiled=True)
+    batch_own = lax.all_to_all(copies, (X, Y), 0, 0, tiled=True)
     batch_own, center_pieces = lax.optimization_barrier((batch_own, center_pieces))
     batch_own = batch_own.reshape(chips, groups, *granules)
     batch_other = from_others(batch_own, K)[1]
@@ -310,54 +323,49 @@
             jax.ShapeDtypeStruct((lines, count), jnp.bfloat16),
             array(vectors, count),
         ),
-        "lift",
         (pltpu.VMEM((lines, count), jnp.float32),),
         limit=6,
     )(eigen_vectors, eigen_scale[None], subset_index[None], coefficients)
     labels = batch_labels.reshape(chips, 1, 2 * LANES)
     index = batch_index.reshape(chips, 1, 2 * LANES)
 
-    products = kernel(
-        kernel_products, array(chips, lines, LANES), "kernel_products", limit=12, padded=padded
-    )
+    products = kernel(kernel_products, array(chips, lines, LANES), limit=12, padded=padded)
     sent = from_others(products(batch_own, *center_pieces, high, low), K)[1]
     kept = products(batch_other, *center_pieces, high, low)
-    own = kernel(add, array(chips, lines, LANES), "add", limit=6)(kept, sent)
+    own = kernel(add, array(chips, lines, LANES), limit=6)(kept, sent)
 
     own = scattered(own, X)
     own = scattered(own.reshape(depth, lines // depth, LANES), Z)
     own = gathered(own, Z).reshape(lines, LANES)
     copies, basis = kernel(
-        part, (array(chips, padded, LANES), array(chips, split, LANES)), "part", limit=4
+        part, (array(chips, padded, LANES), array(chips, split, LANES)), limit=4
     )(own)
-    with jax.named_scope("basis_gather"):
-        basis = from_others(basis, Y)
+    basis = from_others(basis, Y)
     predicted = lax.all_to_all(copies, X, 0, 0, tiled=True)
     predicted, basis = lax.optimization_barrier((predicted, basis))
 
     half = kernel(
-        project, array(groups * split, padded), "project", classes=classes, rows_each=rows
+        project, array(groups * split, padded), classes=classes, rows_each=rows
     )(predicted, *basis, labels)
-    copies = kernel(join, array(chips, groups * split, padded), "join", limit=4)(
+    codes = jax.ShapeDtypeStruct((chips, groups * split, padded), jnp.int16)
+    copies = kernel(join, codes, limit=4, classes=classes)(
         *from_others(half, K)[:2]
     )
     copies, late = lax.optimization_barrier((copies, predicted))
-    with jax.named_scope("projected_gather"):
-        projected = lax.all_to_all(copies, X, 0, 0, tiled=True).reshape(vectors, padded)
-
+    projected = lax.all_to_all(copies, X, 0, 0, tiled=True).reshape(vectors, padded)
+
+    late = from_others(late, K)[:2]
     output, updated = kernel(
-        step_batch,
-        (array(classes, batch), array(classes, count)),
-        "step_batch",
-        rows_each=rows,
-    )(*from_others(late, K)[:2], labels, index, coefficients)
-    result = kernel(correct, array(classes, count), "correct")(updated, projected, weights)
+        step_batch, (array(classes, batch), array(classes, count)), rows_each=rows
+    )(*late, labels, index, coefficients)
+    result = kernel(correct, array(classes, count))(updated, projected, weights)
     return (output, result)
 
 
 def solution(mesh, shape=(16, 4, 2)):
     finer = Mesh(mesh.devices.reshape(*shape, mesh.shape["cls"]), (*ROWS, Y))
     placed = (P(ROWS, Y), P(Y, ROWS), P(ROWS, Y), P(), P(), P(ROWS), P(ROWS, None), P())
+
     return jax.shard_map(
         shards,
         mesh=finer,

time: 171 us -> 168 us (0.982)
  waiting for transfers between devices: 29.8 us -> 26.7 us
    all_to_all x1, waiting for transfers between devices: 7.23 us -> 4.13 us  [shards(): lax.all_to_all(copies, X, 0, 0, tiled=True).reshape(vectors, padded)]
where the time goes in v8:
time: 168 us; the launch traced here: 167 us
  blocking collectives  79.2 us (47%)
  starting transfers between devices  48 us (29%)
  waiting for transfers between devices  26.7 us (16%)
  Pallas kernels  11.6 us (7%)
    ppermute x10, starting transfers between devices, from_others(): lax.ppermute(value, axis, [((d + s) % size, d) for d in range(size)])  33 us
    all_to_all x2, blocking collectives, scattered(): return jnp.sum(lax.all_to_all(tiles, axis, 0, 0, tiled=True), axis=0)  31.3 us
    all_to_all x1, blocking collectives, shards(): lax.all_to_all(kernel(fan, jax.ShapeDtypeStruct((depth, *batch_features.s...  27.4 us
    ppermute x10, waiting for transfers between devices, from_others(): lax.ppermute(value, axis, [((d + s) % size, d) for d in range(size)])  22.5 us
    all_to_all x1, blocking collectives, gathered(): return lax.all_to_all(copies, axis, 0, 0, tiled=True)  20.4 us
    pallas_call x11, Pallas kernels, call(): pl.pallas_call(functools.partial(body, **settings), out_shape=outs, in_sp...  11.6 us
    all_to_all x1, starting transfers between devices, shards(): batch_own = lax.all_to_all(copies, (X, Y), 0, 0, tiled=True)  6.9 us
    all_to_all x1, starting transfers between devices, shards(): lax.all_to_all(copies, X, 0, 0, tiled=True).reshape(vectors, padded)  4.48 us
  transfers between devices with their start and end apart: 13, of which 8 were waited for; matrix products, arithmetic and copies ran while one was open for 0% of the time, Pallas kernels for 4%

profile of v8, /device:TPU:1, one launch (start us, length us, event | category | flops | bytes accessed | tf_op | source)
XLA Modules:
  0.0 167.0 jit_solution(13952311509434900014)
XLA Ops:
  0.6 0.7 copy-done.4
  1.3 27.4 %all_to_all.35.batch = bf16[16,8,320]{2,1,0:T(8,128)(2,1)S(1)} all-to-all(bf16[16,8,320]{2,1,0:T(8,128)(2,1)S(1)} %shard_map.95), channel_id=1, replica_groups=mesh['rows_z'=16,'rows_x'=4,'rows_k'=2,'cls'=4] {'rows_z'}, dimensions={0} | all-to-all | bytes 163840 | tf_op jit(solution)/shard_map/all_to_all | solution.py:295
  28.7 1.3 shard_map.96
  30.0 0.0 copy-start.7
  30.0 6.9 %all-to-all-start.1 = ((bf16[16,40,8,128]{3,2,1,0:T(8,128)(2,1)}), bf16[16,40,8,128]{3,2,1,0:T(8,128)(2,1)S(1)}, u32[]{:S(2)}, u32[]{:S(2)}) async-start(bf16[16,40,8,128]{3,2,1,0:T(8,128)(2,1)} %shard_map.96), calls=%async_computation.1 | async-start | bytes 2621440 | tf_op jit(solution)/shard_map/all_to_all | solution.py:314
  36.9 0.0 copy-done.1
  36.9 4.5 %collective-permute-start = (bf16[320,256]{1,0:T(8,128)(2,1)S(1)}, bf16[320,256]{1,0:T(8,128)(2,1)S(1)}, u32[]{:S(2)}, u32[]{:S(2)}) collective-permute-start(bf16[320,256]{1,0:T(8,128)(2,1)S(1)} %bitcast.13), channel_id=1, source_target_pairs={{1,0},{2,1},{3,2},{0,3},{5,4},{6,5},{7,6},{4,7},{9,8},{10,9},{11,1... | collective-permute-start | bytes 491528 | tf_op jit(solution)/shard_map/ppermute | solution.py:269
  41.4 2.5 %collective-permute-start.1 = (bf16[320,256]{1,0:T(8,128)(2,1)S(1)}, bf16[320,256]{1,0:T(8,128)(2,1)S(1)}, u32[]{:S(2)}, u32[]{:S(2)}) collective-permute-start(bf16[320,256]{1,0:T(8,128)(2,1)S(1)} %bitcast.14), channel_id=1, source_target_pairs={{2,0},{3,1},{0,2},{1,3},{6,4},{7,5},{4,6},{5,7},{10,8},{11,9},{8,1... | collective-permute-start | bytes 491528 | tf_op jit(solution)/shard_map/ppermute | solution.py:269
  43.9 2.5 %collective-permute-start.2 = (bf16[320,256]{1,0:T(8,128)(2,1)S(1)}, bf16[320,256]{1,0:T(8,128)(2,1)S(1)}, u32[]{:S(2)}, u32[]{:S(2)}) collective-permute-start(bf16[320,256]{1,0:T(8,128)(2,1)S(1)} %bitcast.15), channel_id=1, source_target_pairs={{3,0},{0,1},{1,2},{2,3},{7,4},{4,5},{5,6},{6,7},{11,8},{8,9},{9,10... | collective-permute-start | bytes 491528 | tf_op jit(solution)/shard_map/ppermute | solution.py:269
  46.4 11.1 %collective-permute-done.second = bf16[320,256]{1,0:T(8,128)(2,1)S(1)} collective-permute-done((bf16[320,256]{1,0:T(8,128)(2,1)S(1)}, bf16[320,256]{1,0:T(8,128)(2,1)S(1)}, u32[]{:S(2)}, u32[]{:S(2)}) %collective-permute-start) | collective-permute-done | bytes 163872 | tf_op jit(solution)/shard_map/ppermute | solution.py:269
  57.6 2.7 %collective-permute-done.1.third = bf16[320,256]{1,0:T(8,128)(2,1)S(1)} collective-permute-done((bf16[320,256]{1,0:T(8,128)(2,1)S(1)}, bf16[320,256]{1,0:T(8,128)(2,1)S(1)}, u32[]{:S(2)}, u32[]{:S(2)}) %collective-permute-start.1) | collective-permute-done | bytes 163872 | tf_op jit(solution)/shard_map/ppermute | solution.py:269
  60.2 2.9 %collective-permute-done.2.fourth = bf16[320,256]{1,0:T(8,128)(2,1)S(1)} collective-permute-done((bf16[320,256]{1,0:T(8,128)(2,1)S(1)}, bf16[320,256]{1,0:T(8,128)(2,1)S(1)}, u32[]{:S(2)}, u32[]{:S(2)}) %collective-permute-start.2) | collective-permute-done | bytes 163872 | tf_op jit(solution)/shard_map/ppermute | solution.py:269
  63.1 0.0 all-to-all-done.1
  63.1 2.4 %collective-permute-start.3 = (bf16[4,4,40,8,128]{4,3,2,1,0:T(8,128)(2,1)S(1)}, bf16[4,4,40,8,128]{4,3,2,1,0:T(8,128)(2,1)S(1)}, u32[]{:S(2)}, u32[]{:S(2)}) collective-permute-start(bf16[4,4,40,8,128]{4,3,2,1,0:T(8,128)(2,1)S(1)} %bitcast.9), channel_id=1, source_target_pairs={{4,0},{0,4},{5,1},{1,5},{6,2},{2,6},{7,3},{3,7},{12,8},{8,12},{13,... | collective-permute-start | bytes 3932168 | tf_op jit(solution)/shard_map/ppermute | solution.py:269
  65.6 0.0 copy-done
  65.6 0.0 copy-done.2
  65.6 0.0 copy-done.6
  65.6 0.0 copy-done.7
  65.6 0.5 shard_map.97
  66.1 2.0 %shard_map.99 = f32[4,384,128]{2,1,0:T(8,128)S(1)} custom-call(bf16[4,4,40,8,128]{4,3,2,1,0:T(8,128)(2,1)S(1)} %bitcast.10, bf16[320,256]{1,0:T(8,128)(2,1)S(1)} %bitcast.16, bf16[320,256]{1,0:T(8,128)(2,1)S(1)} %collective-permute-done.second, bf16[320,256]{1,0:T(8,128)(2,1)S(1)} %collective-permute-done.1.third, ...), custom_call_target="tpu_custom_call" | custom-call | tf_op jit(solution)/shard_map/pallas_call | solution.py:252
  68.0 1.9 %collective-permute-start.4 = (f32[4,384,128]{2,1,0:T(8,128)S(1)}, f32[4,384,128]{2,1,0:T(8,128)S(1)}, u32[]{:S(2)}, u32[]{:S(2)}) collective-permute-start(f32[4,384,128]{2,1,0:T(8,128)S(1)} %shard_map.99), channel_id=1, source_target_pairs={{4,0},{0,4},{5,1},{1,5},{6,2},{2,6},{7,3},{3,7},{12,8},{8,12},{13,... | collective-permute-start | bytes 2359304 | tf_op jit(solution)/shard_map/ppermute | solution.py:269
  70.0 0.0 collective-permute-done.3.batch
  70.0 2.0 %shard_map.98.own = f32[4,384,128]{2,1,0:T(8,128)S(1)} custom-call(bf16[4,4,40,8,128]{4,3,2,1,0:T(8,128)(2,1)S(1)} %collective-permute-done.3.batch, bf16[320,256]{1,0:T(8,128)(2,1)S(1)} %bitcast.17, bf16[320,256]{1,0:T(8,128)(2,1)S(1)} %collective-permute-done.second, bf16[320,256]{1,0:T(8,128)(2,1)S(1)} %collective-permute-done.1.third, ...), custom_call_target="tpu_custom_call" | custom-call | tf_op jit(solution)/shard_map/pallas_call | solution.py:252
  72.0 0.3 collective-permute-done.4.other
  72.2 0.1 shard_map.100
  72.3 14.4 %all_to_all.36 = f32[4,384,128]{2,1,0:T(8,128)S(1)} all-to-all(f32[4,384,128]{2,1,0:T(8,128)S(1)} %shard_map.100), channel_id=1, replica_groups=mesh['rows_z'=16,'rows_x'=4,'rows_k'=2,'cls'=4] {'rows_x'}, dimensions={0} | all-to-all | bytes 1572864 | tf_op jit(solution)/shard_map/all_to_all | solution.py:32
  86.7 0.0 copy-start.3
  86.7 16.9 %all_to_all.37 = f32[16,24,128]{2,1,0:T(8,128)S(1)} all-to-all(f32[16,24,128]{2,1,0:T(8,128)S(1)} %bitcast.23), channel_id=1, replica_groups=mesh['rows_z'=16,'rows_x'=4,'rows_k'=2,'cls'=4] {'rows_z'}, dimensions={0} | all-to-all | bytes 393216 | tf_op jit(solution)/shard_map/all_to_all | solution.py:32
  103.7 20.4 %all_to_all.38 = f32[16,24,128]{2,1,0:T(8,128)S(1)} all-to-all(f32[16,24,128]{2,1,0:T(8,128)S(1)} %broadcast_in_dim.11), channel_id=1, replica_groups=mesh['rows_z'=16,'rows_x'=4,'rows_k'=2,'cls'=4] {'rows_z'}, dimensions={0} | all-to-all | bytes 393216 | tf_op jit(solution)/shard_map/all_to_all | solution.py:28
  124.2 0.8 shard_map.101
  125.0 3.6 %all-to-all-start.5 = ((f32[4,256,128]{2,1,0:T(8,128)}), f32[4,256,128]{2,1,0:T(8,128)S(1)}, u32[]{:S(2)}, u32[]{:S(2)}) async-start(f32[4,256,128]{2,1,0:T(8,128)} %get-tuple-element.32), calls=%async_computation.5 | async-start | bytes 1048576 | tf_op jit(solution)/shard_map/all_to_all | solution.py:344
  128.6 3.3 %collective-permute-start.5 = (f32[4,32,128]{2,1,0:T(8,128)S(1)}, f32[4,32,128]{2,1,0:T(8,128)S(1)}, u32[]{:S(2)}, u32[]{:S(2)}) collective-permute-start(f32[4,32,128]{2,1,0:T(8,128)S(1)} %get-tuple-element.35.first), channel_id=1, source_target_pairs={{1,0},{2,1},{3,2},{0,3},{5,4},{6,5},{7,6},{4,7},{9,8},{10,9},{11,1... | collective-permute-start | bytes 196616 | tf_op jit(solution)/shard_map/ppermute | solution.py:269
  131.9 3.1 %collective-permute-start.6 = (f32[4,32,128]{2,1,0:T(8,128)S(1)}, f32[4,32,128]{2,1,0:T(8,128)S(1)}, u32[]{:S(2)}, u32[]{:S(2)}) collective-permute-start(f32[4,32,128]{2,1,0:T(8,128)S(1)} %get-tuple-element.35.first), channel_id=1, source_target_pairs={{2,0},{3,1},{0,2},{1,3},{6,4},{7,5},{4,6},{5,7},{10,8},{11,9},{8,1... | collective-permute-start | bytes 196616 | tf_op jit(solution)/shard_map/ppermute | solution.py:269
  135.0 1.9 %collective-permute-start.7 = (f32[4,32,128]{2,1,0:T(8,128)S(1)}, f32[4,32,128]{2,1,0:T(8,128)S(1)}, u32[]{:S(2)}, u32[]{:S(2)}) collective-permute-start(f32[4,32,128]{2,1,0:T(8,128)S(1)} %get-tuple-element.35.first), channel_id=1, source_target_pairs={{3,0},{0,1},{1,2},{2,3},{7,4},{4,5},{5,6},{6,7},{11,8},{8,9},{9,10... | collective-permute-start | bytes 196616 | tf_op jit(solution)/shard_map/ppermute | solution.py:269
  136.9 0.0 collective-permute-done.5.second
  137.0 1.5 collective-permute-done.6.third
  138.4 3.1 %collective-permute-done.7.fourth = f32[4,32,128]{2,1,0:T(8,128)S(1)} collective-permute-done((f32[4,32,128]{2,1,0:T(8,128)S(1)}, f32[4,32,128]{2,1,0:T(8,128)S(1)}, u32[]{:S(2)}, u32[]{:S(2)}) %collective-permute-start.7) | collective-permute-done | bytes 65568 | tf_op jit(solution)/shard_map/ppermute | solution.py:269
  141.5 0.0 all-to-all-done.5.own
  141.5 0.9 shard_map.102.own
  142.4 8.6 %collective-permute-start.8 = (f32[128,256]{1,0:T(8,128)S(1)}, f32[128,256]{1,0:T(8,128)S(1)}, u32[]{:S(2)}, u32[]{:S(2)}) collective-permute-start(f32[128,256]{1,0:T(8,128)S(1)} %shard_map.102.own), channel_id=1, source_target_pairs={{4,0},{0,4},{5,1},{1,5},{6,2},{2,6},{7,3},{3,7},{12,8},{8,12},{13,... | collective-permute-start | bytes 393224 | tf_op jit(solution)/shard_map/ppermute | solution.py:269
  151.1 1.0 collective-permute-done.8.other
  152.0 0.9 shard_map.103
  152.9 2.3 %collective-permute-start.9 = (f32[4,256,128]{2,1,0:T(8,128)S(1)}, f32[4,256,128]{2,1,0:T(8,128)S(1)}, u32[]{:S(2)}, u32[]{:S(2)}) collective-permute-start(f32[4,256,128]{2,1,0:T(8,128)S(1)} %all-to-all-done.5.own), channel_id=1, source_target_pairs={{4,0},{0,4},{5,1},{1,5},{6,2},{2,6},{7,3},{3,7},{12,8},{8,12},{13,... | collective-permute-start | bytes 1572872 | tf_op jit(solution)/shard_map/ppermute | solution.py:269
  155.2 4.5 %all-to-all-start.6 = ((s16[4,128,256]{2,1,0:T(8,128)(2,1)}), s16[4,128,256]{2,1,0:T(8,128)(2,1)S(1)}, u32[]{:S(2)}, u32[]{:S(2)}) async-start(s16[4,128,256]{2,1,0:T(8,128)(2,1)} %shard_map.103), calls=%async_computation.6 | async-start | bytes 524288 | tf_op jit(solution)/shard_map/all_to_all | solution.py:355
  159.7 0.0 collective-permute-done.9.other
  159.7 1.9 %shard_map.104 = (f32[250,1024]{1,0:T(8,128)}, f32[250,256]{1,0:T(8,128)S(1)}) custom-call(f32[4,256,128]{2,1,0:T(8,128)S(1)} %all-to-all-done.5.own, f32[4,256,128]{2,1,0:T(8,128)S(1)} %collective-permute-done.9.other, s32[4,1,256]{2,1,0:T(1,128)S(1)} %bitcast.19, s32[4,1,256]{2,1,0:T(1,128)S(1)} %bitcast.20, f32[250,256]{1,0:T(8,128)S(1)} %copy-done), custom_call_target="tpu_custom_call" | custom-call | tf_op jit(solution)/shard_map/pallas_call | solution.py:252
  161.6 4.1 %all-to-all-done.6 = s16[4,128,256]{2,1,0:T(8,128)(2,1)S(1)} async-done(((s16[4,128,256]{2,1,0:T(8,128)(2,1)}), s16[4,128,256]{2,1,0:T(8,128)(2,1)S(1)}, u32[]{:S(2)}, u32[]{:S(2)}) %all-to-all-start.6) | async-done | bytes 262176 | tf_op jit(solution)/shard_map/all_to_all | solution.py:355
  165.7 1.3 shard_map.105
  (12 shorter events, 0.1 us)
Async XLA Ops:
  0.6 0.7 copy-start.4
  30.0 6.9 %copy-start.1 = (bf16[256,320]{0,1:T(8,128)(2,1)S(1)}, bf16[256,320]{0,1:T(8,128)(2,1)}, u32[]{:S(2)}) copy-start(bf16[256,320]{0,1:T(8,128)(2,1)} %param.8) | copy-start | bytes 491524
  30.0 35.6 %copy-start = (f32[250,256]{1,0:T(8,128)S(1)}, f32[250,256]{1,0:T(8,128)}, u32[]{:S(2)}) copy-start(f32[250,256]{1,0:T(8,128)} %coefficients.3) | copy-start | bytes 768004
  30.0 35.6 %copy-start.2 = (f32[64,512]{1,0:T(8,128)S(1)}, f32[64,512]{1,0:T(8,128)}, u32[]{:S(2)}) copy-start(f32[64,512]{1,0:T(8,128)} %vectors.1) | copy-start | bytes 393220
  30.0 35.6 %copy-start.6 = (f32[512]{0:T(512)S(1)}, f32[512]{0:T(512)}, u32[]{:S(2)}) copy-start(f32[512]{0:T(512)} %param.15) | copy-start | bytes 6148
  30.0 35.6 %copy-start.7 = (s32[64]{0:T(128)S(1)}, s32[64]{0:T(128)}, u32[]{:S(2)}) copy-start(s32[64]{0:T(128)} %param.13) | copy-start | bytes 772
  30.0 33.1 %all-to-all-start.1 = ((bf16[16,40,8,128]{3,2,1,0:T(8,128)(2,1)}), bf16[16,40,8,128]{3,2,1,0:T(8,128)(2,1)S(1)}, u32[]{:S(2)}, u32[]{:S(2)}) async-start(bf16[16,40,8,128]{3,2,1,0:T(8,128)(2,1)} %shard_map.96), calls=%async_computation.1 | async-start | bytes 2621440 | tf_op jit(solution)/shard_map/all_to_all | solution.py:314
  36.9 20.6 %collective-permute-start = (bf16[320,256]{1,0:T(8,128)(2,1)S(1)}, bf16[320,256]{1,0:T(8,128)(2,1)S(1)}, u32[]{:S(2)}, u32[]{:S(2)}) collective-permute-start(bf16[320,256]{1,0:T(8,128)(2,1)S(1)} %bitcast.13), channel_id=1, source_target_pairs={{1,0},{2,1},{3,2},{0,3},{5,4},{6,5},{7,6},{4,7},{9,8},{10,9},{11,1... | collective-permute-start | bytes 491528 | tf_op jit(solution)/shard_map/ppermute | solution.py:269
  41.4 18.8 %collective-permute-start.1 = (bf16[320,256]{1,0:T(8,128)(2,1)S(1)}, bf16[320,256]{1,0:T(8,128)(2,1)S(1)}, u32[]{:S(2)}, u32[]{:S(2)}) collective-permute-start(bf16[320,256]{1,0:T(8,128)(2,1)S(1)} %bitcast.14), channel_id=1, source_target_pairs={{2,0},{3,1},{0,2},{1,3},{6,4},{7,5},{4,6},{5,7},{10,8},{11,9},{8,1... | collective-permute-start | bytes 491528 | tf_op jit(solution)/shard_map/ppermute | solution.py:269
  43.9 19.2 %collective-permute-start.2 = (bf16[320,256]{1,0:T(8,128)(2,1)S(1)}, bf16[320,256]{1,0:T(8,128)(2,1)S(1)}, u32[]{:S(2)}, u32[]{:S(2)}) collective-permute-start(bf16[320,256]{1,0:T(8,128)(2,1)S(1)} %bitcast.15), channel_id=1, source_target_pairs={{3,0},{0,1},{1,2},{2,3},{7,4},{4,5},{5,6},{6,7},{11,8},{8,9},{9,10... | collective-permute-start | bytes 491528 | tf_op jit(solution)/shard_map/ppermute | solution.py:269
  63.1 6.8 %collective-permute-start.3 = (bf16[4,4,40,8,128]{4,3,2,1,0:T(8,128)(2,1)S(1)}, bf16[4,4,40,8,128]{4,3,2,1,0:T(8,128)(2,1)S(1)}, u32[]{:S(2)}, u32[]{:S(2)}) collective-permute-start(bf16[4,4,40,8,128]{4,3,2,1,0:T(8,128)(2,1)S(1)} %bitcast.9), channel_id=1, source_target_pairs={{4,0},{0,4},{5,1},{1,5},{6,2},{2,6},{7,3},{3,7},{12,8},{8,12},{13,... | collective-permute-start | bytes 3932168 | tf_op jit(solution)/shard_map/ppermute | solution.py:269
  68.0 4.2 %collective-permute-start.4 = (f32[4,384,128]{2,1,0:T(8,128)S(1)}, f32[4,384,128]{2,1,0:T(8,128)S(1)}, u32[]{:S(2)}, u32[]{:S(2)}) collective-permute-start(f32[4,384,128]{2,1,0:T(8,128)S(1)} %shard_map.99), channel_id=1, source_target_pairs={{4,0},{0,4},{5,1},{1,5},{6,2},{2,6},{7,3},{3,7},{12,8},{8,12},{13,... | collective-permute-start | bytes 2359304 | tf_op jit(solution)/shard_map/ppermute | solution.py:269
  86.7 54.8 %copy-start.3 = (s32[1024]{0:T(1024)S(1)}, s32[1024]{0:T(1024)}, u32[]{:S(2)}) copy-start(s32[1024]{0:T(1024)} %param.11) | copy-start | bytes 12292
  125.0 34.7 %copy-start.5 = (s32[1024]{0:T(1024)S(1)}, s32[1024]{0:T(1024)}, u32[]{:S(2)}) copy-start(s32[1024]{0:T(1024)} %param.12) | copy-start | bytes 12292
  125.0 16.5 %all-to-all-start.5 = ((f32[4,256,128]{2,1,0:T(8,128)}), f32[4,256,128]{2,1,0:T(8,128)S(1)}, u32[]{:S(2)}, u32[]{:S(2)}) async-start(f32[4,256,128]{2,1,0:T(8,128)} %get-tuple-element.32), calls=%async_computation.5 | async-start | bytes 1048576 | tf_op jit(solution)/shard_map/all_to_all | solution.py:344
  128.6 8.3 %collective-permute-start.5 = (f32[4,32,128]{2,1,0:T(8,128)S(1)}, f32[4,32,128]{2,1,0:T(8,128)S(1)}, u32[]{:S(2)}, u32[]{:S(2)}) collective-permute-start(f32[4,32,128]{2,1,0:T(8,128)S(1)} %get-tuple-element.35.first), channel_id=1, source_target_pairs={{1,0},{2,1},{3,2},{0,3},{5,4},{6,5},{7,6},{4,7},{9,8},{10,9},{11,1... | collective-permute-start | bytes 196616 | tf_op jit(solution)/shard_map/ppermute | solution.py:269
  131.9 6.5 %collective-permute-start.6 = (f32[4,32,128]{2,1,0:T(8,128)S(1)}, f32[4,32,128]{2,1,0:T(8,128)S(1)}, u32[]{:S(2)}, u32[]{:S(2)}) collective-permute-start(f32[4,32,128]{2,1,0:T(8,128)S(1)} %get-tuple-element.35.first), channel_id=1, source_target_pairs={{2,0},{3,1},{0,2},{1,3},{6,4},{7,5},{4,6},{5,7},{10,8},{11,9},{8,1... | collective-permute-start | bytes 196616 | tf_op jit(solution)/shard_map/ppermute | solution.py:269
  135.0 6.5 %collective-permute-start.7 = (f32[4,32,128]{2,1,0:T(8,128)S(1)}, f32[4,32,128]{2,1,0:T(8,128)S(1)}, u32[]{:S(2)}, u32[]{:S(2)}) collective-permute-start(f32[4,32,128]{2,1,0:T(8,128)S(1)} %get-tuple-element.35.first), channel_id=1, source_target_pairs={{3,0},{0,1},{1,2},{2,3},{7,4},{4,5},{5,6},{6,7},{11,8},{8,9},{9,10... | collective-permute-start | bytes 196616 | tf_op jit(solution)/shard_map/ppermute | solution.py:269
  142.4 9.6 %collective-permute-start.8 = (f32[128,256]{1,0:T(8,128)S(1)}, f32[128,256]{1,0:T(8,128)S(1)}, u32[]{:S(2)}, u32[]{:S(2)}) collective-permute-start(f32[128,256]{1,0:T(8,128)S(1)} %shard_map.102.own), channel_id=1, source_target_pairs={{4,0},{0,4},{5,1},{1,5},{6,2},{2,6},{7,3},{3,7},{12,8},{8,12},{13,... | collective-permute-start | bytes 393224 | tf_op jit(solution)/shard_map/ppermute | solution.py:269
  152.9 6.7 %collective-permute-start.9 = (f32[4,256,128]{2,1,0:T(8,128)S(1)}, f32[4,256,128]{2,1,0:T(8,128)S(1)}, u32[]{:S(2)}, u32[]{:S(2)}) collective-permute-start(f32[4,256,128]{2,1,0:T(8,128)S(1)} %all-to-all-done.5.own), channel_id=1, source_target_pairs={{4,0},{0,4},{5,1},{1,5},{6,2},{2,6},{7,3},{3,7},{12,8},{8,12},{13,... | collective-permute-start | bytes 1572872 | tf_op jit(solution)/shard_map/ppermute | solution.py:269
  155.2 10.5 %all-to-all-start.6 = ((s16[4,128,256]{2,1,0:T(8,128)(2,1)}), s16[4,128,256]{2,1,0:T(8,128)(2,1)S(1)}, u32[]{:S(2)}, u32[]{:S(2)}) async-start(s16[4,128,256]{2,1,0:T(8,128)(2,1)} %shard_map.103), calls=%async_computation.6 | async-start | bytes 524288 | tf_op jit(solution)/shard_map/all_to_all | solution.py:355

commit v9 on v8

--- a/solution.py
+++ b/solution.py
@@ -266,7 +266,8 @@
     size = lax.axis_size(axis)
     pieces = [value]
     for s in range(1, size):
-        pieces.append(lax.ppermute(value, axis, [((d + s) % size, d) for d in range(size)]))
+        pairs = [((d + s) % size, d) for d in range(size)]
+        pieces.append(lax.ppermute(value, axis, pairs))
     return pieces + [value] * (4 - size)
 
 
@@ -301,7 +302,7 @@
         0,
         tiled=True,
     )
-    batch_own, turned = lax.optimization_barrier((batch_own, centers.T))
+    turned = centers.T
     center_pieces = from_others(turned, Y)
     rows, width = batch_features.shape
     granules = (depth * (2 * width // LANES) // 2, rows, LANES)
@@ -312,10 +313,6 @@
         limit=2,
     )(batch_own)
     batch_own = lax.all_to_all(copies, (X, Y), 0, 0, tiled=True)
-    batch_own, center_pieces = lax.optimization_barrier((batch_own, center_pieces))
-    batch_own = batch_own.reshape(chips, groups, *granules)
-    batch_other = from_others(batch_own, K)[1]
-
     high, low, weights = kernel(
         lift,
         (
@@ -326,6 +323,12 @@
         (pltpu.VMEM((lines, count), jnp.float32),),
         limit=6,
     )(eigen_vectors, eigen_scale[None], subset_index[None], coefficients)
+    batch_own, center_pieces, high, low, weights = lax.optimization_barrier(
+        (batch_own, center_pieces, high, low, weights)
+    )
+    batch_own = batch_own.reshape(chips, groups, *granules)
+    batch_other = from_others(batch_own, K)[1]
+
     labels = batch_labels.reshape(chips, 1, 2 * LANES)
     index = batch_index.reshape(chips, 1, 2 * LANES)
 

time: 168 us -> 168 us (level)
  no operation moved by 1% of the time
where the time goes in v9:
time: 168 us; the launch traced here: 167 us
  blocking collectives  79.2 us (47%)
  starting transfers between devices  47.9 us (29%)
  waiting for transfers between devices  26.2 us (16%)
  Pallas kernels  11.6 us (7%)
    ppermute x10, starting transfers between devices, from_others(): pieces.append(lax.ppermute(value, axis, pairs))  33 us
    all_to_all x2, blocking collectives, scattered(): return jnp.sum(lax.all_to_all(tiles, axis, 0, 0, tiled=True), axis=0)  31.3 us
    all_to_all x1, blocking collectives, shards(): lax.all_to_all(kernel(fan, jax.ShapeDtypeStruct((depth, *batch_features.s...  27.4 us
    ppermute x10, waiting for transfers between devices, from_others(): pieces.append(lax.ppermute(value, axis, pairs))  22 us
    all_to_all x1, blocking collectives, gathered(): return lax.all_to_all(copies, axis, 0, 0, tiled=True)  20.4 us
    pallas_call x11, Pallas kernels, call(): pl.pallas_call(functools.partial(body, **settings), out_shape=outs, in_sp...  11.6 us
    all_to_all x1, starting transfers between devices, shards(): batch_own = lax.all_to_all(copies, (X, Y), 0, 0, tiled=True)  6.9 us
    all_to_all x1, starting transfers between devices, shards(): lax.all_to_all(copies, X, 0, 0, tiled=True).reshape(vectors, padded)  4.48 us
  transfers between devices with their start and end apart: 13, of which 8 were waited for; matrix products, arithmetic and copies ran while one was open for 0% of the time, Pallas kernels for 4%

profile of v9, /device:TPU:1, one launch (start us, length us, event | category | flops | bytes accessed | tf_op | source)
XLA Modules:
  0.0 166.5 jit_solution(13608621798216948668)
XLA Ops:
  0.6 0.7 copy-done.4
  1.3 27.4 %all_to_all.35.batch = bf16[16,8,320]{2,1,0:T(8,128)(2,1)S(1)} all-to-all(bf16[16,8,320]{2,1,0:T(8,128)(2,1)S(1)} %shard_map.95), channel_id=1, replica_groups=mesh['rows_z'=16,'rows_x'=4,'rows_k'=2,'cls'=4] {'rows_z'}, dimensions={0} | all-to-all | bytes 163840 | tf_op jit(solution)/shard_map/all_to_all | solution.py:296
  28.7 1.3 shard_map.96
  30.0 0.0 copy-start.7
  30.0 6.9 %all-to-all-start.1 = ((bf16[16,40,8,128]{3,2,1,0:T(8,128)(2,1)}), bf16[16,40,8,128]{3,2,1,0:T(8,128)(2,1)S(1)}, u32[]{:S(2)}, u32[]{:S(2)}) async-start(bf16[16,40,8,128]{3,2,1,0:T(8,128)(2,1)} %shard_map.96), calls=%async_computation.1 | async-start | bytes 2621440 | tf_op jit(solution)/shard_map/all_to_all | solution.py:315
  36.9 0.0 copy-done.1
  36.9 4.5 %collective-permute-start = (bf16[320,256]{1,0:T(8,128)(2,1)S(1)}, bf16[320,256]{1,0:T(8,128)(2,1)S(1)}, u32[]{:S(2)}, u32[]{:S(2)}) collective-permute-start(bf16[320,256]{1,0:T(8,128)(2,1)S(1)} %bitcast.13), channel_id=1, source_target_pairs={{1,0},{2,1},{3,2},{0,3},{5,4},{6,5},{7,6},{4,7},{9,8},{10,9},{11,1... | collective-permute-start | bytes 491528 | tf_op jit(solution)/shard_map/ppermute | solution.py:270
  41.4 2.5 %collective-permute-start.1 = (bf16[320,256]{1,0:T(8,128)(2,1)S(1)}, bf16[320,256]{1,0:T(8,128)(2,1)S(1)}, u32[]{:S(2)}, u32[]{:S(2)}) collective-permute-start(bf16[320,256]{1,0:T(8,128)(2,1)S(1)} %bitcast.14), channel_id=1, source_target_pairs={{2,0},{3,1},{0,2},{1,3},{6,4},{7,5},{4,6},{5,7},{10,8},{11,9},{8,1... | collective-permute-start | bytes 491528 | tf_op jit(solution)/shard_map/ppermute | solution.py:270
  43.9 2.5 %collective-permute-start.2 = (bf16[320,256]{1,0:T(8,128)(2,1)S(1)}, bf16[320,256]{1,0:T(8,128)(2,1)S(1)}, u32[]{:S(2)}, u32[]{:S(2)}) collective-permute-start(bf16[320,256]{1,0:T(8,128)(2,1)S(1)} %bitcast.15), channel_id=1, source_target_pairs={{3,0},{0,1},{1,2},{2,3},{7,4},{4,5},{5,6},{6,7},{11,8},{8,9},{9,10... | collective-permute-start | bytes 491528 | tf_op jit(solution)/shard_map/ppermute | solution.py:270
  46.4 0.0 copy-done
  46.4 0.0 copy-done.2
  46.4 0.0 copy-done.6
  46.4 0.0 copy-done.7
  46.5 0.5 shard_map.97
  46.9 10.6 %collective-permute-done.second = bf16[320,256]{1,0:T(8,128)(2,1)S(1)} collective-permute-done((bf16[320,256]{1,0:T(8,128)(2,1)S(1)}, bf16[320,256]{1,0:T(8,128)(2,1)S(1)}, u32[]{:S(2)}, u32[]{:S(2)}) %collective-permute-start) | collective-permute-done | bytes 163872 | tf_op jit(solution)/shard_map/ppermute | solution.py:270
  57.6 2.7 %collective-permute-done.1.third = bf16[320,256]{1,0:T(8,128)(2,1)S(1)} collective-permute-done((bf16[320,256]{1,0:T(8,128)(2,1)S(1)}, bf16[320,256]{1,0:T(8,128)(2,1)S(1)}, u32[]{:S(2)}, u32[]{:S(2)}) %collective-permute-start.1) | collective-permute-done | bytes 163872 | tf_op jit(solution)/shard_map/ppermute | solution.py:270
  60.2 2.9 %collective-permute-done.2.fourth = bf16[320,256]{1,0:T(8,128)(2,1)S(1)} collective-permute-done((bf16[320,256]{1,0:T(8,128)(2,1)S(1)}, bf16[320,256]{1,0:T(8,128)(2,1)S(1)}, u32[]{:S(2)}, u32[]{:S(2)}) %collective-permute-start.2) | collective-permute-done | bytes 163872 | tf_op jit(solution)/shard_map/ppermute | solution.py:270
  63.1 0.0 all-to-all-done.1
  63.1 2.4 %collective-permute-start.3 = (bf16[4,4,40,8,128]{4,3,2,1,0:T(8,128)(2,1)S(1)}, bf16[4,4,40,8,128]{4,3,2,1,0:T(8,128)(2,1)S(1)}, u32[]{:S(2)}, u32[]{:S(2)}) collective-permute-start(bf16[4,4,40,8,128]{4,3,2,1,0:T(8,128)(2,1)S(1)} %bitcast.9), channel_id=1, source_target_pairs={{4,0},{0,4},{5,1},{1,5},{6,2},{2,6},{7,3},{3,7},{12,8},{8,12},{13,... | collective-permute-start | bytes 3932168 | tf_op jit(solution)/shard_map/ppermute | solution.py:270
  65.6 2.0 %shard_map.99 = f32[4,384,128]{2,1,0:T(8,128)S(1)} custom-call(bf16[4,4,40,8,128]{4,3,2,1,0:T(8,128)(2,1)S(1)} %bitcast.10, bf16[320,256]{1,0:T(8,128)(2,1)S(1)} %bitcast.16, bf16[320,256]{1,0:T(8,128)(2,1)S(1)} %collective-permute-done.second, bf16[320,256]{1,0:T(8,128)(2,1)S(1)} %collective-permute-done.1.third, ...), custom_call_target="tpu_custom_call" | custom-call | tf_op jit(solution)/shard_map/pallas_call | solution.py:252
  67.5 1.9 %collective-permute-start.4 = (f32[4,384,128]{2,1,0:T(8,128)S(1)}, f32[4,384,128]{2,1,0:T(8,128)S(1)}, u32[]{:S(2)}, u32[]{:S(2)}) collective-permute-start(f32[4,384,128]{2,1,0:T(8,128)S(1)} %shard_map.99), channel_id=1, source_target_pairs={{4,0},{0,4},{5,1},{1,5},{6,2},{2,6},{7,3},{3,7},{12,8},{8,12},{13,... | collective-permute-start | bytes 2359304 | tf_op jit(solution)/shard_map/ppermute | solution.py:270
  69.5 0.0 collective-permute-done.3.batch
  69.5 2.0 %shard_map.98.own = f32[4,384,128]{2,1,0:T(8,128)S(1)} custom-call(bf16[4,4,40,8,128]{4,3,2,1,0:T(8,128)(2,1)S(1)} %collective-permute-done.3.batch, bf16[320,256]{1,0:T(8,128)(2,1)S(1)} %bitcast.17, bf16[320,256]{1,0:T(8,128)(2,1)S(1)} %collective-permute-done.second, bf16[320,256]{1,0:T(8,128)(2,1)S(1)} %collective-permute-done.1.third, ...), custom_call_target="tpu_custom_call" | custom-call | tf_op jit(solution)/shard_map/pallas_call | solution.py:252
  71.5 0.3 collective-permute-done.4.other
  71.7 0.1 shard_map.100
  71.8 14.4 %all_to_all.36 = f32[4,384,128]{2,1,0:T(8,128)S(1)} all-to-all(f32[4,384,128]{2,1,0:T(8,128)S(1)} %shard_map.100), channel_id=1, replica_groups=mesh['rows_z'=16,'rows_x'=4,'rows_k'=2,'cls'=4] {'rows_x'}, dimensions={0} | all-to-all | bytes 1572864 | tf_op jit(solution)/shard_map/all_to_all | solution.py:32
  86.2 0.0 copy-start.3
  86.2 16.9 %all_to_all.37 = f32[16,24,128]{2,1,0:T(8,128)S(1)} all-to-all(f32[16,24,128]{2,1,0:T(8,128)S(1)} %bitcast.23), channel_id=1, replica_groups=mesh['rows_z'=16,'rows_x'=4,'rows_k'=2,'cls'=4] {'rows_z'}, dimensions={0} | all-to-all | bytes 393216 | tf_op jit(solution)/shard_map/all_to_all | solution.py:32
  103.2 20.4 %all_to_all.38 = f32[16,24,128]{2,1,0:T(8,128)S(1)} all-to-all(f32[16,24,128]{2,1,0:T(8,128)S(1)} %broadcast_in_dim.11), channel_id=1, replica_groups=mesh['rows_z'=16,'rows_x'=4,'rows_k'=2,'cls'=4] {'rows_z'}, dimensions={0} | all-to-all | bytes 393216 | tf_op jit(solution)/shard_map/all_to_all | solution.py:28
  123.7 0.8 shard_map.101
  124.5 3.6 %all-to-all-start.5 = ((f32[4,256,128]{2,1,0:T(8,128)}), f32[4,256,128]{2,1,0:T(8,128)S(1)}, u32[]{:S(2)}, u32[]{:S(2)}) async-start(f32[4,256,128]{2,1,0:T(8,128)} %get-tuple-element.34), calls=%async_computation.5 | async-start | bytes 1048576 | tf_op jit(solution)/shard_map/all_to_all | solution.py:347
  128.1 3.3 %collective-permute-start.5 = (f32[4,32,128]{2,1,0:T(8,128)S(1)}, f32[4,32,128]{2,1,0:T(8,128)S(1)}, u32[]{:S(2)}, u32[]{:S(2)}) collective-permute-start(f32[4,32,128]{2,1,0:T(8,128)S(1)} %get-tuple-element.37.first), channel_id=1, source_target_pairs={{1,0},{2,1},{3,2},{0,3},{5,4},{6,5},{7,6},{4,7},{9,8},{10,9},{11,1... | collective-permute-start | bytes 196616 | tf_op jit(solution)/shard_map/ppermute | solution.py:270
  131.4 3.1 %collective-permute-start.6 = (f32[4,32,128]{2,1,0:T(8,128)S(1)}, f32[4,32,128]{2,1,0:T(8,128)S(1)}, u32[]{:S(2)}, u32[]{:S(2)}) collective-permute-start(f32[4,32,128]{2,1,0:T(8,128)S(1)} %get-tuple-element.37.first), channel_id=1, source_target_pairs={{2,0},{3,1},{0,2},{1,3},{6,4},{7,5},{4,6},{5,7},{10,8},{11,9},{8,1... | collective-permute-start | bytes 196616 | tf_op jit(solution)/shard_map/ppermute | solution.py:270
  134.5 1.9 %collective-permute-start.7 = (f32[4,32,128]{2,1,0:T(8,128)S(1)}, f32[4,32,128]{2,1,0:T(8,128)S(1)}, u32[]{:S(2)}, u32[]{:S(2)}) collective-permute-start(f32[4,32,128]{2,1,0:T(8,128)S(1)} %get-tuple-element.37.first), channel_id=1, source_target_pairs={{3,0},{0,1},{1,2},{2,3},{7,4},{4,5},{5,6},{6,7},{11,8},{8,9},{9,10... | collective-permute-start | bytes 196616 | tf_op jit(solution)/shard_map/ppermute | solution.py:270
  136.4 0.0 collective-permute-done.5.second
  136.4 1.5 collective-permute-done.6.third
  137.9 3.1 %collective-permute-done.7.fourth = f32[4,32,128]{2,1,0:T(8,128)S(1)} collective-permute-done((f32[4,32,128]{2,1,0:T(8,128)S(1)}, f32[4,32,128]{2,1,0:T(8,128)S(1)}, u32[]{:S(2)}, u32[]{:S(2)}) %collective-permute-start.7) | collective-permute-done | bytes 65568 | tf_op jit(solution)/shard_map/ppermute | solution.py:270
  141.0 0.0 all-to-all-done.5.own
  141.0 0.9 shard_map.102.own
  141.9 8.6 %collective-permute-start.8 = (f32[128,256]{1,0:T(8,128)S(1)}, f32[128,256]{1,0:T(8,128)S(1)}, u32[]{:S(2)}, u32[]{:S(2)}) collective-permute-start(f32[128,256]{1,0:T(8,128)S(1)} %shard_map.102.own), channel_id=1, source_target_pairs={{4,0},{0,4},{5,1},{1,5},{6,2},{2,6},{7,3},{3,7},{12,8},{8,12},{13,... | collective-permute-start | bytes 393224 | tf_op jit(solution)/shard_map/ppermute | solution.py:270
  150.6 1.0 collective-permute-done.8.other
  151.5 0.9 shard_map.103
  152.4 2.3 %collective-permute-start.9 = (f32[4,256,128]{2,1,0:T(8,128)S(1)}, f32[4,256,128]{2,1,0:T(8,128)S(1)}, u32[]{:S(2)}, u32[]{:S(2)}) collective-permute-start(f32[4,256,128]{2,1,0:T(8,128)S(1)} %all-to-all-done.5.own), channel_id=1, source_target_pairs={{4,0},{0,4},{5,1},{1,5},{6,2},{2,6},{7,3},{3,7},{12,8},{8,12},{13,... | collective-permute-start | bytes 1572872 | tf_op jit(solution)/shard_map/ppermute | solution.py:270
  154.7 4.5 %all-to-all-start.6 = ((s16[4,128,256]{2,1,0:T(8,128)(2,1)}), s16[4,128,256]{2,1,0:T(8,128)(2,1)S(1)}, u32[]{:S(2)}, u32[]{:S(2)}) async-start(s16[4,128,256]{2,1,0:T(8,128)(2,1)} %shard_map.103), calls=%async_computation.6 | async-start | bytes 524288 | tf_op jit(solution)/shard_map/all_to_all | solution.py:358
  159.2 0.0 collective-permute-done.9.other
  159.2 1.9 %shard_map.104 = (f32[250,1024]{1,0:T(8,128)}, f32[250,256]{1,0:T(8,128)S(1)}) custom-call(f32[4,256,128]{2,1,0:T(8,128)S(1)} %all-to-all-done.5.own, f32[4,256,128]{2,1,0:T(8,128)S(1)} %collective-permute-done.9.other, s32[4,1,256]{2,1,0:T(1,128)S(1)} %bitcast.19, s32[4,1,256]{2,1,0:T(1,128)S(1)} %bitcast.20, f32[250,256]{1,0:T(8,128)S(1)} %copy-done), custom_call_target="tpu_custom_call" | custom-call | tf_op jit(solution)/shard_map/pallas_call | solution.py:252
  161.1 4.1 %all-to-all-done.6 = s16[4,128,256]{2,1,0:T(8,128)(2,1)S(1)} async-done(((s16[4,128,256]{2,1,0:T(8,128)(2,1)}), s16[4,128,256]{2,1,0:T(8,128)(2,1)S(1)}, u32[]{:S(2)}, u32[]{:S(2)}) %all-to-all-start.6) | async-done | bytes 262176 | tf_op jit(solution)/shard_map/all_to_all | solution.py:358
  165.2 1.3 shard_map.105
  (12 shorter events, 0.1 us)
Async XLA Ops:
  0.6 0.7 copy-start.4
  30.0 6.9 %copy-start.1 = (bf16[256,320]{0,1:T(8,128)(2,1)S(1)}, bf16[256,320]{0,1:T(8,128)(2,1)}, u32[]{:S(2)}) copy-start(bf16[256,320]{0,1:T(8,128)(2,1)} %param.8) | copy-start | bytes 491524
  30.0 16.4 %copy-start = (f32[250,256]{1,0:T(8,128)S(1)}, f32[250,256]{1,0:T(8,128)}, u32[]{:S(2)}) copy-start(f32[250,256]{1,0:T(8,128)} %coefficients.3) | copy-start | bytes 768004
  30.0 16.4 %copy-start.2 = (f32[64,512]{1,0:T(8,128)S(1)}, f32[64,512]{1,0:T(8,128)}, u32[]{:S(2)}) copy-start(f32[64,512]{1,0:T(8,128)} %vectors.1) | copy-start | bytes 393220
  30.0 16.4 %copy-start.6 = (f32[512]{0:T(512)S(1)}, f32[512]{0:T(512)}, u32[]{:S(2)}) copy-start(f32[512]{0:T(512)} %param.15) | copy-start | bytes 6148
  30.0 16.4 %copy-start.7 = (s32[64]{0:T(128)S(1)}, s32[64]{0:T(128)}, u32[]{:S(2)}) copy-start(s32[64]{0:T(128)} %param.13) | copy-start | bytes 772
  30.0 33.1 %all-to-all-start.1 = ((bf16[16,40,8,128]{3,2,1,0:T(8,128)(2,1)}), bf16[16,40,8,128]{3,2,1,0:T(8,128)(2,1)S(1)}, u32[]{:S(2)}, u32[]{:S(2)}) async-start(bf16[16,40,8,128]{3,2,1,0:T(8,128)(2,1)} %shard_map.96), calls=%async_computation.1 | async-start | bytes 2621440 | tf_op jit(solution)/shard_map/all_to_all | solution.py:315
  36.9 20.6 %collective-permute-start = (bf16[320,256]{1,0:T(8,128)(2,1)S(1)}, bf16[320,256]{1,0:T(8,128)(2,1)S(1)}, u32[]{:S(2)}, u32[]{:S(2)}) collective-permute-start(bf16[320,256]{1,0:T(8,128)(2,1)S(1)} %bitcast.13), channel_id=1, source_target_pairs={{1,0},{2,1},{3,2},{0,3},{5,4},{6,5},{7,6},{4,7},{9,8},{10,9},{11,1... | collective-permute-start | bytes 491528 | tf_op jit(solution)/shard_map/ppermute | solution.py:270
  41.4 18.8 %collective-permute-start.1 = (bf16[320,256]{1,0:T(8,128)(2,1)S(1)}, bf16[320,256]{1,0:T(8,128)(2,1)S(1)}, u32[]{:S(2)}, u32[]{:S(2)}) collective-permute-start(bf16[320,256]{1,0:T(8,128)(2,1)S(1)} %bitcast.14), channel_id=1, source_target_pairs={{2,0},{3,1},{0,2},{1,3},{6,4},{7,5},{4,6},{5,7},{10,8},{11,9},{8,1... | collective-permute-start | bytes 491528 | tf_op jit(solution)/shard_map/ppermute | solution.py:270
  43.9 19.2 %collective-permute-start.2 = (bf16[320,256]{1,0:T(8,128)(2,1)S(1)}, bf16[320,256]{1,0:T(8,128)(2,1)S(1)}, u32[]{:S(2)}, u32[]{:S(2)}) collective-permute-start(bf16[320,256]{1,0:T(8,128)(2,1)S(1)} %bitcast.15), channel_id=1, source_target_pairs={{3,0},{0,1},{1,2},{2,3},{7,4},{4,5},{5,6},{6,7},{11,8},{8,9},{9,10... | collective-permute-start | bytes 491528 | tf_op jit(solution)/shard_map/ppermute | solution.py:270
  63.1 6.3 %collective-permute-start.3 = (bf16[4,4,40,8,128]{4,3,2,1,0:T(8,128)(2,1)S(1)}, bf16[4,4,40,8,128]{4,3,2,1,0:T(8,128)(2,1)S(1)}, u32[]{:S(2)}, u32[]{:S(2)}) collective-permute-start(bf16[4,4,40,8,128]{4,3,2,1,0:T(8,128)(2,1)S(1)} %bitcast.9), channel_id=1, source_target_pairs={{4,0},{0,4},{5,1},{1,5},{6,2},{2,6},{7,3},{3,7},{12,8},{8,12},{13,... | collective-permute-start | bytes 3932168 | tf_op jit(solution)/shard_map/ppermute | solution.py:270
  67.5 4.2 %collective-permute-start.4 = (f32[4,384,128]{2,1,0:T(8,128)S(1)}, f32[4,384,128]{2,1,0:T(8,128)S(1)}, u32[]{:S(2)}, u32[]{:S(2)}) collective-permute-start(f32[4,384,128]{2,1,0:T(8,128)S(1)} %shard_map.99), channel_id=1, source_target_pairs={{4,0},{0,4},{5,1},{1,5},{6,2},{2,6},{7,3},{3,7},{12,8},{8,12},{13,... | collective-permute-start | bytes 2359304 | tf_op jit(solution)/shard_map/ppermute | solution.py:270
  86.2 54.8 %copy-start.3 = (s32[1024]{0:T(1024)S(1)}, s32[1024]{0:T(1024)}, u32[]{:S(2)}) copy-start(s32[1024]{0:T(1024)} %param.11) | copy-start | bytes 12292
  124.5 34.7 %copy-start.5 = (s32[1024]{0:T(1024)S(1)}, s32[1024]{0:T(1024)}, u32[]{:S(2)}) copy-start(s32[1024]{0:T(1024)} %param.12) | copy-start | bytes 12292
  124.5 16.5 %all-to-all-start.5 = ((f32[4,256,128]{2,1,0:T(8,128)}), f32[4,256,128]{2,1,0:T(8,128)S(1)}, u32[]{:S(2)}, u32[]{:S(2)}) async-start(f32[4,256,128]{2,1,0:T(8,128)} %get-tuple-element.34), calls=%async_computation.5 | async-start | bytes 1048576 | tf_op jit(solution)/shard_map/all_to_all | solution.py:347
  128.1 8.3 %collective-permute-start.5 = (f32[4,32,128]{2,1,0:T(8,128)S(1)}, f32[4,32,128]{2,1,0:T(8,128)S(1)}, u32[]{:S(2)}, u32[]{:S(2)}) collective-permute-start(f32[4,32,128]{2,1,0:T(8,128)S(1)} %get-tuple-element.37.first), channel_id=1, source_target_pairs={{1,0},{2,1},{3,2},{0,3},{5,4},{6,5},{7,6},{4,7},{9,8},{10,9},{11,1... | collective-permute-start | bytes 196616 | tf_op jit(solution)/shard_map/ppermute | solution.py:270
  131.4 6.5 %collective-permute-start.6 = (f32[4,32,128]{2,1,0:T(8,128)S(1)}, f32[4,32,128]{2,1,0:T(8,128)S(1)}, u32[]{:S(2)}, u32[]{:S(2)}) collective-permute-start(f32[4,32,128]{2,1,0:T(8,128)S(1)} %get-tuple-element.37.first), channel_id=1, source_target_pairs={{2,0},{3,1},{0,2},{1,3},{6,4},{7,5},{4,6},{5,7},{10,8},{11,9},{8,1... | collective-permute-start | bytes 196616 | tf_op jit(solution)/shard_map/ppermute | solution.py:270
  134.5 6.5 %collective-permute-start.7 = (f32[4,32,128]{2,1,0:T(8,128)S(1)}, f32[4,32,128]{2,1,0:T(8,128)S(1)}, u32[]{:S(2)}, u32[]{:S(2)}) collective-permute-start(f32[4,32,128]{2,1,0:T(8,128)S(1)} %get-tuple-element.37.first), channel_id=1, source_target_pairs={{3,0},{0,1},{1,2},{2,3},{7,4},{4,5},{5,6},{6,7},{11,8},{8,9},{9,10... | collective-permute-start | bytes 196616 | tf_op jit(solution)/shard_map/ppermute | solution.py:270
  141.9 9.6 %collective-permute-start.8 = (f32[128,256]{1,0:T(8,128)S(1)}, f32[128,256]{1,0:T(8,128)S(1)}, u32[]{:S(2)}, u32[]{:S(2)}) collective-permute-start(f32[128,256]{1,0:T(8,128)S(1)} %shard_map.102.own), channel_id=1, source_target_pairs={{4,0},{0,4},{5,1},{1,5},{6,2},{2,6},{7,3},{3,7},{12,8},{8,12},{13,... | collective-permute-start | bytes 393224 | tf_op jit(solution)/shard_map/ppermute | solution.py:270
  152.4 6.8 %collective-permute-start.9 = (f32[4,256,128]{2,1,0:T(8,128)S(1)}, f32[4,256,128]{2,1,0:T(8,128)S(1)}, u32[]{:S(2)}, u32[]{:S(2)}) collective-permute-start(f32[4,256,128]{2,1,0:T(8,128)S(1)} %all-to-all-done.5.own), channel_id=1, source_target_pairs={{4,0},{0,4},{5,1},{1,5},{6,2},{2,6},{7,3},{3,7},{12,8},{8,12},{13,... | collective-permute-start | bytes 1572872 | tf_op jit(solution)/shard_map/ppermute | solution.py:270
  154.7 10.5 %all-to-all-start.6 = ((s16[4,128,256]{2,1,0:T(8,128)(2,1)}), s16[4,128,256]{2,1,0:T(8,128)(2,1)S(1)}, u32[]{:S(2)}, u32[]{:S(2)}) async-start(s16[4,128,256]{2,1,0:T(8,128)(2,1)} %shard_map.103), calls=%async_computation.6 | async-start | bytes 524288 | tf_op jit(solution)/shard_map/all_to_all | solution.py:358

commit v10 on v9

--- a/solution.py
+++ b/solution.py
@@ -350,14 +350,14 @@
     half = kernel(
         project, array(groups * split, padded), classes=classes, rows_each=rows
     )(predicted, *basis, labels)
+    halves = from_others(half, K)[:2]
     codes = jax.ShapeDtypeStruct((chips, groups * split, padded), jnp.int16)
     copies = kernel(join, codes, limit=4, classes=classes)(
-        *from_others(half, K)[:2]
+        *halves
     )
-    copies, late = lax.optimization_barrier((copies, predicted))
     projected = lax.all_to_all(copies, X, 0, 0, tiled=True).reshape(vectors, padded)
 
-    late = from_others(late, K)[:2]
+    late = from_others(predicted, K)[:2]
     output, updated = kernel(
         step_batch, (array(classes, batch), array(classes, count)), rows_each=rows
     )(*late, labels, index, coefficients)

time: 168 us -> 168 us (level)
  transfers between devices with their start and end apart: 13 -> 13, of which waited for: 8 -> 8; matrix products, arithmetic and copies ran while one was open for 0% -> 0% of each run, Pallas kernels for 4% -> 5%
where the time goes in v10:
time: 168 us; the launch traced here: 167 us
  blocking collectives  79.2 us (47%)
  starting transfers between devices  47.6 us (28%)
  waiting for transfers between devices  26.5 us (16%)
  Pallas kernels  11.6 us (7%)
    ppermute x10, starting transfers between devices, from_others(): pieces.append(lax.ppermute(value, axis, pairs))  32.6 us
    all_to_all x2, blocking collectives, scattered(): return jnp.sum(lax.all_to_all(tiles, axis, 0, 0, tiled=True), axis=0)  31.3 us
    all_to_all x1, blocking collectives, shards(): lax.all_to_all(kernel(fan, jax.ShapeDtypeStruct((depth, *batch_features.s...  27.4 us
    ppermute x10, waiting for transfers between devices, from_others(): pieces.append(lax.ppermute(value, axis, pairs))  22.4 us
    all_to_all x1, blocking collectives, gathered(): return lax.all_to_all(copies, axis, 0, 0, tiled=True)  20.4 us
    pallas_call x11, Pallas kernels, call(): pl.pallas_call(functools.partial(body, **settings), out_shape=outs, in_sp...  11.6 us
    all_to_all x1, starting transfers between devices, shards(): batch_own = lax.all_to_all(copies, (X, Y), 0, 0, tiled=True)  6.9 us
    all_to_all x1, starting transfers between devices, shards(): lax.all_to_all(copies, X, 0, 0, tiled=True).reshape(vectors, padded)  4.46 us
  transfers between devices with their start and end apart: 13, of which 8 were waited for; matrix products, arithmetic and copies ran while one was open for 0% of the time, Pallas kernels for 5%

profile of v10, /device:TPU:1, one launch (start us, length us, event | category | flops | bytes accessed | tf_op | source)
XLA Modules:
  0.0 166.5 jit_solution(11513102788563223863)
XLA Ops:
  0.6 0.7 copy-done.4
  1.3 27.4 %all_to_all.35.batch = bf16[16,8,320]{2,1,0:T(8,128)(2,1)S(1)} all-to-all(bf16[16,8,320]{2,1,0:T(8,128)(2,1)S(1)} %shard_map.95), channel_id=1, replica_groups=mesh['rows_z'=16,'rows_x'=4,'rows_k'=2,'cls'=4] {'rows_z'}, dimensions={0} | all-to-all | bytes 163840 | tf_op jit(solution)/shard_map/all_to_all | solution.py:296
  28.7 1.3 shard_map.96
  30.0 0.0 copy-start.7
  30.0 6.9 %all-to-all-start.1 = ((bf16[16,40,8,128]{3,2,1,0:T(8,128)(2,1)}), bf16[16,40,8,128]{3,2,1,0:T(8,128)(2,1)S(1)}, u32[]{:S(2)}, u32[]{:S(2)}) async-start(bf16[16,40,8,128]{3,2,1,0:T(8,128)(2,1)} %shard_map.96), calls=%async_computation.1 | async-start | bytes 2621440 | tf_op jit(solution)/shard_map/all_to_all | solution.py:315
  36.9 0.0 copy-done.1
  36.9 4.5 %collective-permute-start = (bf16[320,256]{1,0:T(8,128)(2,1)S(1)}, bf16[320,256]{1,0:T(8,128)(2,1)S(1)}, u32[]{:S(2)}, u32[]{:S(2)}) collective-permute-start(bf16[320,256]{1,0:T(8,128)(2,1)S(1)} %bitcast.13), channel_id=1, source_target_pairs={{1,0},{2,1},{3,2},{0,3},{5,4},{6,5},{7,6},{4,7},{9,8},{10,9},{11,1... | collective-permute-start | bytes 491528 | tf_op jit(solution)/shard_map/ppermute | solution.py:270
  41.4 2.5 %collective-permute-start.1 = (bf16[320,256]{1,0:T(8,128)(2,1)S(1)}, bf16[320,256]{1,0:T(8,128)(2,1)S(1)}, u32[]{:S(2)}, u32[]{:S(2)}) collective-permute-start(bf16[320,256]{1,0:T(8,128)(2,1)S(1)} %bitcast.14), channel_id=1, source_target_pairs={{2,0},{3,1},{0,2},{1,3},{6,4},{7,5},{4,6},{5,7},{10,8},{11,9},{8,1... | collective-permute-start | bytes 491528 | tf_op jit(solution)/shard_map/ppermute | solution.py:270
  43.9 2.5 %collective-permute-start.2 = (bf16[320,256]{1,0:T(8,128)(2,1)S(1)}, bf16[320,256]{1,0:T(8,128)(2,1)S(1)}, u32[]{:S(2)}, u32[]{:S(2)}) collective-permute-start(bf16[320,256]{1,0:T(8,128)(2,1)S(1)} %bitcast.15), channel_id=1, source_target_pairs={{3,0},{0,1},{1,2},{2,3},{7,4},{4,5},{5,6},{6,7},{11,8},{8,9},{9,10... | collective-permute-start | bytes 491528 | tf_op jit(solution)/shard_map/ppermute | solution.py:270
  46.4 0.0 copy-done
  46.4 0.0 copy-done.2
  46.4 0.0 copy-done.6
  46.4 0.0 copy-done.7
  46.5 0.5 shard_map.97
  46.9 10.6 %collective-permute-done.second = bf16[320,256]{1,0:T(8,128)(2,1)S(1)} collective-permute-done((bf16[320,256]{1,0:T(8,128)(2,1)S(1)}, bf16[320,256]{1,0:T(8,128)(2,1)S(1)}, u32[]{:S(2)}, u32[]{:S(2)}) %collective-permute-start) | collective-permute-done | bytes 163872 | tf_op jit(solution)/shard_map/ppermute | solution.py:270
  57.6 2.7 %collective-permute-done.1.third = bf16[320,256]{1,0:T(8,128)(2,1)S(1)} collective-permute-done((bf16[320,256]{1,0:T(8,128)(2,1)S(1)}, bf16[320,256]{1,0:T(8,128)(2,1)S(1)}, u32[]{:S(2)}, u32[]{:S(2)}) %collective-permute-start.1) | collective-permute-done | bytes 163872 | tf_op jit(solution)/shard_map/ppermute | solution.py:270
  60.2 2.9 %collective-permute-done.2.fourth = bf16[320,256]{1,0:T(8,128)(2,1)S(1)} collective-permute-done((bf16[320,256]{1,0:T(8,128)(2,1)S(1)}, bf16[320,256]{1,0:T(8,128)(2,1)S(1)}, u32[]{:S(2)}, u32[]{:S(2)}) %collective-permute-start.2) | collective-permute-done | bytes 163872 | tf_op jit(solution)/shard_map/ppermute | solution.py:270
  63.1 0.0 all-to-all-done.1
  63.1 2.4 %collective-permute-start.3 = (bf16[4,4,40,8,128]{4,3,2,1,0:T(8,128)(2,1)S(1)}, bf16[4,4,40,8,128]{4,3,2,1,0:T(8,128)(2,1)S(1)}, u32[]{:S(2)}, u32[]{:S(2)}) collective-permute-start(bf16[4,4,40,8,128]{4,3,2,1,0:T(8,128)(2,1)S(1)} %bitcast.9), channel_id=1, source_target_pairs={{4,0},{0,4},{5,1},{1,5},{6,2},{2,6},{7,3},{3,7},{12,8},{8,12},{13,... | collective-permute-start | bytes 3932168 | tf_op jit(solution)/shard_map/ppermute | solution.py:270
  65.6 2.0 %shard_map.99 = f32[4,384,128]{2,1,0:T(8,128)S(1)} custom-call(bf16[4,4,40,8,128]{4,3,2,1,0:T(8,128)(2,1)S(1)} %bitcast.10, bf16[320,256]{1,0:T(8,128)(2,1)S(1)} %bitcast.16, bf16[320,256]{1,0:T(8,128)(2,1)S(1)} %collective-permute-done.second, bf16[320,256]{1,0:T(8,128)(2,1)S(1)} %collective-permute-done.1.third, ...), custom_call_target="tpu_custom_call" | custom-call | tf_op jit(solution)/shard_map/pallas_call | solution.py:252
  67.5 1.9 %collective-permute-start.4 = (f32[4,384,128]{2,1,0:T(8,128)S(1)}, f32[4,384,128]{2,1,0:T(8,128)S(1)}, u32[]{:S(2)}, u32[]{:S(2)}) collective-permute-start(f32[4,384,128]{2,1,0:T(8,128)S(1)} %shard_map.99), channel_id=1, source_target_pairs={{4,0},{0,4},{5,1},{1,5},{6,2},{2,6},{7,3},{3,7},{12,8},{8,12},{13,... | collective-permute-start | bytes 2359304 | tf_op jit(solution)/shard_map/ppermute | solution.py:270
  69.5 0.0 collective-permute-done.3.batch
  69.5 2.0 %shard_map.98.own = f32[4,384,128]{2,1,0:T(8,128)S(1)} custom-call(bf16[4,4,40,8,128]{4,3,2,1,0:T(8,128)(2,1)S(1)} %collective-permute-done.3.batch, bf16[320,256]{1,0:T(8,128)(2,1)S(1)} %bitcast.17, bf16[320,256]{1,0:T(8,128)(2,1)S(1)} %collective-permute-done.second, bf16[320,256]{1,0:T(8,128)(2,1)S(1)} %collective-permute-done.1.third, ...), custom_call_target="tpu_custom_call" | custom-call | tf_op jit(solution)/shard_map/pallas_call | solution.py:252
  71.5 0.3 collective-permute-done.4.other
  71.7 0.1 shard_map.100
  71.8 14.4 %all_to_all.36 = f32[4,384,128]{2,1,0:T(8,128)S(1)} all-to-all(f32[4,384,128]{2,1,0:T(8,128)S(1)} %shard_map.100), channel_id=1, replica_groups=mesh['rows_z'=16,'rows_x'=4,'rows_k'=2,'cls'=4] {'rows_x'}, dimensions={0} | all-to-all | bytes 1572864 | tf_op jit(solution)/shard_map/all_to_all | solution.py:32
  86.2 0.0 copy-start.3
  86.2 16.9 %all_to_all.37 = f32[16,24,128]{2,1,0:T(8,128)S(1)} all-to-all(f32[16,24,128]{2,1,0:T(8,128)S(1)} %bitcast.23), channel_id=1, replica_groups=mesh['rows_z'=16,'rows_x'=4,'rows_k'=2,'cls'=4] {'rows_z'}, dimensions={0} | all-to-all | bytes 393216 | tf_op jit(solution)/shard_map/all_to_all | solution.py:32
  103.2 20.4 %all_to_all.38 = f32[16,24,128]{2,1,0:T(8,128)S(1)} all-to-all(f32[16,24,128]{2,1,0:T(8,128)S(1)} %broadcast_in_dim.11), channel_id=1, replica_groups=mesh['rows_z'=16,'rows_x'=4,'rows_k'=2,'cls'=4] {'rows_z'}, dimensions={0} | all-to-all | bytes 393216 | tf_op jit(solution)/shard_map/all_to_all | solution.py:28
  123.7 0.8 shard_map.101
  124.5 3.6 %all-to-all-start.5 = ((f32[4,256,128]{2,1,0:T(8,128)}), f32[4,256,128]{2,1,0:T(8,128)S(1)}, u32[]{:S(2)}, u32[]{:S(2)}) async-start(f32[4,256,128]{2,1,0:T(8,128)} %get-tuple-element.32), calls=%async_computation.5 | async-start | bytes 1048576 | tf_op jit(solution)/shard_map/all_to_all | solution.py:347
  128.1 3.3 %collective-permute-start.5 = (f32[4,32,128]{2,1,0:T(8,128)S(1)}, f32[4,32,128]{2,1,0:T(8,128)S(1)}, u32[]{:S(2)}, u32[]{:S(2)}) collective-permute-start(f32[4,32,128]{2,1,0:T(8,128)S(1)} %get-tuple-element.37.first), channel_id=1, source_target_pairs={{1,0},{2,1},{3,2},{0,3},{5,4},{6,5},{7,6},{4,7},{9,8},{10,9},{11,1... | collective-permute-start | bytes 196616 | tf_op jit(solution)/shard_map/ppermute | solution.py:270
  131.4 3.1 %collective-permute-start.6 = (f32[4,32,128]{2,1,0:T(8,128)S(1)}, f32[4,32,128]{2,1,0:T(8,128)S(1)}, u32[]{:S(2)}, u32[]{:S(2)}) collective-permute-start(f32[4,32,128]{2,1,0:T(8,128)S(1)} %get-tuple-element.37.first), channel_id=1, source_target_pairs={{2,0},{3,1},{0,2},{1,3},{6,4},{7,5},{4,6},{5,7},{10,8},{11,9},{8,1... | collective-permute-start | bytes 196616 | tf_op jit(solution)/shard_map/ppermute | solution.py:270
  134.5 1.9 %collective-permute-start.7 = (f32[4,32,128]{2,1,0:T(8,128)S(1)}, f32[4,32,128]{2,1,0:T(8,128)S(1)}, u32[]{:S(2)}, u32[]{:S(2)}) collective-permute-start(f32[4,32,128]{2,1,0:T(8,128)S(1)} %get-tuple-element.37.first), channel_id=1, source_target_pairs={{3,0},{0,1},{1,2},{2,3},{7,4},{4,5},{5,6},{6,7},{11,8},{8,9},{9,10... | collective-permute-start | bytes 196616 | tf_op jit(solution)/shard_map/ppermute | solution.py:270
  136.4 0.0 collective-permute-done.5.second
  136.4 1.5 collective-permute-done.6.third
  137.9 3.1 %collective-permute-done.7.fourth = f32[4,32,128]{2,1,0:T(8,128)S(1)} collective-permute-done((f32[4,32,128]{2,1,0:T(8,128)S(1)}, f32[4,32,128]{2,1,0:T(8,128)S(1)}, u32[]{:S(2)}, u32[]{:S(2)}) %collective-permute-start.7) | collective-permute-done | bytes 65568 | tf_op jit(solution)/shard_map/ppermute | solution.py:270
  141.0 0.0 all-to-all-done.5.own
  141.0 8.6 %collective-permute-start.8 = (f32[4,256,128]{2,1,0:T(8,128)S(1)}, f32[4,256,128]{2,1,0:T(8,128)S(1)}, u32[]{:S(2)}, u32[]{:S(2)}) collective-permute-start(f32[4,256,128]{2,1,0:T(8,128)S(1)} %all-to-all-done.5.own), channel_id=1, source_target_pairs={{4,0},{0,4},{5,1},{1,5},{6,2},{2,6},{7,3},{3,7},{12,8},{8,12},{13,... | collective-permute-start | bytes 1572872 | tf_op jit(solution)/shard_map/ppermute | solution.py:270
  149.7 0.9 shard_map.103.own
  150.6 1.9 %collective-permute-start.9 = (f32[128,256]{1,0:T(8,128)S(1)}, f32[128,256]{1,0:T(8,128)S(1)}, u32[]{:S(2)}, u32[]{:S(2)}) collective-permute-start(f32[128,256]{1,0:T(8,128)S(1)} %shard_map.103.own), channel_id=1, source_target_pairs={{4,0},{0,4},{5,1},{1,5},{6,2},{2,6},{7,3},{3,7},{12,8},{8,12},{13,... | collective-permute-start | bytes 393224 | tf_op jit(solution)/shard_map/ppermute | solution.py:270
  152.5 1.3 collective-permute-done.9.other
  153.8 0.9 shard_map.104
  154.7 4.5 %all-to-all-start.6 = ((s16[4,128,256]{2,1,0:T(8,128)(2,1)}), s16[4,128,256]{2,1,0:T(8,128)(2,1)S(1)}, u32[]{:S(2)}, u32[]{:S(2)}) async-start(s16[4,128,256]{2,1,0:T(8,128)(2,1)} %shard_map.104), calls=%async_computation.6 | async-start | bytes 524288 | tf_op jit(solution)/shard_map/all_to_all | solution.py:358
  159.2 0.0 collective-permute-done.8.other
  159.2 1.9 %shard_map.102 = (f32[250,1024]{1,0:T(8,128)}, f32[250,256]{1,0:T(8,128)S(1)}) custom-call(f32[4,256,128]{2,1,0:T(8,128)S(1)} %all-to-all-done.5.own, f32[4,256,128]{2,1,0:T(8,128)S(1)} %collective-permute-done.8.other, s32[4,1,256]{2,1,0:T(1,128)S(1)} %bitcast.19, s32[4,1,256]{2,1,0:T(1,128)S(1)} %bitcast.20, f32[250,256]{1,0:T(8,128)S(1)} %copy-done), custom_call_target="tpu_custom_call" | custom-call | tf_op jit(solution)/shard_map/pallas_call | solution.py:252
  161.1 4.1 %all-to-all-done.6 = s16[4,128,256]{2,1,0:T(8,128)(2,1)S(1)} async-done(((s16[4,128,256]{2,1,0:T(8,128)(2,1)}), s16[4,128,256]{2,1,0:T(8,128)(2,1)S(1)}, u32[]{:S(2)}, u32[]{:S(2)}) %all-to-all-start.6) | async-done | bytes 262176 | tf_op jit(solution)/shard_map/all_to_all | solution.py:358
  165.2 1.3 shard_map.105
  (12 shorter events, 0.1 us)
Async XLA Ops:
  0.6 0.7 copy-start.4
  30.0 6.9 %copy-start.1 = (bf16[256,320]{0,1:T(8,128)(2,1)S(1)}, bf16[256,320]{0,1:T(8,128)(2,1)}, u32[]{:S(2)}) copy-start(bf16[256,320]{0,1:T(8,128)(2,1)} %param.8) | copy-start | bytes 491524
  30.0 16.4 %copy-start = (f32[250,256]{1,0:T(8,128)S(1)}, f32[250,256]{1,0:T(8,128)}, u32[]{:S(2)}) copy-start(f32[250,256]{1,0:T(8,128)} %coefficients.3) | copy-start | bytes 768004
  30.0 16.4 %copy-start.2 = (f32[64,512]{1,0:T(8,128)S(1)}, f32[64,512]{1,0:T(8,128)}, u32[]{:S(2)}) copy-start(f32[64,512]{1,0:T(8,128)} %vectors.1) | copy-start | bytes 393220
  30.0 16.4 %copy-start.6 = (f32[512]{0:T(512)S(1)}, f32[512]{0:T(512)}, u32[]{:S(2)}) copy-start(f32[512]{0:T(512)} %param.15) | copy-start | bytes 6148
  30.0 16.4 %copy-start.7 = (s32[64]{0:T(128)S(1)}, s32[64]{0:T(128)}, u32[]{:S(2)}) copy-start(s32[64]{0:T(128)} %param.13) | copy-start | bytes 772
  30.0 33.1 %all-to-all-start.1 = ((bf16[16,40,8,128]{3,2,1,0:T(8,128)(2,1)}), bf16[16,40,8,128]{3,2,1,0:T(8,128)(2,1)S(1)}, u32[]{:S(2)}, u32[]{:S(2)}) async-start(bf16[16,40,8,128]{3,2,1,0:T(8,128)(2,1)} %shard_map.96), calls=%async_computation.1 | async-start | bytes 2621440 | tf_op jit(solution)/shard_map/all_to_all | solution.py:315
  36.9 20.6 %collective-permute-start = (bf16[320,256]{1,0:T(8,128)(2,1)S(1)}, bf16[320,256]{1,0:T(8,128)(2,1)S(1)}, u32[]{:S(2)}, u32[]{:S(2)}) collective-permute-start(bf16[320,256]{1,0:T(8,128)(2,1)S(1)} %bitcast.13), channel_id=1, source_target_pairs={{1,0},{2,1},{3,2},{0,3},{5,4},{6,5},{7,6},{4,7},{9,8},{10,9},{11,1... | collective-permute-start | bytes 491528 | tf_op jit(solution)/shard_map/ppermute | solution.py:270
  41.4 18.8 %collective-permute-start.1 = (bf16[320,256]{1,0:T(8,128)(2,1)S(1)}, bf16[320,256]{1,0:T(8,128)(2,1)S(1)}, u32[]{:S(2)}, u32[]{:S(2)}) collective-permute-start(bf16[320,256]{1,0:T(8,128)(2,1)S(1)} %bitcast.14), channel_id=1, source_target_pairs={{2,0},{3,1},{0,2},{1,3},{6,4},{7,5},{4,6},{5,7},{10,8},{11,9},{8,1... | collective-permute-start | bytes 491528 | tf_op jit(solution)/shard_map/ppermute | solution.py:270
  43.9 19.2 %collective-permute-start.2 = (bf16[320,256]{1,0:T(8,128)(2,1)S(1)}, bf16[320,256]{1,0:T(8,128)(2,1)S(1)}, u32[]{:S(2)}, u32[]{:S(2)}) collective-permute-start(bf16[320,256]{1,0:T(8,128)(2,1)S(1)} %bitcast.15), channel_id=1, source_target_pairs={{3,0},{0,1},{1,2},{2,3},{7,4},{4,5},{5,6},{6,7},{11,8},{8,9},{9,10... | collective-permute-start | bytes 491528 | tf_op jit(solution)/shard_map/ppermute | solution.py:270
  63.1 6.3 %collective-permute-start.3 = (bf16[4,4,40,8,128]{4,3,2,1,0:T(8,128)(2,1)S(1)}, bf16[4,4,40,8,128]{4,3,2,1,0:T(8,128)(2,1)S(1)}, u32[]{:S(2)}, u32[]{:S(2)}) collective-permute-start(bf16[4,4,40,8,128]{4,3,2,1,0:T(8,128)(2,1)S(1)} %bitcast.9), channel_id=1, source_target_pairs={{4,0},{0,4},{5,1},{1,5},{6,2},{2,6},{7,3},{3,7},{12,8},{8,12},{13,... | collective-permute-start | bytes 3932168 | tf_op jit(solution)/shard_map/ppermute | solution.py:270
  67.5 4.2 %collective-permute-start.4 = (f32[4,384,128]{2,1,0:T(8,128)S(1)}, f32[4,384,128]{2,1,0:T(8,128)S(1)}, u32[]{:S(2)}, u32[]{:S(2)}) collective-permute-start(f32[4,384,128]{2,1,0:T(8,128)S(1)} %shard_map.99), channel_id=1, source_target_pairs={{4,0},{0,4},{5,1},{1,5},{6,2},{2,6},{7,3},{3,7},{12,8},{8,12},{13,... | collective-permute-start | bytes 2359304 | tf_op jit(solution)/shard_map/ppermute | solution.py:270
  86.2 63.4 %copy-start.3 = (s32[1024]{0:T(1024)S(1)}, s32[1024]{0:T(1024)}, u32[]{:S(2)}) copy-start(s32[1024]{0:T(1024)} %param.11) | copy-start | bytes 12292
  124.5 34.7 %copy-start.5 = (s32[1024]{0:T(1024)S(1)}, s32[1024]{0:T(1024)}, u32[]{:S(2)}) copy-start(s32[1024]{0:T(1024)} %param.12) | copy-start | bytes 12292
  124.5 16.5 %all-to-all-start.5 = ((f32[4,256,128]{2,1,0:T(8,128)}), f32[4,256,128]{2,1,0:T(8,128)S(1)}, u32[]{:S(2)}, u32[]{:S(2)}) async-start(f32[4,256,128]{2,1,0:T(8,128)} %get-tuple-element.32), calls=%async_computation.5 | async-start | bytes 1048576 | tf_op jit(solution)/shard_map/all_to_all | solution.py:347
  128.1 8.3 %collective-permute-start.5 = (f32[4,32,128]{2,1,0:T(8,128)S(1)}, f32[4,32,128]{2,1,0:T(8,128)S(1)}, u32[]{:S(2)}, u32[]{:S(2)}) collective-permute-start(f32[4,32,128]{2,1,0:T(8,128)S(1)} %get-tuple-element.37.first), channel_id=1, source_target_pairs={{1,0},{2,1},{3,2},{0,3},{5,4},{6,5},{7,6},{4,7},{9,8},{10,9},{11,1... | collective-permute-start | bytes 196616 | tf_op jit(solution)/shard_map/ppermute | solution.py:270
  131.4 6.5 %collective-permute-start.6 = (f32[4,32,128]{2,1,0:T(8,128)S(1)}, f32[4,32,128]{2,1,0:T(8,128)S(1)}, u32[]{:S(2)}, u32[]{:S(2)}) collective-permute-start(f32[4,32,128]{2,1,0:T(8,128)S(1)} %get-tuple-element.37.first), channel_id=1, source_target_pairs={{2,0},{3,1},{0,2},{1,3},{6,4},{7,5},{4,6},{5,7},{10,8},{11,9},{8,1... | collective-permute-start | bytes 196616 | tf_op jit(solution)/shard_map/ppermute | solution.py:270
  134.5 6.5 %collective-permute-start.7 = (f32[4,32,128]{2,1,0:T(8,128)S(1)}, f32[4,32,128]{2,1,0:T(8,128)S(1)}, u32[]{:S(2)}, u32[]{:S(2)}) collective-permute-start(f32[4,32,128]{2,1,0:T(8,128)S(1)} %get-tuple-element.37.first), channel_id=1, source_target_pairs={{3,0},{0,1},{1,2},{2,3},{7,4},{4,5},{5,6},{6,7},{11,8},{8,9},{9,10... | collective-permute-start | bytes 196616 | tf_op jit(solution)/shard_map/ppermute | solution.py:270
  141.0 18.1 %collective-permute-start.8 = (f32[4,256,128]{2,1,0:T(8,128)S(1)}, f32[4,256,128]{2,1,0:T(8,128)S(1)}, u32[]{:S(2)}, u32[]{:S(2)}) collective-permute-start(f32[4,256,128]{2,1,0:T(8,128)S(1)} %all-to-all-done.5.own), channel_id=1, source_target_pairs={{4,0},{0,4},{5,1},{1,5},{6,2},{2,6},{7,3},{3,7},{12,8},{8,12},{13,... | collective-permute-start | bytes 1572872 | tf_op jit(solution)/shard_map/ppermute | solution.py:270
  150.6 3.2 %collective-permute-start.9 = (f32[128,256]{1,0:T(8,128)S(1)}, f32[128,256]{1,0:T(8,128)S(1)}, u32[]{:S(2)}, u32[]{:S(2)}) collective-permute-start(f32[128,256]{1,0:T(8,128)S(1)} %shard_map.103.own), channel_id=1, source_target_pairs={{4,0},{0,4},{5,1},{1,5},{6,2},{2,6},{7,3},{3,7},{12,8},{8,12},{13,... | collective-permute-start | bytes 393224 | tf_op jit(solution)/shard_map/ppermute | solution.py:270
  154.7 10.5 %all-to-all-start.6 = ((s16[4,128,256]{2,1,0:T(8,128)(2,1)}), s16[4,128,256]{2,1,0:T(8,128)(2,1)S(1)}, u32[]{:S(2)}, u32[]{:S(2)}) async-start(s16[4,128,256]{2,1,0:T(8,128)(2,1)} %shard_map.104), calls=%async_computation.6 | async-start | bytes 524288 | tf_op jit(solution)/shard_map/all_to_all | solution.py:358
